TPU v7x, 256 devices: a whole 4x4x8 slice. The times are simulated.
256 devices in a mesh: wide: 64 (over x, z, y_hi), narrow: 4 (over y_lo, core).
Axes of the slice: x: 4, y: 4 (y_hi: 2, y_lo: 2; y = y_hi * 2 + y_lo), z: 8, core: 2. Of those that a mesh axis runs over, the one named last changes fastest.
Arguments:
- latent: bfloat16 [64, 32, 48, 256], P('wide', 'narrow'), may hold values from -12 to 12
- conv_first: bfloat16 [6912, 256], P(None, 'wide'), may hold values from -0.078125 to 0.078125
- conv_second: bfloat16 [6912, 256], P(None, 'wide'), may hold values from -0.078125 to 0.078125
- embed_weight: bfloat16 [1024, 2240], P(None, 'wide'), may hold values from -0.1875 to 0.1875
- qkv_weight: bfloat16 [3, 2240, 2240], P(None, None, 'narrow'), may hold values from -0.125 to 0.125
Outputs:
- mixed: bfloat16 [24576, 2240], P('wide', 'narrow')
All inputs are finite; a program needn't handle non-finite values.
Results may differ from a plain program's by a relative error of at most 0.011.
Values may be sent and summed in bfloat16 or wider, within the bound.
No kernel may reach another device: no remote copies, remote signals or barrier semaphores. Data moves between devices by JAX's collectives and lax.ppermute only.
A program may use at most 128 MiB of HBM per device.

v0:
```python
import jax
import jax.numpy as jnp
from jax import lax
from jax.sharding import PartitionSpec as P

HEAD_DIM = 112


def shifted(x, axis, by):
    size = lax.axis_size(axis)
    pairs = [(i, i + by) for i in range(size) if 0 <= i + by < size]
    return lax.ppermute(x, axis, pairs)


def extended(block, sides, width):
    for axis, dim in sides:
        count = lax.axis_size(axis)
        forward = [(i, i + 1) for i in range(count - 1)]
        backward = [(target, source) for source, target in forward]
        low = lax.ppermute(
            lax.slice_in_dim(block, block.shape[dim] - width, None, axis=dim), axis, forward
        )
        high = lax.ppermute(lax.slice_in_dim(block, 0, width, axis=dim), axis, backward)
        block = jnp.concatenate([low, block, high], axis=dim)
    return block


def laid_out(blocks, dim):
    lengths = list(blocks.shape[1:])
    lengths[dim] *= blocks.shape[0]
    return jnp.moveaxis(blocks, 0, dim).reshape(lengths)


def work_in_pieces(x, axis, dim, work, out_dim):
    extent = x.shape[dim]
    pieces = jnp.split(x, 2, axis=dim) if extent % 2 == 0 else [x]
    first = jnp.arange(lax.axis_size(axis)) * extent
    blocks = [lax.all_gather(share, axis) for share in pieces]
    made = [jax.vmap(work)(b, first + k * (extent // len(pieces))) for k, b in enumerate(blocks)]
    return laid_out(jnp.concatenate(made, axis=out_dim + 1), out_dim)


def exchange_in_groups(x, axis, split_dim, concat_dim, work, item_dim, out_dim):

    def moved(group):
        return lax.all_to_all(group, axis, split_axis=split_dim, concat_axis=concat_dim, tiled=True)

    items = jax.tree.leaves(x)[0].shape[item_dim]
    ends = [items * k // 2 for k in range(2 + 1)] if items % 2 == 0 else [0, items]
    groups = [
        jax.tree.map(lambda a: lax.slice_in_dim(a, low, high, axis=item_dim), x)
        for low, high in zip(ends, ends[1:])
    ]
    arrived = [moved(group) for group in groups]
    made = [work(group) for group in arrived]
    return jax.tree.map(lambda *parts: jnp.concatenate(parts, axis=out_dim), *made)


def causal_conv(current, weight):
    before = shifted(current, "wide", 1)
    earlier = shifted(current, "wide", 2)
    stacked = jnp.concatenate([earlier, before, current], axis=0)
    rimmed = extended(stacked, (("narrow", 1),), 1)
    padded = jnp.pad(rimmed, ((0, 0), (0, 0), (1, 1), (0, 0)))
    row_count = current.shape[1]
    col_count = current.shape[2]
    chan_count = current.shape[3]
    block_cols = lax.all_gather(weight, "wide", axis=1, tiled=True)
    summed = jnp.zeros((row_count * col_count, block_cols.shape[1]), jnp.float32)
    for kernel_tap in range(27):
        time_step = kernel_tap // 9
        row_step = kernel_tap // 3 % 3
        col_step = kernel_tap % 3
        window = padded[time_step, row_step : row_step + row_count, col_step : col_step + col_count]
        window = window.reshape(row_count * col_count, chan_count)
        summed = summed + jnp.dot(
            window,
            block_cols[kernel_tap * chan_count : (kernel_tap + 1) * chan_count],
            preferred_element_type=jnp.float32,
        )
    return summed


def embed_tokens(patch_feats, embed_weight):

    def project(block_cols, offset):
        return jnp.dot(patch_feats, block_cols, preferred_element_type=jnp.float32)

    return work_in_pieces(embed_weight, "wide", 1, project, 1).astype(jnp.bfloat16)


def per_device(latent, conv_first, conv_second, embed_weight, qkv_weight):
    row_count = latent.shape[1]
    col_count = latent.shape[2]
    chan_count = latent.shape[3]
    first = causal_conv(latent, conv_first)
    activated = jax.nn.silu(first).astype(jnp.bfloat16).reshape(latent.shape)
    second = causal_conv(activated, conv_second) + latent.reshape(-1, chan_count).astype(
        jnp.float32
    )
    block_out = second.astype(jnp.bfloat16)
    patches = block_out.reshape(row_count // 2, 2, col_count // 2, 2, chan_count)
    patches = patches.transpose(0, 2, 1, 3, 4).reshape(-1, 4 * chan_count)
    whole_patches = lax.all_gather(patches, "narrow", axis=0, tiled=True)
    embedded = embed_tokens(whole_patches, embed_weight)
    heads_here = qkv_weight.shape[2] // HEAD_DIM
    token_count = embedded.shape[0]
    query_raw = jnp.dot(embedded, qkv_weight[0], preferred_element_type=jnp.float32)
    key_raw = jnp.dot(embedded, qkv_weight[1], preferred_element_type=jnp.float32)
    val_rows = jnp.dot(embedded, qkv_weight[2], preferred_element_type=jnp.float32).astype(
        jnp.bfloat16
    )
    query_feat = (
        (jax.nn.elu(query_raw) + 1.0)
        .astype(jnp.bfloat16)
        .reshape(token_count, heads_here, HEAD_DIM)
    )
    key_feat = (
        (jax.nn.elu(key_raw) + 1.0).astype(jnp.bfloat16).reshape(token_count, heads_here, HEAD_DIM)
    )
    val_heads = val_rows.reshape(token_count, heads_here, HEAD_DIM)
    scores = jnp.einsum("thd,shd->hts", query_feat, key_feat, preferred_element_type=jnp.float32)
    row_ids = lax.broadcasted_iota(jnp.int32, (token_count, token_count), 0)
    col_ids = lax.broadcasted_iota(jnp.int32, (token_count, token_count), 1)
    scores = jnp.where((col_ids <= row_ids)[None], scores, 0.0)
    local_den = jnp.sum(scores, axis=-1)
    local_num = jnp.einsum(
        "hts,she->the", scores.astype(jnp.bfloat16), val_heads, preferred_element_type=jnp.float32
    )
    state_local = jnp.einsum(
        "thd,the->hde", key_feat, val_heads, preferred_element_type=jnp.float32
    )
    key_local = jnp.sum(key_feat, axis=0, dtype=jnp.float32)
    flat_state = jnp.concatenate([state_local.reshape(-1), key_local.reshape(-1)])
    length_all = flat_state.shape[0]
    peer_count = lax.axis_size("wide")
    per_peer = -(-length_all // peer_count)
    piece_grid = jnp.pad(flat_state, (0, per_peer * peer_count - length_all)).reshape(
        peer_count, per_peer
    )
    lower_ones = (
        lax.broadcasted_iota(jnp.int32, (peer_count, peer_count), 1)
        < lax.broadcasted_iota(jnp.int32, (peer_count, peer_count), 0)
    ).astype(jnp.float32)

    def running(columns_in):
        partial_sums = jnp.dot(lower_ones, columns_in, precision=lax.Precision.HIGHEST)
        return lax.all_to_all(
            partial_sums.astype(jnp.bfloat16), "wide", split_axis=0, concat_axis=0, tiled=True
        ).astype(partial_sums.dtype)

    spread = exchange_in_groups(
        piece_grid.astype(jnp.bfloat16),
        "wide",
        0,
        0,
        lambda group: running(group.astype(jnp.float32)),
        1,
        1,
    )
    flat_prefix = spread.reshape(-1)[:length_all]
    state_size = state_local.size
    state_prev = flat_prefix[:state_size].reshape(state_local.shape)
    key_prev = flat_prefix[state_size:].reshape(key_local.shape)
    query_wide = query_feat.astype(jnp.float32)
    carried_num = jnp.einsum(
        "thd,hde->the", query_wide, state_prev, precision=lax.Precision.HIGHEST
    )
    carried_den = jnp.einsum("thd,hd->th", query_wide, key_prev, precision=lax.Precision.HIGHEST)
    result = (local_num + carried_num) / (local_den.T + carried_den)[..., None]
    return result.astype(jnp.bfloat16).reshape(token_count, heads_here * HEAD_DIM)


def solution(mesh):
    return jax.shard_map(
        per_device,
        mesh=mesh,
        in_specs=(
            P("wide", "narrow", None, None),
            P(None, "wide"),
            P(None, "wide"),
            P(None, "wide"),
            P(None, None, "narrow"),
        ),
        out_specs=P("wide", "narrow"),
        check_vma=False,
    )
```

profile of v0, /device:TPU:8, one launch (start us, length us, event | category | flops | bytes accessed | tf_op | source)
XLA Modules:
  0.0 465.5 jit_solution(17870810909222242809)
XLA Ops:
  8.1 3.8 collective-permute-start
  11.9 4.2 collective-permute-start.1
  16.4 3.9 collective-permute-done.1
  21.4 1.9 collective-permute-start.2
  23.3 3.6 collective-permute-start.3
  27.0 1.9 collective-permute-done.3
  29.4 1.8 fusion.150
  32.3 105.1 %all-gather.9.cloned.1.call-done = bf16[64,4,6912]{2,1,0:T(4,128)(2,1)} async-done(((bf16[1,4,6912]{2,1,0:T(4,128)(2,1)}), bf16[64,4,6912]{2,1,0:T(4,128)(2,1)}) %all-gather.9.cloned.1.call-update) | async-done | bytes 3538960 | tf_op jit(solution)/shard_map/all_gather | solution.py:68
  137.5 5.3 %reshape.81 = bf16[256,6912]{1,0:T(8,128)(2,1)S(1)} reshape(bf16[64,4,6912]{2,1,0:T(4,128)(2,1)} %all-gather.9.cloned.1.call-done) | data formatting | bytes 7077888
  154.7 2.8 collective-permute-start.4
  157.6 3.3 collective-permute-start.5
  160.9 3.1 collective-permute-done.5
  164.8 1.9 collective-permute-start.7
  167.4 94.9 %all-gather.11.cloned.1.call-done = bf16[64,4,6912]{2,1,0:T(4,128)(2,1)} async-done(((bf16[1,4,6912]{2,1,0:T(4,128)(2,1)}), bf16[64,4,6912]{2,1,0:T(4,128)(2,1)}) %all-gather.11.cloned.1.call-update) | async-done | bytes 3538960 | tf_op jit(solution)/shard_map/all_gather | solution.py:68
  262.3 5.3 %reshape.83 = bf16[256,6912]{1,0:T(8,128)(2,1)S(1)} reshape(bf16[64,4,6912]{2,1,0:T(4,128)(2,1)} %all-gather.11.cloned.1.call-done) | data formatting | bytes 7077888
  267.6 1.9 collective-permute-start.6
  270.8 2.7 collective-permute-done.6
  274.7 1.6 select_maximum_fusion
  285.6 7.4 %all_gather.17 = bf16[384,1024]{1,0:T(8,128)(2,1)S(1)} all-gather(bf16[96,1024]{1,0:T(8,128)(2,1)S(1)} %reshape.70), channel_id=1, replica_groups=mesh['wide'=64,'narrow'=4] {'narrow'}, dimensions={0}, use_global_device_ids=true | all-gather | bytes 983040 | tf_op jit(solution)/shard_map/all_gather | solution.py:104
  293.0 101.8 %all-gather.7.cloned.1.call-done = bf16[65536,35]{0,1:T(8,128)(2,1)} async-done(((bf16[1024,35]{0,1:T(8,128)(2,1)}), bf16[65536,35]{0,1:T(8,128)(2,1)}) %all-gather.7.cloned.1.call-update) | async-done | bytes 4587536 | tf_op jit(solution)/shard_map/all_gather | solution.py:38
  394.7 5.5 %copy.29 = bf16[5,8,64,1024]{3,2,1,0:T(8,128)(2,1)S(1)} copy(bf16[5,8,64,1024]{3,1,2,0:T(8,128)(2,1)} %bitcast.244) | data formatting | bytes 10485760
  400.2 2.6 fusion.12
  403.8 1.5 convert_element_type.63
  405.4 4.2 fusion.152
  409.6 3.2 fusion.22
  414.4 8.1 %all-to-all-start = ((bf16[64,1,989]{2,1,0:T(2,128)(2,1)}), bf16[64,1,989]{2,1,0:T(2,128)(2,1)S(1)}, u32[]{:S(2)}, u32[]{:S(2)}) async-start(bf16[64,1,989]{2,1,0:T(2,128)(2,1)} %convert_element_type.72), calls=%async_computation | async-start | bytes 524288 | tf_op jit(solution)/shard_map/all_to_all | solution.py:46
  422.5 3.5 fusion.49
  425.9 9.1 %all-to-all-done = bf16[64,1,989]{2,1,0:T(2,128)(2,1)S(1)} async-done(((bf16[64,1,989]{2,1,0:T(2,128)(2,1)}), bf16[64,1,989]{2,1,0:T(2,128)(2,1)S(1)}, u32[]{:S(2)}, u32[]{:S(2)}) %all-to-all-start) | async-done | bytes 126624 | tf_op jit(solution)/shard_map/all_to_all | solution.py:46
  436.1 5.8 %all-to-all-start.1 = ((bf16[64,1,989]{2,1,0:T(2,128)(2,1)}), bf16[64,1,989]{2,1,0:T(2,128)(2,1)S(1)}, u32[]{:S(2)}, u32[]{:S(2)}) async-start(bf16[64,1,989]{2,1,0:T(2,128)(2,1)} %copy.22), calls=%async_computation.1 | async-start | bytes 524288 | tf_op jit(solution)/shard_map/all_to_all | solution.py:148
  441.9 1.8 select_reduce_fusion
  443.8 10.7 %all-to-all-done.1 = bf16[64,1,989]{2,1,0:T(2,128)(2,1)S(1)} async-done(((bf16[64,1,989]{2,1,0:T(2,128)(2,1)}), bf16[64,1,989]{2,1,0:T(2,128)(2,1)S(1)}, u32[]{:S(2)}, u32[]{:S(2)}) %all-to-all-start.1) | async-done | bytes 126624 | tf_op jit(solution)/shard_map/all_to_all | solution.py:148
  456.3 2.6 fusion.25
  (159 shorter events, 34.1 us)
Async XLA Ops:
  6.5 130.9 %all-gather.9.cloned.1.call-start = ((), (), s32[]{:S(2)}) async-start(), calls=%async_computation.3 | async-start | bytes 3594240 | tf_op jit(solution)/shard_map/all_gather | solution.py:68
  7.3 255.1 %all-gather.11.cloned.1.call-start = ((), (), s32[]{:S(2)}) async-start(), calls=%async_computation.4 | async-start | bytes 3594240 | tf_op jit(solution)/shard_map/all_gather | solution.py:68
  8.0 386.7 %all-gather.7.cloned.1.call-start = ((), (), s32[]{:S(2)}) async-start(), calls=%async_computation.2 | async-start | bytes 5324800 | tf_op jit(solution)/shard_map/all_gather | solution.py:38
  8.1 8.3 %collective-permute-start = (bf16[1,8,48,256]{3,2,1,0:T(8,128)(2,1)}, bf16[1,8,48,256]{3,2,1,0:T(8,128)(2,1)S(1)}, u32[]{:S(2)}, u32[]{:S(2)}) collective-permute-start(bf16[1,8,48,256]{3,2,1,0:T(8,128)(2,1)} %param.5), channel_id=1, source_target_pairs={{0,8},{4,12},{8,16},{12,20},{16,24},{20,28},{24,32},{28,36},{32,40... | collective-permute-start | bytes 589832 | tf_op jit(solution)/shard_map/ppermute | solution.py:12
  11.9 8.4 %collective-permute-start.1 = (bf16[1,8,48,256]{3,2,1,0:T(8,128)(2,1)}, bf16[1,8,48,256]{3,2,1,0:T(8,128)(2,1)S(1)}, u32[]{:S(2)}, u32[]{:S(2)}) collective-permute-start(bf16[1,8,48,256]{3,2,1,0:T(8,128)(2,1)} %param.5), channel_id=1, source_target_pairs={{0,4},{4,8},{8,12},{12,16},{16,20},{20,24},{24,28},{28,32},{32,36}... | collective-permute-start | bytes 589832 | tf_op jit(solution)/shard_map/ppermute | solution.py:12
  16.3 5.0 %copy-start.29 = (bf16[1,8,48,256]{3,2,1,0:T(8,128)(2,1)}, bf16[1,8,48,256]{3,2,1,0:T(8,128)(2,1)S(1)}, u32[]{:S(2)}) copy-start(bf16[1,8,48,256]{3,2,1,0:T(8,128)(2,1)S(1)} %collective-permute-done) | copy-start | bytes 589828
  21.4 5.7 %collective-permute-start.2 = (bf16[3,1,48,256]{3,2,1,0:T(8,128)(2,1)S(1)}, bf16[3,1,48,256]{3,2,1,0:T(8,128)(2,1)S(1)}, u32[]{:S(2)}, u32[]{:S(2)}) collective-permute-start(bf16[3,1,48,256]{3,2,1,0:T(8,128)(2,1)S(1)} %get-tuple-element.58), channel_id=1, source_target_pairs={{0,1},{1,2},{2,3},{4,5},{5,6},{6,7},{8,9},{9,10},{10,11},{12,13},{... | collective-permute-start | bytes 221192 | tf_op jit(solution)/shard_map/ppermute | solution.py:20
  23.3 5.7 %collective-permute-start.3 = (bf16[3,1,48,256]{3,2,1,0:T(8,128)(2,1)S(1)}, bf16[3,1,48,256]{3,2,1,0:T(8,128)(2,1)S(1)}, u32[]{:S(2)}, u32[]{:S(2)}) collective-permute-start(bf16[3,1,48,256]{3,2,1,0:T(8,128)(2,1)S(1)} %get-tuple-element.59), channel_id=1, source_target_pairs={{1,0},{2,1},{3,2},{5,4},{6,5},{7,6},{9,8},{10,9},{11,10},{13,12},{... | collective-permute-start | bytes 221192 | tf_op jit(solution)/shard_map/ppermute | solution.py:23
  142.8 6.1 %copy-start.11 = (bf16[1,8,48,256]{3,2,1,0:T(8,128)(2,1)S(1)}, bf16[1,8,48,256]{3,2,1,0:T(8,128)(2,1)}, u32[]{:S(2)}) copy-start(bf16[1,8,48,256]{3,2,1,0:T(8,128)(2,1)} %get-tuple-element.28) | copy-start | bytes 589828
  142.8 6.3 %copy-start.10 = (bf16[1,8,48,256]{3,2,1,0:T(8,128)(2,1)S(1)}, bf16[1,8,48,256]{3,2,1,0:T(8,128)(2,1)}, u32[]{:S(2)}) copy-start(bf16[1,8,48,256]{3,2,1,0:T(8,128)(2,1)} %get-tuple-element.26) | copy-start | bytes 589828
  142.8 6.6 %copy-start.26 = (bf16[1,8,48,256]{3,2,1,0:T(8,128)(2,1)S(1)}, bf16[1,8,48,256]{3,2,1,0:T(8,128)(2,1)}, u32[]{:S(2)}) copy-start(bf16[1,8,48,256]{3,2,1,0:T(8,128)(2,1)} %get-tuple-element.55) | copy-start | bytes 589828
  142.8 6.8 %copy-start.21 = (bf16[1,8,48,256]{3,2,1,0:T(8,128)(2,1)S(1)}, bf16[1,8,48,256]{3,2,1,0:T(8,128)(2,1)}, u32[]{:S(2)}) copy-start(bf16[1,8,48,256]{3,2,1,0:T(8,128)(2,1)} %get-tuple-element.38) | copy-start | bytes 589828
  142.8 7.1 %copy-start.20 = (bf16[1,8,48,256]{3,2,1,0:T(8,128)(2,1)S(1)}, bf16[1,8,48,256]{3,2,1,0:T(8,128)(2,1)}, u32[]{:S(2)}) copy-start(bf16[1,8,48,256]{3,2,1,0:T(8,128)(2,1)} %get-tuple-element.37) | copy-start | bytes 589828
  145.2 4.9 %copy-start.30 = (bf16[1,8,48,256]{3,2,1,0:T(8,128)(2,1)S(1)}, bf16[1,8,48,256]{3,2,1,0:T(8,128)(2,1)}, u32[]{:S(2)}) copy-start(bf16[1,8,48,256]{3,2,1,0:T(8,128)(2,1)} %copy-done.29) | copy-start | bytes 589828
  147.6 2.8 copy-start.19
  148.8 1.8 copy-start.25
  149.3 1.6 copy-start.18
  149.6 1.6 copy-start.24
  152.0 1.6 copy-start.13
  152.3 1.6 copy-start.9
  152.6 1.6 copy-start.12
  154.7 9.4 %copy-start = (bf16[384,256]{1,0:T(8,128)(2,1)}, bf16[384,256]{1,0:T(8,128)(2,1)S(1)}, u32[]{:S(2)}) copy-start(bf16[384,256]{1,0:T(8,128)(2,1)S(1)} %multiply_convert_fusion) | copy-start | bytes 589828
  154.7 6.2 %collective-permute-start.4 = (bf16[1,8,48,256]{3,2,1,0:T(8,128)(2,1)S(1)}, bf16[1,8,48,256]{3,2,1,0:T(8,128)(2,1)S(1)}, u32[]{:S(2)}, u32[]{:S(2)}) collective-permute-start(bf16[1,8,48,256]{3,2,1,0:T(8,128)(2,1)S(1)} %bitcast.246), channel_id=1, source_target_pairs={{0,8},{4,12},{8,16},{12,20},{16,24},{20,28},{24,32},{28,36},{32,40... | collective-permute-start | bytes 589832 | tf_op jit(solution)/shard_map/ppermute | solution.py:12
  157.6 6.5 %collective-permute-start.5 = (bf16[1,8,48,256]{3,2,1,0:T(8,128)(2,1)S(1)}, bf16[1,8,48,256]{3,2,1,0:T(8,128)(2,1)S(1)}, u32[]{:S(2)}, u32[]{:S(2)}) collective-permute-start(bf16[1,8,48,256]{3,2,1,0:T(8,128)(2,1)S(1)} %bitcast.247), channel_id=1, source_target_pairs={{0,4},{4,8},{8,12},{12,16},{16,20},{20,24},{24,28},{28,32},{32,36}... | collective-permute-start | bytes 589832 | tf_op jit(solution)/shard_map/ppermute | solution.py:12
  160.9 3.9 copy-start.4
  164.8 104.8 %collective-permute-start.7 = (bf16[3,1,48,256]{3,2,1,0:T(8,128)(2,1)}, bf16[3,1,48,256]{3,2,1,0:T(8,128)(2,1)}, u32[]{:S(2)}, u32[]{:S(2)}) collective-permute-start(bf16[3,1,48,256]{3,2,1,0:T(8,128)(2,1)} %get-tuple-element.54), channel_id=1, source_target_pairs={{1,0},{2,1},{3,2},{5,4},{6,5},{7,6},{9,8},{10,9},{11,10},{13,12},{... | collective-permute-start | bytes 221192 | tf_op jit(solution)/shard_map/ppermute | solution.py:23
  267.6 5.9 %collective-permute-start.6 = (bf16[3,1,48,256]{3,2,1,0:T(8,128)(2,1)}, bf16[3,1,48,256]{3,2,1,0:T(8,128)(2,1)S(1)}, u32[]{:S(2)}, u32[]{:S(2)}) collective-permute-start(bf16[3,1,48,256]{3,2,1,0:T(8,128)(2,1)} %get-tuple-element.53), channel_id=1, source_target_pairs={{0,1},{1,2},{2,3},{4,5},{5,6},{6,7},{8,9},{9,10},{10,11},{12,13},{... | collective-permute-start | bytes 221192 | tf_op jit(solution)/shard_map/ppermute | solution.py:20
  277.6 2.0 copy-start.5
  405.4 4.2 copy-start.8
  414.4 20.7 %all-to-all-start = ((bf16[64,1,989]{2,1,0:T(2,128)(2,1)}), bf16[64,1,989]{2,1,0:T(2,128)(2,1)S(1)}, u32[]{:S(2)}, u32[]{:S(2)}) async-start(bf16[64,1,989]{2,1,0:T(2,128)(2,1)} %convert_element_type.72), calls=%async_computation | async-start | bytes 524288 | tf_op jit(solution)/shard_map/all_to_all | solution.py:46
  422.5 19.5 %copy-start.32 = (pred[384,384]{0,1:T(8,128)(4,1)S(1)}, pred[384,384]{0,1:T(8,128)(4,1)}, u32[]{:S(2)}) copy-start(pred[384,384]{0,1:T(8,128)(4,1)} %iota_compare_fusion.2) | copy-start | bytes 442372
  436.1 18.3 %all-to-all-start.1 = ((bf16[64,1,989]{2,1,0:T(2,128)(2,1)}), bf16[64,1,989]{2,1,0:T(2,128)(2,1)S(1)}, u32[]{:S(2)}, u32[]{:S(2)}) async-start(bf16[64,1,989]{2,1,0:T(2,128)(2,1)} %copy.22), calls=%async_computation.1 | async-start | bytes 524288 | tf_op jit(solution)/shard_map/all_to_all | solution.py:148
  (14 other events, 18.3 us)
Sparse Core Ops, SparseCore 0:
  10.8 126.5 all-gather.8
  140.9 121.3 all-gather.10
  265.9 128.8 all-gather.6
where the time goes:
time: 466 us; the launch traced here: 465 us
  waiting for transfers between devices  335 us (72%)
  starting transfers between devices  37.6 us (8%)
  matrix products  37.5 us (8%)
  local copies, waits for them, and re-layouts  26.1 us (6%)
  between operations  14.1 us (3%)
  other arithmetic  7.71 us (2%)
  blocking collectives  7.41 us (2%)
    all_gather x2, waiting for transfers between devices, causal_conv(): block_cols = lax.all_gather(weight, 'wide', axis=1, tiled=True)  200 us
    all_gather x1, waiting for transfers between devices, work_in_pieces(): blocks = [lax.all_gather(share, axis) for share in pieces]  102 us
    dot_general x54, matrix products, causal_conv(): jnp.dot(window, block_cols[kernel_tap * chan_count:(kernel_tap + 1) * cha...  18.6 us
    unnamed x71, local copies, waits for them, and re-layouts  16.3 us
    ppermute x4, starting transfers between devices, shifted(): return lax.ppermute(x, axis, pairs)  14.2 us
    all_to_all x1, waiting for transfers between devices, running(): lax.all_to_all(partial_sums.astype(jnp.bfloat16), 'wide', split_axis=0, c...  10.7 us
  transfers between devices with their start and end apart: 13, of which 11 were waited for; matrix products, arithmetic and copies ran while one was open for 10% of the time, Pallas kernels for 0%

commit v1 on v0

v1 whole, which is shorter than its diff:
```python
import jax
import jax.numpy as jnp
from jax import lax
from jax.experimental import pallas as pl
from jax.experimental.pallas import tpu as pltpu
from jax.sharding import PartitionSpec as P

HEAD_DIM = 112
NX, NZ, NY = 4, 8, 2
BF16 = jnp.bfloat16
F32 = jnp.float32


def wide_index(x, z, y):
    return (x * NZ + z) * NY + y


ALONG_Z = [
    [wide_index(x, z, y) for z in range(NZ)] for x in range(NX) for y in range(NY)
]
ALONG_XY = [
    [wide_index(x, z, y) for x in range(NX) for y in range(NY)] for z in range(NZ)
]


def delayed(x, by):
    size = lax.axis_size("wide")
    return lax.ppermute(x, "wide", [(i, i + by) for i in range(size - by)])


def other(x, mask):
    return lax.ppermute(x, "narrow", [(i, i ^ mask) for i in range(4)])


def spread(x, groups):
    count = len(groups[0])
    copies = jnp.broadcast_to(x[None], (count,) + x.shape)
    return lax.all_to_all(copies, "wide", 0, 0, axis_index_groups=groups, tiled=True)


def gather_wide(shard):
    by_z = spread(shard, ALONG_Z)
    by_xy = spread(by_z, ALONG_XY)
    blocks = by_xy.reshape((NX, NY, NZ) + shard.shape)
    return jnp.moveaxis(blocks, 1, 2).reshape((NX * NY * NZ,) + shard.shape)


def dot_nt(a, b):
    return lax.dot_general(a, b, (((1,), (1,)), ((), ())), preferred_element_type=F32)


def column_sum(prod_ref, rows, cols, width):
    col = lax.broadcasted_iota(jnp.int32, (rows, 1), 0) % cols
    left = prod_ref[7 : 7 + rows, :width]
    mid = prod_ref[8 : 8 + rows, width : 2 * width]
    right = prod_ref[9 : 9 + rows, 2 * width : 3 * width]
    return jnp.where(col != 0, left, 0.0) + mid + jnp.where(col != cols - 1, right, 0.0)


def first_conv_kernel(cols, x_ref, w_ref, o_ref, pad_ref, tap_ref, prod_ref):
    tokens = x_ref.shape[1]
    width = w_ref.shape[0]
    pad_ref[:, :cols, :] = jnp.zeros((3, cols, 256), BF16)
    pad_ref[:, cols + tokens :, :] = jnp.zeros((3, cols, 256), BF16)
    pad_ref[:, cols : cols + tokens, :] = x_ref[...]
    for tap in range(27):
        tap_ref[tap // 3, tap % 3 * width : (tap % 3 + 1) * width, :] = w_ref[
            :, tap * 256 : (tap + 1) * 256
        ]
    prod_ref[0:8, :] = jnp.zeros((8, 3 * width), F32)
    prod_ref[8 + tokens :, :] = jnp.zeros((8, 3 * width), F32)
    chunk = tokens // 4
    for part in range(4):
        total = jnp.zeros((chunk, 3 * width), F32)
        for tap in range(9):
            start = part * chunk + tap % 3 * cols
            total += dot_nt(pad_ref[tap // 3, start : start + chunk, :], tap_ref[tap])
        prod_ref[8 + part * chunk : 8 + (part + 1) * chunk, :] = total
    first = column_sum(prod_ref, tokens, cols, width)
    o_ref[...] = (first / (1.0 + jnp.exp(-first))).astype(BF16)


def first_conv(frames, weight, cols):
    tokens = frames.shape[1]
    width = weight.shape[0]

    def kernel(*refs):
        first_conv_kernel(cols, *refs)

    return pl.pallas_call(
        kernel,
        out_shape=jax.ShapeDtypeStruct((tokens, width), BF16),
        in_specs=[pl.BlockSpec(memory_space=pltpu.VMEM)] * 2,
        out_specs=pl.BlockSpec(memory_space=pltpu.VMEM),
        scratch_shapes=[
            pltpu.VMEM((3, tokens + 2 * cols, 256), BF16),
            pltpu.VMEM((9, 3 * width, 256), BF16),
            pltpu.VMEM((tokens + 16, 3 * width), F32),
        ],
        name="first_conv",
    )(frames, weight)


def second_conv_kernel(
    cols, side_ref, a2_ref, a1_ref, a0_ref, w_ref, keep_ref, send_ref, pad_ref, tap_ref, prod_ref
):
    tokens, chans = a0_ref.shape
    depth = 3 * chans
    width = w_ref.shape[0]
    half = tokens // 2
    pad_ref[:cols, :] = jnp.zeros((cols, depth), BF16)
    pad_ref[cols + tokens :, :] = jnp.zeros((cols, depth), BF16)
    pad_ref[cols : cols + tokens, :] = jnp.concatenate(
        [a2_ref[...], a1_ref[...], a0_ref[...]], axis=1
    )
    for tap in range(9):
        tap_ref[tap // 3, tap % 3 * width : (tap % 3 + 1) * width, :] = w_ref[
            :, tap * depth : (tap + 1) * depth
        ]
    prod_ref[0:8, :] = jnp.zeros((8, 3 * width), F32)
    prod_ref[8 + tokens :, :] = jnp.zeros((8, 3 * width), F32)
    chunk = tokens // 8
    for part in range(8):
        total = jnp.zeros((chunk, 3 * width), F32)
        for tap in range(3):
            start = part * chunk + tap * cols
            total += dot_nt(pad_ref[start : start + chunk, :], tap_ref[tap])
        prod_ref[8 + part * chunk : 8 + (part + 1) * chunk, :] = total
    summed = column_sum(prod_ref, tokens, cols, width)

    @pl.when(side_ref[0] == 0)
    def _():
        keep_ref[...] = summed[:half]
        send_ref[...] = summed[half:].astype(BF16)

    @pl.when(side_ref[0] == 1)
    def _():
        keep_ref[...] = summed[half:]
        send_ref[...] = summed[:half].astype(BF16)


def second_conv(side, a2, a1, a0, weight, cols):
    tokens, chans = a0.shape
    width = weight.shape[0]

    def kernel(*refs):
        second_conv_kernel(cols, *refs)

    return pl.pallas_call(
        kernel,
        out_shape=(
            jax.ShapeDtypeStruct((tokens // 2, width), F32),
            jax.ShapeDtypeStruct((tokens // 2, width), BF16),
        ),
        in_specs=[pl.BlockSpec(memory_space=pltpu.SMEM)]
        + [pl.BlockSpec(memory_space=pltpu.VMEM)] * 4,
        out_specs=(
            pl.BlockSpec(memory_space=pltpu.VMEM),
            pl.BlockSpec(memory_space=pltpu.VMEM),
        ),
        scratch_shapes=[
            pltpu.VMEM((tokens + 2 * cols, 3 * chans), BF16),
            pltpu.VMEM((3, 3 * width, 3 * chans), BF16),
            pltpu.VMEM((tokens + 16, 3 * width), F32),
        ],
        name="second_conv",
    )(side, a2, a1, a0, weight)


def whole_frames(latent):
    me = lax.axis_index("narrow")
    strip = jnp.concatenate([delayed(latent, 2), delayed(latent, 1), latent], axis=0)
    far = other(strip, 2)
    near = other(jnp.stack([strip, far]), 1)
    pieces = jnp.stack([strip, near[0], far, near[1]])
    ordered = [lax.dynamic_index_in_dim(pieces, me ^ k, 0, keepdims=False) for k in range(4)]
    frames = jnp.concatenate(ordered, axis=1)
    return frames.reshape(3, -1, latent.shape[3])


def own_column(weight, index):
    return lax.dynamic_index_in_dim(weight.T, index, 0, keepdims=False)


def per_device(latent, conv_first, conv_second, embed_weight, qkv_weight):
    row_count = latent.shape[1]
    col_count = latent.shape[2]
    chan_count = latent.shape[3]
    lane_count = 4
    me = lax.axis_index("narrow")
    core = me % 2
    chans_here = chan_count // lane_count

    first_shard = own_column(conv_first, me).reshape(-1, 128)
    first_weight = gather_wide(first_shard).reshape(chans_here, -1)

    pick = (
        lax.broadcasted_iota(jnp.int32, (chan_count, chans_here), 0)
        == lane_count * lax.broadcasted_iota(jnp.int32, (chan_count, chans_here), 1) + me
    ).astype(BF16)
    second_shard = jnp.dot(
        conv_second.T.reshape(-1, chan_count), pick, preferred_element_type=F32
    ).astype(BF16)
    second_shard = second_shard.reshape(lane_count, 3, 9, chans_here)
    second_shard = jnp.moveaxis(second_shard, 1, 2).reshape(-1, 128)
    second_weight = gather_wide(second_shard).reshape(chan_count, -1)

    quarter = embed_weight.shape[0] // 4
    embed_shard = lax.dynamic_slice_in_dim(embed_weight.T, me * quarter, quarter, axis=1)
    embed_mine = gather_wide(embed_shard.reshape(-1, 128)).reshape(-1, quarter)
    embed_pair = jnp.stack([embed_mine, other(embed_mine, 2)])
    embed_near = other(embed_pair, 1)
    embed_all = jnp.stack([embed_pair[0], embed_near[0], embed_pair[1], embed_near[1]])
    embed_all = [
        lax.dynamic_index_in_dim(embed_all, me ^ k, 0, keepdims=False) for k in range(4)
    ]

    frames = whole_frames(latent)
    activated = first_conv(frames, first_weight, col_count)
    keep, send = second_conv(
        core.astype(jnp.int32).reshape(1),
        delayed(activated, 2),
        delayed(activated, 1),
        activated,
        second_weight,
        col_count,
    )
    half = keep.shape[0]
    chip_sum = keep + other(send, 1).astype(F32)
    residual = lax.dynamic_slice_in_dim(frames[2], core * half, half, axis=0)
    block_out = chip_sum + other(chip_sum.astype(BF16), 2).astype(F32) + residual.astype(F32)
    block_out = block_out.astype(BF16)
    half_rows = half // col_count
    patches = block_out.reshape(half_rows // 2, 2, col_count // 2, 2, chan_count)
    patches = patches.transpose(0, 2, 1, 3, 4).reshape(-1, 4 * chan_count)
    near_patches = other(patches, 1)
    whole_patches = jnp.concatenate(
        [
            jnp.where(core == 0, patches, near_patches),
            jnp.where(core == 0, near_patches, patches),
        ],
        axis=0,
    )
    embedded = sum(
        dot_nt(whole_patches[:, k * quarter : (k + 1) * quarter], embed_all[k]) for k in range(4)
    ).astype(BF16)

    heads_here = qkv_weight.shape[2] // HEAD_DIM
    token_count = embedded.shape[0]
    key_raw = jnp.dot(embedded, qkv_weight[1], preferred_element_type=F32).astype(BF16).astype(F32)
    val_rows = jnp.dot(embedded, qkv_weight[2], preferred_element_type=F32).astype(BF16)
    query_raw = (
        jnp.dot(embedded, qkv_weight[0], preferred_element_type=F32).astype(BF16).astype(F32)
    )
    query_feat = (
        (jax.nn.elu(query_raw) + 1.0).astype(BF16).reshape(token_count, heads_here, HEAD_DIM)
    )
    key_feat = (jax.nn.elu(key_raw) + 1.0).astype(BF16).reshape(token_count, heads_here, HEAD_DIM)
    val_heads = val_rows.reshape(token_count, heads_here, HEAD_DIM)
    scores = jnp.einsum("thd,shd->hts", query_feat, key_feat, preferred_element_type=F32)
    row_ids = lax.broadcasted_iota(jnp.int32, (token_count, token_count), 0)
    col_ids = lax.broadcasted_iota(jnp.int32, (token_count, token_count), 1)
    scores = jnp.where((col_ids <= row_ids)[None], scores, 0.0)
    local_den = jnp.sum(scores, axis=-1)
    local_num = jnp.einsum(
        "hts,she->the", scores.astype(BF16), val_heads, preferred_element_type=F32
    )
    state_local = jnp.einsum("thd,the->hde", key_feat, val_heads, preferred_element_type=F32)
    key_local = jnp.sum(key_feat, axis=0, dtype=F32)
    flat_state = jnp.concatenate([state_local.reshape(-1), key_local.reshape(-1)])
    length_all = flat_state.shape[0]
    peer_count = lax.axis_size("wide")
    per_peer = -(-length_all // peer_count)
    piece_grid = jnp.pad(flat_state, (0, per_peer * peer_count - length_all)).reshape(
        peer_count, per_peer
    )
    lower_ones = (
        lax.broadcasted_iota(jnp.int32, (peer_count, peer_count), 1)
        < lax.broadcasted_iota(jnp.int32, (peer_count, peer_count), 0)
    ).astype(F32)
    arrived = lax.all_to_all(
        piece_grid.astype(BF16), "wide", split_axis=0, concat_axis=0, tiled=True
    )
    partial_sums = jnp.dot(lower_ones, arrived.astype(F32), precision=lax.Precision.HIGHEST)
    spread_back = lax.all_to_all(
        partial_sums.astype(BF16), "wide", split_axis=0, concat_axis=0, tiled=True
    ).astype(F32)
    flat_prefix = spread_back.reshape(-1)[:length_all]
    state_size = state_local.size
    state_prev = flat_prefix[:state_size].reshape(state_local.shape)
    key_prev = flat_prefix[state_size:].reshape(key_local.shape)
    query_wide = query_feat.astype(F32)
    carried_num = jnp.einsum(
        "thd,hde->the", query_wide, state_prev, precision=lax.Precision.HIGHEST
    )
    carried_den = jnp.einsum("thd,hd->th", query_wide, key_prev, precision=lax.Precision.HIGHEST)
    result = (local_num + carried_num) / (local_den.T + carried_den)[..., None]
    return result.astype(BF16).reshape(token_count, heads_here * HEAD_DIM)


def solution(mesh):
    return jax.shard_map(
        per_device,
        mesh=mesh,
        in_specs=(
            P("wide", "narrow", None, None),
            P(None, "wide"),
            P(None, "wide"),
            P(None, "wide"),
            P(None, None, "narrow"),
        ),
        out_specs=P("wide", "narrow"),
        check_vma=False,
    )
```

time: 466 us -> 244 us (0.52)
  waiting for transfers between devices: 335 us -> 102 us
  starting transfers between devices: 37.6 us -> 73.7 us
  matrix products: 37.5 us -> 15.6 us
  between operations: 14.1 us -> 0.48 us
  Pallas kernels: 0 us -> 11.3 us
  blocking collectives: 7.41 us -> 0 us
    all_gather x3 -> x0, waiting for transfers between devices: 302 us -> none  [the longest x2 200 us: causal_conv(): block_cols = lax.all_gather(weight, 'wide', axis=1, tiled=True)]
    all_to_all x2 -> x8, waiting for transfers between devices: 19.8 us -> 68.8 us  [the longest x6 46.9 us: spread(): lax.all_to_all(copies, 'wide', 0, 0, axis_index_groups=groups, tiled=True)]
    all_to_all x2 -> x8, starting transfers between devices: 13.9 us -> 50.8 us  [the longest x6 28.2 us: spread(): lax.all_to_all(copies, 'wide', 0, 0, axis_index_groups=groups, tiled=True)]
    dot_general x62 -> x12, matrix products: 37 us -> 15.2 us  [the longest x1 3.47 us: per_device(): jnp.dot(embedded, qkv_weight[0], preferred_element_type=F32).astype(BF16)]
    ppermute x8 -> x11, waiting for transfers between devices: 12 us -> 33.6 us  [the longest x7 28.6 us: other(): return lax.ppermute(x, 'narrow', [(i, i ^ mask) for i in range(4)])]
    unnamed x71 -> x27, local copies, waits for them, and re-layouts: 16.3 us -> 3.14 us
    pallas_call x0 -> x2, Pallas kernels: none -> 11.3 us  [the longest x1 6.29 us: second_conv(): pl.pallas_call(kernel, out_shape=(jax.ShapeDtypeStruct((tokens // 2, widt...]
    all_gather x1 -> x0, blocking collectives: 7.41 us -> none  [per_device(): whole_patches = lax.all_gather(patches, 'narrow', axis=0, tiled=True)]
  transfers between devices with their start and end apart: 13 -> 19, of which waited for: 11 -> 12; matrix products, arithmetic and copies ran while one was open for 10% -> 14% of each run, Pallas kernels for 0% -> 5%
where the time goes in v1:
time: 244 us; the launch traced here: 241 us
  waiting for transfers between devices  102 us (42%)
  starting transfers between devices  73.7 us (30%)
  local copies, waits for them, and re-layouts  27 us (11%)
  matrix products  15.6 us (6%)
  Pallas kernels  11.3 us (5%)
  other arithmetic  10.9 us (4%)
    all_to_all x6, waiting for transfers between devices, spread(): lax.all_to_all(copies, 'wide', 0, 0, axis_index_groups=groups, tiled=True)  46.9 us
    ppermute x7, waiting for transfers between devices, other(): return lax.ppermute(x, 'narrow', [(i, i ^ mask) for i in range(4)])  28.6 us
    all_to_all x6, starting transfers between devices, spread(): lax.all_to_all(copies, 'wide', 0, 0, axis_index_groups=groups, tiled=True)  28.2 us
    ppermute x4, starting transfers between devices, delayed(): return lax.ppermute(x, 'wide', [(i, i + by) for i in range(size - by)])  18.9 us
    all_to_all x1, starting transfers between devices, per_device(): lax.all_to_all(piece_grid.astype(BF16), 'wide', split_axis=0, concat_axis...  16.7 us
    all_to_all x1, waiting for transfers between devices, per_device(): lax.all_to_all(partial_sums.astype(BF16), 'wide', split_axis=0, concat_ax...  11.5 us
    all_to_all x1, waiting for transfers between devices, per_device(): lax.all_to_all(piece_grid.astype(BF16), 'wide', split_axis=0, concat_axis...  10.4 us
    pallas_call x1, Pallas kernels, second_conv(): pl.pallas_call(kernel, out_shape=(jax.ShapeDtypeStruct((tokens // 2, widt...  6.29 us
  transfers between devices with their start and end apart: 19, of which 12 were waited for; matrix products, arithmetic and copies ran while one was open for 14% of the time, Pallas kernels for 5%

profile of v1, /device:TPU:8, one launch (start us, length us, event | category | flops | bytes accessed | tf_op | source)
XLA Modules:
  0.0 241.4 jit_solution(15201746410533136161)
XLA Ops:
  0.0 4.0 %collective-permute-start = (bf16[1,8,48,256]{3,2,1,0:T(8,128)(2,1)}, bf16[1,8,48,256]{3,2,1,0:T(8,128)(2,1)S(1)}, u32[]{:S(2)}, u32[]{:S(2)}) collective-permute-start(bf16[1,8,48,256]{3,2,1,0:T(8,128)(2,1)} %param.5), channel_id=1, source_target_pairs={{0,8},{4,12},{8,16},{12,20},{16,24},{20,28},{24,32},{28,36},{32,40... | collective-permute-start | bytes 589832 | tf_op jit(solution)/shard_map/ppermute | solution.py:28
  4.0 4.2 %collective-permute-start.1 = (bf16[1,8,48,256]{3,2,1,0:T(8,128)(2,1)}, bf16[1,8,48,256]{3,2,1,0:T(8,128)(2,1)S(1)}, u32[]{:S(2)}, u32[]{:S(2)}) collective-permute-start(bf16[1,8,48,256]{3,2,1,0:T(8,128)(2,1)} %param.5), channel_id=1, source_target_pairs={{0,4},{4,8},{8,12},{12,16},{16,20},{20,24},{24,28},{28,32},{32,36}... | collective-permute-start | bytes 589832 | tf_op jit(solution)/shard_map/ppermute | solution.py:28
  9.8 7.6 %all-to-all-start = ((bf16[8,54,128]{2,1,0:T(8,128)(2,1)}), bf16[8,54,128]{2,1,0:T(8,128)(2,1)S(1)}, u32[]{:S(2)}, u32[]{:S(2)}) async-start(bf16[8,54,128]{2,1,0:T(8,128)(2,1)} %broadcast_in_dim.58), calls=%async_computation | async-start | bytes 229376 | tf_op jit(solution)/shard_map/all_to_all | solution.py:38
  18.2 8.0 %all-to-all-done = bf16[8,54,128]{2,1,0:T(8,128)(2,1)S(1)} async-done(((bf16[8,54,128]{2,1,0:T(8,128)(2,1)}), bf16[8,54,128]{2,1,0:T(8,128)(2,1)S(1)}, u32[]{:S(2)}, u32[]{:S(2)}) %all-to-all-start) | async-done | bytes 110624 | tf_op jit(solution)/shard_map/all_to_all | solution.py:38
  26.9 3.4 %all-to-all-start.4 = ((bf16[8,70,128]{2,1,0:T(8,128)(2,1)}), bf16[8,70,128]{2,1,0:T(8,128)(2,1)S(1)}, u32[]{:S(2)}, u32[]{:S(2)}) async-start(bf16[8,70,128]{2,1,0:T(8,128)(2,1)} %broadcast_in_dim.64), calls=%async_computation.4 | async-start | bytes 294912 | tf_op jit(solution)/shard_map/all_to_all | solution.py:38
  30.8 8.7 %all-to-all-done.4 = bf16[8,70,128]{2,1,0:T(8,128)(2,1)S(1)} async-done(((bf16[8,70,128]{2,1,0:T(8,128)(2,1)}), bf16[8,70,128]{2,1,0:T(8,128)(2,1)S(1)}, u32[]{:S(2)}, u32[]{:S(2)}) %all-to-all-start.4) | async-done | bytes 143392 | tf_op jit(solution)/shard_map/all_to_all | solution.py:38
  40.1 3.4 %all-to-all-start.2 = ((bf16[8,54,128]{2,1,0:T(8,128)(2,1)}), bf16[8,54,128]{2,1,0:T(8,128)(2,1)S(1)}, u32[]{:S(2)}, u32[]{:S(2)}) async-start(bf16[8,54,128]{2,1,0:T(8,128)(2,1)} %broadcast_in_dim.61), calls=%async_computation.2 | async-start | bytes 229376 | tf_op jit(solution)/shard_map/all_to_all | solution.py:38
  45.0 7.3 %all-to-all-done.2 = bf16[8,54,128]{2,1,0:T(8,128)(2,1)S(1)} async-done(((bf16[8,54,128]{2,1,0:T(8,128)(2,1)}), bf16[8,54,128]{2,1,0:T(8,128)(2,1)S(1)}, u32[]{:S(2)}, u32[]{:S(2)}) %all-to-all-start.2) | async-done | bytes 110624 | tf_op jit(solution)/shard_map/all_to_all | solution.py:38
  53.5 5.4 %all-to-all-start.5 = ((bf16[8,8,70,128]{3,1,2,0:T(8,128)(2,1)}), bf16[8,8,70,128]{3,1,2,0:T(8,128)(2,1)S(1)}, u32[]{:S(2)}, u32[]{:S(2)}) async-start(bf16[8,8,70,128]{3,1,2,0:T(8,128)(2,1)} %broadcast_in_dim.65), calls=%async_computation.5 | async-start | bytes 2293760 | tf_op jit(solution)/shard_map/all_to_all | solution.py:38
  60.2 12.2 %all-to-all-done.5 = bf16[8,8,70,128]{3,1,2,0:T(8,128)(2,1)S(1)} async-done(((bf16[8,8,70,128]{3,1,2,0:T(8,128)(2,1)}), bf16[8,8,70,128]{3,1,2,0:T(8,128)(2,1)S(1)}, u32[]{:S(2)}, u32[]{:S(2)}) %all-to-all-start.5) | async-done | bytes 1146912 | tf_op jit(solution)/shard_map/all_to_all | solution.py:38
  73.4 4.2 %all-to-all-start.1 = ((bf16[8,8,54,128]{3,1,2,0:T(8,128)(2,1)}), bf16[8,8,54,128]{3,1,2,0:T(8,128)(2,1)}, u32[]{:S(2)}, u32[]{:S(2)}) async-start(bf16[8,8,54,128]{3,1,2,0:T(8,128)(2,1)} %broadcast_in_dim.59), calls=%async_computation.1 | async-start | bytes 1769472 | tf_op jit(solution)/shard_map/all_to_all | solution.py:38
  80.5 10.8 %all-to-all-done.1 = bf16[8,8,54,128]{3,1,2,0:T(8,128)(2,1)} async-done(((bf16[8,8,54,128]{3,1,2,0:T(8,128)(2,1)}), bf16[8,8,54,128]{3,1,2,0:T(8,128)(2,1)}, u32[]{:S(2)}, u32[]{:S(2)}) %all-to-all-start.1) | async-done | bytes 884768 | tf_op jit(solution)/shard_map/all_to_all | solution.py:38
  92.4 4.2 %all-to-all-start.3 = ((bf16[8,8,54,128]{3,1,2,0:T(8,128)(2,1)}), bf16[8,8,54,128]{3,1,2,0:T(8,128)(2,1)}, u32[]{:S(2)}, u32[]{:S(2)}) async-start(bf16[8,8,54,128]{3,1,2,0:T(8,128)(2,1)} %broadcast_in_dim.62), calls=%async_computation.3 | async-start | bytes 1769472 | tf_op jit(solution)/shard_map/all_to_all | solution.py:38
  101.7 17.1 %collective-permute-done.9 = bf16[2240,256]{1,0:T(8,128)(2,1)S(1)} collective-permute-done((bf16[2240,256]{1,0:T(8,128)(2,1)}, bf16[2240,256]{1,0:T(8,128)(2,1)S(1)}, u32[]{:S(2)}, u32[]{:S(2)}) %collective-permute-start.9) | collective-permute-done | bytes 1146912 | tf_op jit(solution)/shard_map/ppermute | solution.py:32
  122.2 5.0 %first_conv.1.refs_3_ = bf16[1536,64]{1,0:T(8,128)(2,1)} custom-call(bf16[3,1536,256]{2,1,0:T(8,128)(2,1)} %bitcast.118, bf16[64,6912]{1,0:T(8,128)(2,1)} %bitcast.123), custom_call_target="tpu_custom_call" | custom-call | tf_op jit(solution)/shard_map/first_conv/pallas_call | solution.py:90
  127.2 4.2 %collective-permute-start.4 = (bf16[1536,64]{1,0:T(8,128)(2,1)}, bf16[1536,64]{1,0:T(8,128)(2,1)}, u32[]{:S(2)}, u32[]{:S(2)}) collective-permute-start(bf16[1536,64]{1,0:T(8,128)(2,1)} %first_conv.1.refs_3_), channel_id=1, source_target_pairs={{0,8},{4,12},{8,16},{12,20},{16,24},{20,28},{24,32},{28,36},{32,40... | collective-permute-start | bytes 589832 | tf_op jit(solution)/shard_map/ppermute | solution.py:28
  131.4 6.5 %collective-permute-start.5 = (bf16[1536,64]{1,0:T(8,128)(2,1)}, bf16[1536,64]{1,0:T(8,128)(2,1)}, u32[]{:S(2)}, u32[]{:S(2)}) collective-permute-start(bf16[1536,64]{1,0:T(8,128)(2,1)} %first_conv.1.refs_3_), channel_id=1, source_target_pairs={{0,4},{4,8},{8,12},{12,16},{16,20},{20,24},{24,28},{28,32},{32,36}... | collective-permute-start | bytes 589832 | tf_op jit(solution)/shard_map/ppermute | solution.py:28
  139.2 1.9 reshape_reshape.10.refs_4_
  141.1 5.1 %collective-permute-done.5.refs_2_ = bf16[1536,64]{1,0:T(8,128)(2,1)} collective-permute-done((bf16[1536,64]{1,0:T(8,128)(2,1)}, bf16[1536,64]{1,0:T(8,128)(2,1)}, u32[]{:S(2)}, u32[]{:S(2)}) %collective-permute-start.5) | collective-permute-done | bytes 196640 | tf_op jit(solution)/shard_map/ppermute | solution.py:28
  146.2 6.3 %second_conv.1 = (f32[768,256]{1,0:T(8,128)}, bf16[768,256]{1,0:T(8,128)(2,1)}) custom-call(s32[1]{0:T(128)} %bitcast.refs_0_, bf16[1536,64]{1,0:T(8,128)(2,1)} %collective-permute-done.4.refs_1_, bf16[1536,64]{1,0:T(8,128)(2,1)} %collective-permute-done.5.refs_2_, bf16[1536,64]{1,0:T(8,128)(2,1)} %first_conv.1.refs_3_, ...), custom_call_target="tpu_custom_call" | custom-call | tf_op jit(solution)/shard_map/second_conv/pallas_call | solution.py:149
  152.5 1.9 collective-permute-done.6
  154.4 2.0 fusion.61
  156.4 1.9 collective-permute-start.7
  159.5 8.5 %collective-permute-done.7 = bf16[768,256]{1,0:T(8,128)(2,1)} collective-permute-done((bf16[768,256]{1,0:T(8,128)(2,1)}, bf16[768,256]{1,0:T(8,128)(2,1)}, u32[]{:S(2)}, u32[]{:S(2)}) %collective-permute-start.7) | collective-permute-done | bytes 393248 | tf_op jit(solution)/shard_map/ppermute | solution.py:32
  168.1 1.9 add_convert_fusion
  181.0 1.9 fusion.89
  185.9 16.7 %all-to-all-start.6 = ((bf16[64,1,989]{2,1,0:T(2,128)(2,1)}), bf16[64,1,989]{2,1,0:T(2,128)(2,1)S(1)}, u32[]{:S(2)}, u32[]{:S(2)}) async-start(bf16[64,1,989]{2,1,0:T(2,128)(2,1)} %convert_element_type.96), calls=%async_computation.6 | async-start | bytes 524288 | tf_op jit(solution)/shard_map/all_to_all | solution.py:281
  202.6 3.5 %fusion.49 = bf16[384,560]{0,1:T(8,128)(2,1)S(1)} fusion(bf16[384,2240]{0,1:T(8,128)(2,1)S(1)} %fusion, bf16[3,2240,560]{1,2,0:T(8,128)(2,1)} %param.9), kind=kOutput, calls=%fused_computation.59 | convolution fusion | flops 964884480 | bytes 4730880 | tf_op jit(solution)/shard_map/dot_general | solution.py:253
  206.1 10.4 %all-to-all-done.6 = bf16[64,1,989]{2,1,0:T(2,128)(2,1)S(1)} async-done(((bf16[64,1,989]{2,1,0:T(2,128)(2,1)}), bf16[64,1,989]{2,1,0:T(2,128)(2,1)S(1)}, u32[]{:S(2)}, u32[]{:S(2)}) %all-to-all-start.6) | async-done | bytes 126624 | tf_op jit(solution)/shard_map/all_to_all | solution.py:281
  217.6 6.0 %all-to-all-start.7 = ((bf16[64,1,989]{2,1,0:T(2,128)(2,1)}), bf16[64,1,989]{2,1,0:T(2,128)(2,1)S(1)}, u32[]{:S(2)}, u32[]{:S(2)}) async-start(bf16[64,1,989]{2,1,0:T(2,128)(2,1)} %copy.49), calls=%async_computation.7 | async-start | bytes 524288 | tf_op jit(solution)/shard_map/all_to_all | solution.py:285
  225.5 11.5 %all-to-all-done.7 = bf16[64,1,989]{2,1,0:T(2,128)(2,1)S(1)} async-done(((bf16[64,1,989]{2,1,0:T(2,128)(2,1)}), bf16[64,1,989]{2,1,0:T(2,128)(2,1)S(1)}, u32[]{:S(2)}, u32[]{:S(2)}) %all-to-all-start.7) | async-done | bytes 126624 | tf_op jit(solution)/shard_map/all_to_all | solution.py:285
  238.8 2.6 %fusion.31 = bf16[384,5,112]{0,2,1:T(8,128)(2,1)} fusion(f32[5,112,384]{2,1,0:T(8,128)S(1)} %fusion.90, bf16[384,5,112]{0,2,1:T(8,128)(2,1)S(1)} %bitcast.135, bf16[5,384,384]{1,2,0:T(8,128)(2,1)} %get-tuple-element.22, pred[384,384]{0,1:T(8,128)(4,1)S(1)} %copy-done.9, f32[384,5]{0,1:T(8,128)S(1)} %fusion.77), kind=kOutput, calls=%fused_computation.34 | convolution fusion | flops 166533120 | bytes 3350016 | tf_op jit(solution)/shard_map/hts,she->the/dot_general | solution.py:265
  (101 shorter events, 42.8 us)
Async XLA Ops:
  0.0 18.2 %copy-start = (bf16[1024,35]{0,1:T(8,128)(2,1)S(1)}, bf16[1024,35]{0,1:T(8,128)(2,1)}, u32[]{:S(2)}) copy-start(bf16[1024,35]{0,1:T(8,128)(2,1)} %param.8) | copy-start | bytes 215044
  0.0 43.5 %copy-start.8 = (bf16[1,8,48,256]{3,2,1,0:T(8,128)(2,1)S(1)}, bf16[1,8,48,256]{3,2,1,0:T(8,128)(2,1)}, u32[]{:S(2)}) copy-start(bf16[1,8,48,256]{3,2,1,0:T(8,128)(2,1)} %param.5) | copy-start | bytes 589828
  0.0 30.7 %collective-permute-start = (bf16[1,8,48,256]{3,2,1,0:T(8,128)(2,1)}, bf16[1,8,48,256]{3,2,1,0:T(8,128)(2,1)S(1)}, u32[]{:S(2)}, u32[]{:S(2)}) collective-permute-start(bf16[1,8,48,256]{3,2,1,0:T(8,128)(2,1)} %param.5), channel_id=1, source_target_pairs={{0,8},{4,12},{8,16},{12,20},{16,24},{20,28},{24,32},{28,36},{32,40... | collective-permute-start | bytes 589832 | tf_op jit(solution)/shard_map/ppermute | solution.py:28
  4.0 26.8 %collective-permute-start.1 = (bf16[1,8,48,256]{3,2,1,0:T(8,128)(2,1)}, bf16[1,8,48,256]{3,2,1,0:T(8,128)(2,1)S(1)}, u32[]{:S(2)}, u32[]{:S(2)}) collective-permute-start(bf16[1,8,48,256]{3,2,1,0:T(8,128)(2,1)} %param.5), channel_id=1, source_target_pairs={{0,4},{4,8},{8,12},{12,16},{16,20},{20,24},{24,28},{28,32},{32,36}... | collective-permute-start | bytes 589832 | tf_op jit(solution)/shard_map/ppermute | solution.py:28
  9.8 16.5 %all-to-all-start = ((bf16[8,54,128]{2,1,0:T(8,128)(2,1)}), bf16[8,54,128]{2,1,0:T(8,128)(2,1)S(1)}, u32[]{:S(2)}, u32[]{:S(2)}) async-start(bf16[8,54,128]{2,1,0:T(8,128)(2,1)} %broadcast_in_dim.58), calls=%async_computation | async-start | bytes 229376 | tf_op jit(solution)/shard_map/all_to_all | solution.py:38
  26.9 12.6 %all-to-all-start.4 = ((bf16[8,70,128]{2,1,0:T(8,128)(2,1)}), bf16[8,70,128]{2,1,0:T(8,128)(2,1)S(1)}, u32[]{:S(2)}, u32[]{:S(2)}) async-start(bf16[8,70,128]{2,1,0:T(8,128)(2,1)} %broadcast_in_dim.64), calls=%async_computation.4 | async-start | bytes 294912 | tf_op jit(solution)/shard_map/all_to_all | solution.py:38
  40.1 12.2 %all-to-all-start.2 = ((bf16[8,54,128]{2,1,0:T(8,128)(2,1)}), bf16[8,54,128]{2,1,0:T(8,128)(2,1)S(1)}, u32[]{:S(2)}, u32[]{:S(2)}) async-start(bf16[8,54,128]{2,1,0:T(8,128)(2,1)} %broadcast_in_dim.61), calls=%async_computation.2 | async-start | bytes 229376 | tf_op jit(solution)/shard_map/all_to_all | solution.py:38
  43.5 16.6 %copy-start.2 = (bf16[3,8,48,256]{3,2,1,0:T(8,128)(2,1)}, bf16[3,8,48,256]{3,2,1,0:T(8,128)(2,1)S(1)}, u32[]{:S(2)}) copy-start(bf16[3,8,48,256]{3,2,1,0:T(8,128)(2,1)S(1)} %constant_dynamic-update-slice_fusion) | copy-start | bytes 1769476
  43.5 15.4 %collective-permute-start.2 = (bf16[3,8,48,256]{3,2,1,0:T(8,128)(2,1)S(1)}, bf16[3,8,48,256]{3,2,1,0:T(8,128)(2,1)S(1)}, u32[]{:S(2)}, u32[]{:S(2)}) collective-permute-start(bf16[3,8,48,256]{3,2,1,0:T(8,128)(2,1)S(1)} %constant_dynamic-update-slice_fusion), channel_id=1, source_target_pairs={{0,2},{1,3},{2,0},{3,1},{4,6},{5,7},{6,4},{7,5},{8,10},{9,11},{10,... | collective-permute-start | bytes 1769480 | tf_op jit(solution)/shard_map/ppermute | solution.py:32
  52.3 1.2 copy-start.7
  53.5 18.9 %all-to-all-start.5 = ((bf16[8,8,70,128]{3,1,2,0:T(8,128)(2,1)}), bf16[8,8,70,128]{3,1,2,0:T(8,128)(2,1)S(1)}, u32[]{:S(2)}, u32[]{:S(2)}) async-start(bf16[8,8,70,128]{3,1,2,0:T(8,128)(2,1)} %broadcast_in_dim.65), calls=%async_computation.5 | async-start | bytes 2293760 | tf_op jit(solution)/shard_map/all_to_all | solution.py:38
  58.9 14.5 %copy-start.5 = (bf16[3,8,48,256]{3,2,1,0:T(8,128)(2,1)}, bf16[3,8,48,256]{3,2,1,0:T(8,128)(2,1)S(1)}, u32[]{:S(2)}) copy-start(bf16[3,8,48,256]{3,2,1,0:T(8,128)(2,1)S(1)} %collective-permute-done.2) | copy-start | bytes 1769476
  60.2 39.5 %collective-permute-start.3 = (bf16[2,3,8,48,256]{4,3,2,1,0:T(8,128)(2,1)}, bf16[2,3,8,48,256]{4,3,2,1,0:T(8,128)(2,1)}, u32[]{:S(2)}, u32[]{:S(2)}) collective-permute-start(bf16[2,3,8,48,256]{4,3,2,1,0:T(8,128)(2,1)} %pad_maximum_fusion.4), channel_id=1, source_target_pairs={{0,1},{1,0},{2,3},{3,2},{4,5},{5,4},{6,7},{7,6},{8,9},{9,8},{10,11... | collective-permute-start | bytes 3538952 | tf_op jit(solution)/shard_map/ppermute | solution.py:32
  73.4 18.0 %all-to-all-start.1 = ((bf16[8,8,54,128]{3,1,2,0:T(8,128)(2,1)}), bf16[8,8,54,128]{3,1,2,0:T(8,128)(2,1)}, u32[]{:S(2)}, u32[]{:S(2)}) async-start(bf16[8,8,54,128]{3,1,2,0:T(8,128)(2,1)} %broadcast_in_dim.59), calls=%async_computation.1 | async-start | bytes 1769472 | tf_op jit(solution)/shard_map/all_to_all | solution.py:38
  79.2 39.7 %collective-permute-start.9 = (bf16[2240,256]{1,0:T(8,128)(2,1)}, bf16[2240,256]{1,0:T(8,128)(2,1)S(1)}, u32[]{:S(2)}, u32[]{:S(2)}) collective-permute-start(bf16[2240,256]{1,0:T(8,128)(2,1)} %reshape_reshape.11), channel_id=1, source_target_pairs={{0,2},{1,3},{2,0},{3,1},{4,6},{5,7},{6,4},{7,5},{8,10},{9,11},{10,... | collective-permute-start | bytes 3440648 | tf_op jit(solution)/shard_map/ppermute | solution.py:32
  92.4 45.5 %all-to-all-start.3 = ((bf16[8,8,54,128]{3,1,2,0:T(8,128)(2,1)}), bf16[8,8,54,128]{3,1,2,0:T(8,128)(2,1)}, u32[]{:S(2)}, u32[]{:S(2)}) async-start(bf16[8,8,54,128]{3,1,2,0:T(8,128)(2,1)} %broadcast_in_dim.62), calls=%async_computation.3 | async-start | bytes 1769472 | tf_op jit(solution)/shard_map/all_to_all | solution.py:38
  99.6 1.4 copy-start.3
  99.6 1.6 copy-start.6
  120.5 53.1 %collective-permute-start.10 = (bf16[2,2240,256]{2,1,0:T(8,128)(2,1)}, bf16[2,2240,256]{2,1,0:T(8,128)(2,1)}, u32[]{:S(2)}, u32[]{:S(2)}) collective-permute-start(bf16[2,2240,256]{2,1,0:T(8,128)(2,1)} %pad_maximum_fusion.3), channel_id=1, source_target_pairs={{0,1},{1,0},{2,3},{3,2},{4,5},{5,4},{6,7},{7,6},{8,9},{9,8},{10,11... | collective-permute-start | bytes 6881288 | tf_op jit(solution)/shard_map/ppermute | solution.py:32
  127.2 14.0 %collective-permute-start.4 = (bf16[1536,64]{1,0:T(8,128)(2,1)}, bf16[1536,64]{1,0:T(8,128)(2,1)}, u32[]{:S(2)}, u32[]{:S(2)}) collective-permute-start(bf16[1536,64]{1,0:T(8,128)(2,1)} %first_conv.1.refs_3_), channel_id=1, source_target_pairs={{0,8},{4,12},{8,16},{12,20},{16,24},{20,28},{24,32},{28,36},{32,40... | collective-permute-start | bytes 589832 | tf_op jit(solution)/shard_map/ppermute | solution.py:28
  131.4 14.8 %collective-permute-start.5 = (bf16[1536,64]{1,0:T(8,128)(2,1)}, bf16[1536,64]{1,0:T(8,128)(2,1)}, u32[]{:S(2)}, u32[]{:S(2)}) collective-permute-start(bf16[1536,64]{1,0:T(8,128)(2,1)} %first_conv.1.refs_3_), channel_id=1, source_target_pairs={{0,4},{4,8},{8,12},{12,16},{16,20},{20,24},{24,28},{28,32},{32,36}... | collective-permute-start | bytes 589832 | tf_op jit(solution)/shard_map/ppermute | solution.py:28
  152.5 15.6 %copy-start.4 = (f32[768,256]{1,0:T(8,128)S(1)}, f32[768,256]{1,0:T(8,128)}, u32[]{:S(2)}) copy-start(f32[768,256]{1,0:T(8,128)} %get-tuple-element.7) | copy-start | bytes 2359300
  152.5 1.9 collective-permute-start.6
  156.4 11.7 %collective-permute-start.7 = (bf16[768,256]{1,0:T(8,128)(2,1)}, bf16[768,256]{1,0:T(8,128)(2,1)}, u32[]{:S(2)}, u32[]{:S(2)}) collective-permute-start(bf16[768,256]{1,0:T(8,128)(2,1)} %fusion.61), channel_id=1, source_target_pairs={{0,2},{1,3},{2,0},{3,1},{4,6},{5,7},{6,4},{7,5},{8,10},{9,11},{10,... | collective-permute-start | bytes 1179656 | tf_op jit(solution)/shard_map/ppermute | solution.py:32
  171.7 1.8 collective-permute-start.8
  177.5 2.2 slice-start
  178.3 2.7 %slice-start.1 = ((s8[7741440]{0:T(1024)(128)(4,1)}), s8[3547136]{0:T(1024)(128)(4,1)S(1)}, s32[]{:S(2)}) async-start(s8[7741440]{0:T(1024)(128)(4,1)} %bitcast.141), calls=%async_computation.9 | async-start | bytes 7094272
  185.9 30.6 %all-to-all-start.6 = ((bf16[64,1,989]{2,1,0:T(2,128)(2,1)}), bf16[64,1,989]{2,1,0:T(2,128)(2,1)S(1)}, u32[]{:S(2)}, u32[]{:S(2)}) async-start(bf16[64,1,989]{2,1,0:T(2,128)(2,1)} %convert_element_type.96), calls=%async_computation.6 | async-start | bytes 524288 | tf_op jit(solution)/shard_map/all_to_all | solution.py:281
  202.6 21.0 %copy-start.9 = (pred[384,384]{0,1:T(8,128)(4,1)S(1)}, pred[384,384]{0,1:T(8,128)(4,1)}, u32[]{:S(2)}) copy-start(pred[384,384]{0,1:T(8,128)(4,1)} %iota_compare_fusion) | copy-start | bytes 442372
  217.6 19.3 %all-to-all-start.7 = ((bf16[64,1,989]{2,1,0:T(2,128)(2,1)}), bf16[64,1,989]{2,1,0:T(2,128)(2,1)S(1)}, u32[]{:S(2)}, u32[]{:S(2)}) async-start(bf16[64,1,989]{2,1,0:T(2,128)(2,1)} %copy.49), calls=%async_computation.7 | async-start | bytes 524288 | tf_op jit(solution)/shard_map/all_to_all | solution.py:285
  238.8 2.7 %copy-start.1 = (bf16[1024,35]{0,1:T(8,128)(2,1)S(1)}, bf16[1024,35]{0,1:T(8,128)(2,1)}, u32[]{:S(2)}) copy-start(bf16[1024,35]{0,1:T(8,128)(2,1)} %param.8) | copy-start | bytes 215044

commit v2 on v1

--- a/solution.py
+++ b/solution.py
@@ -5,8 +5,10 @@
 from jax.experimental.pallas import tpu as pltpu
 from jax.sharding import PartitionSpec as P
 
+
 HEAD_DIM = 112
 NX, NZ, NY = 4, 8, 2
+BOTH = ("wide", "narrow")
 BF16 = jnp.bfloat16
 F32 = jnp.float32
 
@@ -19,30 +21,33 @@
     [wide_index(x, z, y) for z in range(NZ)] for x in range(NX) for y in range(NY)
 ]
 ALONG_XY = [
-    [wide_index(x, z, y) for x in range(NX) for y in range(NY)] for z in range(NZ)
+    [wide_index(x, z, y) * 4 + (role ^ 2 * y) for x in range(NX) for y in range(NY)]
+    for z in range(NZ)
+    for role in range(4)
 ]
 
 
 def delayed(x, by):
     size = lax.axis_size("wide")
-    return lax.ppermute(x, "wide", [(i, i + by) for i in range(size - by)])
+    pairs = [
+        (4 * i + n, 4 * (i + by) + (n ^ 2 * (by % 2))) for i in range(size - by) for n in range(4)
+    ]
+    return lax.ppermute(x, BOTH, pairs)
 
 
 def other(x, mask):
     return lax.ppermute(x, "narrow", [(i, i ^ mask) for i in range(4)])
 
 
-def spread(x, groups):
+def spread(x, axis, groups):
     count = len(groups[0])
     copies = jnp.broadcast_to(x[None], (count,) + x.shape)
-    return lax.all_to_all(copies, "wide", 0, 0, axis_index_groups=groups, tiled=True)
-
-
-def gather_wide(shard):
-    by_z = spread(shard, ALONG_Z)
-    by_xy = spread(by_z, ALONG_XY)
-    blocks = by_xy.reshape((NX, NY, NZ) + shard.shape)
-    return jnp.moveaxis(blocks, 1, 2).reshape((NX * NY * NZ,) + shard.shape)
+    return lax.all_to_all(copies, axis, 0, 0, axis_index_groups=groups, tiled=True)
+
+
+def in_wide_order(by_xy, shape):
+    blocks = by_xy.reshape((NX, NY, NZ) + shape)
+    return jnp.moveaxis(blocks, 1, 2).reshape((NX * NY * NZ,) + shape)
 
 
 def dot_nt(a, b):
@@ -57,12 +62,24 @@
     return jnp.where(col != 0, left, 0.0) + mid + jnp.where(col != cols - 1, right, 0.0)
 
 
-def first_conv_kernel(cols, x_ref, w_ref, o_ref, pad_ref, tap_ref, prod_ref):
-    tokens = x_ref.shape[1]
+def first_conv_kernel(
+    cols, me_ref, now0, now1, now2, now3, old0, old1, old2, old3, w_ref, o_ref, res_ref,
+    pad_ref, tap_ref, prod_ref,
+):
+    strip = now0.shape[0]
+    tokens = 4 * strip
     width = w_ref.shape[0]
+    me = me_ref[0]
     pad_ref[:, :cols, :] = jnp.zeros((3, cols, 256), BF16)
     pad_ref[:, cols + tokens :, :] = jnp.zeros((3, cols, 256), BF16)
-    pad_ref[:, cols : cols + tokens, :] = x_ref[...]
+    for k, (now, old) in enumerate(((now0, old0), (now1, old1), (now2, old2), (now3, old3))):
+        place = pl.ds(pl.multiple_of(cols + (me ^ k) * strip, 16), strip)
+        pad_ref[2, place, :] = now[...]
+        pad_ref[0, place, :] = old[0]
+        place = pl.ds(pl.multiple_of(cols + (me ^ k ^ 2) * strip, 16), strip)
+        pad_ref[1, place, :] = old[1]
+    half = tokens // 2
+    res_ref[...] = pad_ref[2, pl.ds(pl.multiple_of(cols + (me & 1) * half, 16), half), :]
     for tap in range(27):
         tap_ref[tap // 3, tap % 3 * width : (tap % 3 + 1) * width, :] = w_ref[
             :, tap * 256 : (tap + 1) * 256
@@ -80,8 +97,12 @@
     o_ref[...] = (first / (1.0 + jnp.exp(-first))).astype(BF16)
 
 
-def first_conv(frames, weight, cols):
-    tokens = frames.shape[1]
+VMEM_SPEC = pl.BlockSpec(memory_space=pltpu.VMEM)
+SMEM_SPEC = pl.BlockSpec(memory_space=pltpu.SMEM)
+
+
+def first_conv(me, now, old, weight, cols):
+    tokens = 4 * now[0].shape[0]
     width = weight.shape[0]
 
     def kernel(*refs):
@@ -89,16 +110,19 @@
 
     return pl.pallas_call(
         kernel,
-        out_shape=jax.ShapeDtypeStruct((tokens, width), BF16),
-        in_specs=[pl.BlockSpec(memory_space=pltpu.VMEM)] * 2,
-        out_specs=pl.BlockSpec(memory_space=pltpu.VMEM),
+        out_shape=(
+            jax.ShapeDtypeStruct((tokens, width), BF16),
+            jax.ShapeDtypeStruct((tokens // 2, 256), BF16),
+        ),
+        in_specs=[SMEM_SPEC] + [VMEM_SPEC] * 9,
+        out_specs=(VMEM_SPEC, VMEM_SPEC),
         scratch_shapes=[
             pltpu.VMEM((3, tokens + 2 * cols, 256), BF16),
             pltpu.VMEM((9, 3 * width, 256), BF16),
             pltpu.VMEM((tokens + 16, 3 * width), F32),
         ],
         name="first_conv",
-    )(frames, weight)
+    )(me, *now, *old, weight)
 
 
 def second_conv_kernel(
@@ -152,12 +176,8 @@
             jax.ShapeDtypeStruct((tokens // 2, width), F32),
             jax.ShapeDtypeStruct((tokens // 2, width), BF16),
         ),
-        in_specs=[pl.BlockSpec(memory_space=pltpu.SMEM)]
-        + [pl.BlockSpec(memory_space=pltpu.VMEM)] * 4,
-        out_specs=(
-            pl.BlockSpec(memory_space=pltpu.VMEM),
-            pl.BlockSpec(memory_space=pltpu.VMEM),
-        ),
+        in_specs=[SMEM_SPEC] + [VMEM_SPEC] * 4,
+        out_specs=(VMEM_SPEC, VMEM_SPEC),
         scratch_shapes=[
             pltpu.VMEM((tokens + 2 * cols, 3 * chans), BF16),
             pltpu.VMEM((3, 3 * width, 3 * chans), BF16),
@@ -167,15 +187,73 @@
     )(side, a2, a1, a0, weight)
 
 
-def whole_frames(latent):
-    me = lax.axis_index("narrow")
-    strip = jnp.concatenate([delayed(latent, 2), delayed(latent, 1), latent], axis=0)
-    far = other(strip, 2)
-    near = other(jnp.stack([strip, far]), 1)
-    pieces = jnp.stack([strip, near[0], far, near[1]])
-    ordered = [lax.dynamic_index_in_dim(pieces, me ^ k, 0, keepdims=False) for k in range(4)]
-    frames = jnp.concatenate(ordered, axis=1)
-    return frames.reshape(3, -1, latent.shape[3])
+def chip_sum_kernel(keep_ref, near_ref, o_ref):
+    o_ref[...] = (keep_ref[...] + near_ref[...].astype(F32)).astype(BF16)
+
+
+def chip_sum(keep, near):
+    return pl.pallas_call(
+        chip_sum_kernel,
+        out_shape=jax.ShapeDtypeStruct(keep.shape, BF16),
+        in_specs=[VMEM_SPEC] * 2,
+        out_specs=VMEM_SPEC,
+        name="chip_sum",
+    )(keep, near)
+
+
+def patch_kernel(cols, mine_ref, far_ref, res_ref, o_ref, whole_ref):
+    chans = mine_ref.shape[1]
+    rows = mine_ref.shape[0] // cols
+    block = mine_ref[...].astype(F32) + far_ref[...].astype(F32) + res_ref[...].astype(F32)
+    for part in range(chans // 128):
+        whole_ref[part] = block[:, part * 128 : (part + 1) * 128]
+    for p in range(rows // 2):
+        for b in range(2):
+            for e in range(2):
+                for part in range(chans // 128):
+                    lane = (b * 2 + e) * chans + part * 128
+                    o_ref[p * cols // 2 : (p + 1) * cols // 2, lane : lane + 128] = whole_ref[
+                        part, pl.ds((2 * p + b) * cols + e, cols // 2, stride=2), :
+                    ].astype(BF16)
+
+
+def patch_rows(mine, far, res, cols):
+    tokens, chans = mine.shape
+
+    def kernel(*refs):
+        patch_kernel(cols, *refs)
+
+    return pl.pallas_call(
+        kernel,
+        out_shape=jax.ShapeDtypeStruct((tokens // 4, 4 * chans), BF16),
+        in_specs=[VMEM_SPEC] * 3,
+        out_specs=VMEM_SPEC,
+        scratch_shapes=[pltpu.VMEM((chans // 128, tokens, 128), F32)],
+        name="patch_rows",
+    )(mine, far, res)
+
+
+def embed_kernel(me_ref, role_ref, mine_ref, near_ref, w0, w1, w2, w3, o_ref):
+    half = mine_ref.shape[0]
+    depth = w0.shape[1]
+    core = me_ref[0] & 1
+    for side, ref in ((core, mine_ref), (1 - core, near_ref)):
+        total = None
+        for k, w_ref in enumerate((w0, w1, w2, w3)):
+            lanes = pl.ds(pl.multiple_of((role_ref[0] ^ k) * depth, depth), depth)
+            part = dot_nt(ref[:, lanes], w_ref[...])
+            total = part if total is None else total + part
+        o_ref[pl.ds(pl.multiple_of(side * half, 16), half), :] = total.astype(BF16)
+
+
+def embed_tokens(me, role, mine, near, weights):
+    return pl.pallas_call(
+        embed_kernel,
+        out_shape=jax.ShapeDtypeStruct((2 * mine.shape[0], weights[0].shape[0]), BF16),
+        in_specs=[SMEM_SPEC] * 2 + [VMEM_SPEC] * 6,
+        out_specs=VMEM_SPEC,
+        name="embed_tokens",
+    )(me, role, mine, near, *weights)
 
 
 def own_column(weight, index):
@@ -183,7 +261,6 @@
 
 
 def per_device(latent, conv_first, conv_second, embed_weight, qkv_weight):
-    row_count = latent.shape[1]
     col_count = latent.shape[2]
     chan_count = latent.shape[3]
     lane_count = 4
@@ -191,32 +268,49 @@
     core = me % 2
     chans_here = chan_count // lane_count
 
-    first_shard = own_column(conv_first, me).reshape(-1, 128)
-    first_weight = gather_wide(first_shard).reshape(chans_here, -1)
+    odd = lax.axis_index("wide") % NY == 1
+    role = jnp.where(odd, me ^ 2, me)
+    me_ref = me.astype(jnp.int32).reshape(1)
+
+    mine = latent.reshape(-1, chan_count)
+    far = other(mine, 2)
+    near = other(mine, 1)
+    cross = other(far, 1)
+    old = jnp.stack([delayed(mine, 2), delayed(mine, 1)])
+    old_far = other(old, 2)
+    old_near = other(old, 1)
+    old_cross = other(old_far, 1)
 
     pick = (
         lax.broadcasted_iota(jnp.int32, (chan_count, chans_here), 0)
-        == lane_count * lax.broadcasted_iota(jnp.int32, (chan_count, chans_here), 1) + me
+        == lane_count * lax.broadcasted_iota(jnp.int32, (chan_count, chans_here), 1) + role
     ).astype(BF16)
+    first_shard = own_column(conv_first, role).reshape(-1, 128)
     second_shard = jnp.dot(
         conv_second.T.reshape(-1, chan_count), pick, preferred_element_type=F32
     ).astype(BF16)
     second_shard = second_shard.reshape(lane_count, 3, 9, chans_here)
     second_shard = jnp.moveaxis(second_shard, 1, 2).reshape(-1, 128)
-    second_weight = gather_wide(second_shard).reshape(chan_count, -1)
-
     quarter = embed_weight.shape[0] // 4
-    embed_shard = lax.dynamic_slice_in_dim(embed_weight.T, me * quarter, quarter, axis=1)
-    embed_mine = gather_wide(embed_shard.reshape(-1, 128)).reshape(-1, quarter)
-    embed_pair = jnp.stack([embed_mine, other(embed_mine, 2)])
-    embed_near = other(embed_pair, 1)
-    embed_all = jnp.stack([embed_pair[0], embed_near[0], embed_pair[1], embed_near[1]])
-    embed_all = [
-        lax.dynamic_index_in_dim(embed_all, me ^ k, 0, keepdims=False) for k in range(4)
-    ]
-
-    frames = whole_frames(latent)
-    activated = first_conv(frames, first_weight, col_count)
+    embed_shard = lax.dynamic_slice_in_dim(embed_weight.T, role * quarter, quarter, axis=1)
+    embed_shard = embed_shard.reshape(-1, 128)
+    shards = jnp.concatenate([first_shard, second_shard, embed_shard])
+    by_z = spread(shards, "wide", ALONG_Z)
+    split = first_shard.shape[0]
+    conv_weights = spread(by_z[:, : 2 * split], BOTH, ALONG_XY)
+    conv_weights = in_wide_order(conv_weights, (2 * split, 128))
+    first_weight = conv_weights[:, :split].reshape(chans_here, -1)
+    second_weight = conv_weights[:, split:].reshape(chan_count, -1)
+    embed_mine = spread(by_z[:, 2 * split :], BOTH, ALONG_XY)
+    embed_mine = in_wide_order(embed_mine, embed_shard.shape).reshape(-1, quarter)
+    embed_far = other(embed_mine, 2)
+    embed_near = other(embed_mine, 1)
+    embed_cross = other(embed_far, 1)
+
+    activated, residual = first_conv(
+        me_ref, (mine, near, far, cross), (old, old_near, old_far, old_cross),
+        first_weight, col_count,
+    )
     keep, send = second_conv(
         core.astype(jnp.int32).reshape(1),
         delayed(activated, 2),
@@ -225,25 +319,15 @@
         second_weight,
         col_count,
     )
-    half = keep.shape[0]
-    chip_sum = keep + other(send, 1).astype(F32)
-    residual = lax.dynamic_slice_in_dim(frames[2], core * half, half, axis=0)
-    block_out = chip_sum + other(chip_sum.astype(BF16), 2).astype(F32) + residual.astype(F32)
-    block_out = block_out.astype(BF16)
-    half_rows = half // col_count
-    patches = block_out.reshape(half_rows // 2, 2, col_count // 2, 2, chan_count)
-    patches = patches.transpose(0, 2, 1, 3, 4).reshape(-1, 4 * chan_count)
-    near_patches = other(patches, 1)
-    whole_patches = jnp.concatenate(
-        [
-            jnp.where(core == 0, patches, near_patches),
-            jnp.where(core == 0, near_patches, patches),
-        ],
-        axis=0,
-    )
-    embedded = sum(
-        dot_nt(whole_patches[:, k * quarter : (k + 1) * quarter], embed_all[k]) for k in range(4)
-    ).astype(BF16)
+    summed = chip_sum(keep, other(send, 1))
+    patches = patch_rows(summed, other(summed, 2), residual, col_count)
+    embedded = embed_tokens(
+        me_ref,
+        role.astype(jnp.int32).reshape(1),
+        patches,
+        other(patches, 1),
+        (embed_mine, embed_near, embed_far, embed_cross),
+    )
 
     heads_here = qkv_weight.shape[2] // HEAD_DIM
     token_count = embedded.shape[0]

time: 244 us -> 226 us (0.926)
  blocking collectives: 0 us -> 22.6 us
  starting transfers between devices: 73.7 us -> 53.5 us
  waiting for transfers between devices: 102 us -> 88.1 us
  Pallas kernels: 11.3 us -> 22.4 us
  other arithmetic: 10.9 us -> 1.92 us
  local copies, waits for them, and re-layouts: 27 us -> 19.1 us
    all_to_all x6 -> x2, waiting for transfers between devices: 46.9 us -> 15.4 us  [spread(): lax.all_to_all(copies, axis, 0, 0, axis_index_groups=groups, tiled=True)]
    all_to_all x0 -> x1, blocking collectives: none -> 22.6 us  [spread(): lax.all_to_all(copies, axis, 0, 0, axis_index_groups=groups, tiled=True)]
    all_to_all x6 -> x2, starting transfers between devices: 28.2 us -> 8.9 us  [spread(): lax.all_to_all(copies, axis, 0, 0, axis_index_groups=groups, tiled=True)]
    pallas_call x1 -> x4, Pallas kernels: 4.98 us -> 16.3 us  [the longest x1 6.64 us: embed_tokens(): pl.pallas_call(embed_kernel, out_shape=jax.ShapeDtypeStruct((2 * mine.sha...]
    ppermute x7 -> x12, waiting for transfers between devices: 28.6 us -> 39.5 us  [other(): return lax.ppermute(x, 'narrow', [(i, i ^ mask) for i in range(4)])]
    ppermute x4, starting transfers between devices: 18.9 us -> 11.7 us  [delayed(): return lax.ppermute(x, BOTH, pairs)]
    ppermute x4, waiting for transfers between devices: 5.07 us -> 11.3 us  [delayed(): return lax.ppermute(x, BOTH, pairs)]
    ppermute x7 -> x12, starting transfers between devices: 3.92 us -> 9.94 us  [other(): return lax.ppermute(x, 'narrow', [(i, i ^ mask) for i in range(4)])]
  transfers between devices with their start and end apart: 19 -> 20, of which waited for: 12 -> 11; matrix products, arithmetic and copies ran while one was open for 14% -> 7% of each run, Pallas kernels for 5% -> 7%
where the time goes in v2:
time: 226 us; the launch traced here: 224 us
  waiting for transfers between devices  88.1 us (39%)
  starting transfers between devices  53.5 us (24%)
  blocking collectives  22.6 us (10%)
  Pallas kernels  22.4 us (10%)
  local copies, waits for them, and re-layouts  19.1 us (8%)
  matrix products  16.5 us (7%)
    ppermute x12, waiting for transfers between devices, other(): return lax.ppermute(x, 'narrow', [(i, i ^ mask) for i in range(4)])  39.5 us
    all_to_all x1, blocking collectives, spread(): lax.all_to_all(copies, axis, 0, 0, axis_index_groups=groups, tiled=True)  22.6 us
    all_to_all x1, starting transfers between devices, per_device(): lax.all_to_all(piece_grid.astype(BF16), 'wide', split_axis=0, concat_axis...  17 us
    all_to_all x2, waiting for transfers between devices, spread(): lax.all_to_all(copies, axis, 0, 0, axis_index_groups=groups, tiled=True)  15.4 us
    ppermute x4, starting transfers between devices, delayed(): return lax.ppermute(x, BOTH, pairs)  11.7 us
    all_to_all x1, waiting for transfers between devices, per_device(): lax.all_to_all(partial_sums.astype(BF16), 'wide', split_axis=0, concat_ax...  11.5 us
    ppermute x4, waiting for transfers between devices, delayed(): return lax.ppermute(x, BOTH, pairs)  11.3 us
    all_to_all x1, waiting for transfers between devices, per_device(): lax.all_to_all(piece_grid.astype(BF16), 'wide', split_axis=0, concat_axis...  10.4 us
  transfers between devices with their start and end apart: 20, of which 11 were waited for; matrix products, arithmetic and copies ran while one was open for 7% of the time, Pallas kernels for 7%

profile of v2, /device:TPU:8, one launch (start us, length us, event | category | flops | bytes accessed | tf_op | source)
XLA Modules:
  0.0 224.4 jit_solution(13389509049675097736)
XLA Ops:
  3.2 22.6 %all_to_all.33 = bf16[8,178,128]{2,1,0:T(8,128)(2,1)S(1)} all-to-all(bf16[8,178,128]{2,1,0:T(8,128)(2,1)S(1)} %broadcast_in_dim.18), channel_id=1, replica_groups={{0,8,16,24,32,40,48,56},{4,12,20,28,36,44,52,60},{64,72,80,88,96,104,11..., dimensions={0} | all-to-all | bytes 729088 | tf_op jit(solution)/shard_map/all_to_all | solution.py:45
  27.1 5.3 %all-to-all-start.2 = ((bf16[8,8,70,128]{3,1,2,0:T(8,128)(2,1)}), bf16[8,8,70,128]{3,1,2,0:T(8,128)(2,1)S(1)}, u32[]{:S(2)}, u32[]{:S(2)}) async-start(bf16[8,8,70,128]{3,1,2,0:T(8,128)(2,1)} %broadcast_in_dim.38), calls=%async_computation.2 | async-start | bytes 2293760 | tf_op jit(solution)/shard_map/all_to_all | solution.py:45
  32.5 15.4 %all-to-all-done.2 = bf16[8,8,70,128]{3,1,2,0:T(8,128)(2,1)S(1)} async-done(((bf16[8,8,70,128]{3,1,2,0:T(8,128)(2,1)}), bf16[8,8,70,128]{3,1,2,0:T(8,128)(2,1)S(1)}, u32[]{:S(2)}, u32[]{:S(2)}) %all-to-all-start.2) | async-done | bytes 1146912 | tf_op jit(solution)/shard_map/all_to_all | solution.py:45
  49.4 3.6 %all-to-all-start.1 = ((bf16[8,8,108,128]{3,1,2,0:T(8,128)(2,1)}), bf16[8,8,108,128]{3,1,2,0:T(8,128)(2,1)S(1)}, u32[]{:S(2)}, u32[]{:S(2)}) async-start(bf16[8,8,108,128]{3,1,2,0:T(8,128)(2,1)} %broadcast_in_dim.23), calls=%async_computation.1 | async-start | bytes 3538944 | tf_op jit(solution)/shard_map/all_to_all | solution.py:45
  53.0 2.4 %collective-permute-start.3 = (bf16[384,256]{1,0:T(8,128)(2,1)}, bf16[384,256]{1,0:T(8,128)(2,1)}, u32[]{:S(2)}, u32[]{:S(2)}) collective-permute-start(bf16[384,256]{1,0:T(8,128)(2,1)} %bitcast.3.refs_1_), channel_id=1, source_target_pairs={{0,8},{1,9},{2,10},{3,11},{4,12},{5,13},{6,14},{7,15},{8,16},{9,17... | collective-permute-start | bytes 589832 | tf_op jit(solution)/shard_map/ppermute | solution.py:35
  55.5 4.5 %collective-permute-start.4 = (bf16[384,256]{1,0:T(8,128)(2,1)}, bf16[384,256]{1,0:T(8,128)(2,1)}, u32[]{:S(2)}, u32[]{:S(2)}) collective-permute-start(bf16[384,256]{1,0:T(8,128)(2,1)} %bitcast.3.refs_1_), channel_id=1, source_target_pairs={{0,6},{1,7},{2,4},{3,5},{4,10},{5,11},{6,8},{7,9},{8,14},{9,15},{1... | collective-permute-start | bytes 589832 | tf_op jit(solution)/shard_map/ppermute | solution.py:35
  62.8 3.6 %collective-permute-start.14 = (bf16[2240,256]{1,0:T(8,128)(2,1)}, bf16[2240,256]{1,0:T(8,128)(2,1)S(1)}, u32[]{:S(2)}, u32[]{:S(2)}) collective-permute-start(bf16[2240,256]{1,0:T(8,128)(2,1)} %reshape_reshape.3.w0), channel_id=1, source_target_pairs={{0,2},{1,3},{2,0},{3,1},{4,6},{5,7},{6,4},{7,5},{8,10},{9,11},{10,... | collective-permute-start | bytes 3440648 | tf_op jit(solution)/shard_map/ppermute | solution.py:39
  66.4 5.5 %collective-permute-done.4 = bf16[384,256]{1,0:T(8,128)(2,1)} collective-permute-done((bf16[384,256]{1,0:T(8,128)(2,1)}, bf16[384,256]{1,0:T(8,128)(2,1)}, u32[]{:S(2)}, u32[]{:S(2)}) %collective-permute-start.4) | collective-permute-done | bytes 196640 | tf_op jit(solution)/shard_map/ppermute | solution.py:35
  73.0 2.7 %collective-permute-start.6 = (bf16[2,384,256]{2,1,0:T(8,128)(2,1)S(1)}, bf16[2,384,256]{2,1,0:T(8,128)(2,1)}, u32[]{:S(2)}, u32[]{:S(2)}) collective-permute-start(bf16[2,384,256]{2,1,0:T(8,128)(2,1)S(1)} %pad_maximum_fusion.refs_5_), channel_id=1, source_target_pairs={{0,2},{1,3},{2,0},{3,1},{4,6},{5,7},{6,4},{7,5},{8,10},{9,11},{10,... | collective-permute-start | bytes 1179656 | tf_op jit(solution)/shard_map/ppermute | solution.py:39
  75.8 25.1 %collective-permute-done.6.refs_7_ = bf16[2,384,256]{2,1,0:T(8,128)(2,1)} collective-permute-done((bf16[2,384,256]{2,1,0:T(8,128)(2,1)S(1)}, bf16[2,384,256]{2,1,0:T(8,128)(2,1)}, u32[]{:S(2)}, u32[]{:S(2)}) %collective-permute-start.6) | collective-permute-done | bytes 393248 | tf_op jit(solution)/shard_map/ppermute | solution.py:39
  103.0 1.9 copy.35
  106.1 5.4 %first_conv.1 = (bf16[1536,64]{1,0:T(8,128)(2,1)}, bf16[768,256]{1,0:T(8,128)(2,1)}) custom-call(s32[1]{0:T(128)} %bitcast.refs_0_.me_ref, bf16[384,256]{1,0:T(8,128)(2,1)} %bitcast.3.refs_1_, bf16[384,256]{1,0:T(8,128)(2,1)} %collective-permute-done.refs_2_, bf16[384,256]{1,0:T(8,128)(2,1)} %collective-permute-done.1.refs_3_, ...), custom_call_target="tpu_custom_call" | custom-call | tf_op jit(solution)/shard_map/first_conv/pallas_call | solution.py:111
  111.5 2.1 collective-permute-start.8
  113.5 2.8 %collective-permute-start.9 = (bf16[1536,64]{1,0:T(8,128)(2,1)}, bf16[1536,64]{1,0:T(8,128)(2,1)}, u32[]{:S(2)}, u32[]{:S(2)}) collective-permute-start(bf16[1536,64]{1,0:T(8,128)(2,1)} %get-tuple-element.9.refs_3_), channel_id=1, source_target_pairs={{0,6},{1,7},{2,4},{3,5},{4,10},{5,11},{6,8},{7,9},{8,14},{9,15},{1... | collective-permute-start | bytes 589832 | tf_op jit(solution)/shard_map/ppermute | solution.py:35
  116.9 1.9 reshape.113.refs_4_
  118.8 3.6 %collective-permute-done.8.refs_1_ = bf16[1536,64]{1,0:T(8,128)(2,1)} collective-permute-done((bf16[1536,64]{1,0:T(8,128)(2,1)}, bf16[1536,64]{1,0:T(8,128)(2,1)}, u32[]{:S(2)}, u32[]{:S(2)}) %collective-permute-start.8) | collective-permute-done | bytes 196640 | tf_op jit(solution)/shard_map/ppermute | solution.py:35
  122.4 2.2 collective-permute-done.9.refs_2_
  124.6 6.0 %second_conv.1 = (f32[768,256]{1,0:T(8,128)}, bf16[768,256]{1,0:T(8,128)(2,1)}) custom-call(s32[1]{0:T(128)} %bitcast.2.refs_0_, bf16[1536,64]{1,0:T(8,128)(2,1)} %collective-permute-done.8.refs_1_, bf16[1536,64]{1,0:T(8,128)(2,1)} %collective-permute-done.9.refs_2_, bf16[1536,64]{1,0:T(8,128)(2,1)} %get-tuple-element.9.refs_3_, ...), custom_call_target="tpu_custom_call" | custom-call | tf_op jit(solution)/shard_map/second_conv/pallas_call | solution.py:173
  133.3 2.0 chip_sum.1.refs_0_
  135.4 2.4 %collective-permute-start.11 = (bf16[768,256]{1,0:T(8,128)(2,1)}, bf16[768,256]{1,0:T(8,128)(2,1)S(1)}, u32[]{:S(2)}, u32[]{:S(2)}) collective-permute-start(bf16[768,256]{1,0:T(8,128)(2,1)} %chip_sum.1.refs_0_), channel_id=1, source_target_pairs={{0,2},{1,3},{2,0},{3,1},{4,6},{5,7},{6,4},{7,5},{8,10},{9,11},{10,... | collective-permute-start | bytes 1179656 | tf_op jit(solution)/shard_map/ppermute | solution.py:39
  137.7 9.6 %collective-permute-done.11.refs_1_ = bf16[768,256]{1,0:T(8,128)(2,1)S(1)} collective-permute-done((bf16[768,256]{1,0:T(8,128)(2,1)}, bf16[768,256]{1,0:T(8,128)(2,1)S(1)}, u32[]{:S(2)}, u32[]{:S(2)}) %collective-permute-start.11) | collective-permute-done | bytes 393248 | tf_op jit(solution)/shard_map/ppermute | solution.py:39
  148.1 2.3 %patch_rows.1.mine_ref = bf16[192,1024]{1,0:T(8,128)(2,1)} custom-call(bf16[768,256]{1,0:T(8,128)(2,1)} %chip_sum.1.refs_0_, bf16[768,256]{1,0:T(8,128)(2,1)} %copy-done.7, bf16[768,256]{1,0:T(8,128)(2,1)} %get-tuple-element.12.refs_2_), custom_call_target="tpu_custom_call" | custom-call | tf_op jit(solution)/shard_map/patch_rows/pallas_call | solution.py:226
  150.4 1.9 collective-permute-done.12.near_ref
  153.0 6.6 %embed_tokens.1 = bf16[384,2240]{1,0:T(8,128)(2,1)} custom-call(s32[1]{0:T(128)} %bitcast.refs_0_.me_ref, s32[1]{0:T(128)} %bitcast.1.role_ref, bf16[192,1024]{1,0:T(8,128)(2,1)} %patch_rows.1.mine_ref, bf16[192,1024]{1,0:T(8,128)(2,1)} %copy-done.8, bf16[2240,256]{1,0:T(8,128)(2,1)} %reshape_reshape.3.w0, bf16[2240,256]{1,0:T(8,128)(2,1)} %collective-permute-done.13.w1, ...), custom_call_target="tpu_custom_call" | custom-call | tf_op jit(solution)/shard_map/embed_tokens/pallas_call | solution.py:250
  159.7 4.2 %fusion.62 = (bf16[560]{0:T(1024)(128)(2,1)S(1)}, bf16[384,560]{0,1:T(8,128)(2,1)S(1)}) fusion(bf16[384,2240]{1,0:T(8,128)(2,1)} %embed_tokens.1, bf16[3,2240,560]{1,2,0:T(8,128)(2,1)} %param.9), kind=kOutput, calls=%fused_computation.60 | convolution fusion | flops 965098944 | bytes 4781152 | tf_op jit(solution)/shard_map/dot_general | solution.py:334
  163.9 3.2 %fusion.15 = bf16[384,560]{0,1:T(8,128)(2,1)S(1)} fusion(bf16[384,2240]{1,0:T(8,128)(2,1)S(1)} %copy-done.3, bf16[3,2240,560]{1,2,0:T(8,128)(2,1)} %param.9), kind=kOutput, calls=%fused_computation.21 | convolution fusion | flops 963594240 | bytes 4730880 | tf_op jit(solution)/shard_map/dot_general | solution.py:335
  168.7 17.0 %all-to-all-start.3 = ((bf16[64,1,989]{2,1,0:T(2,128)(2,1)}), bf16[64,1,989]{2,1,0:T(2,128)(2,1)S(1)}, u32[]{:S(2)}, u32[]{:S(2)}) async-start(bf16[64,1,989]{2,1,0:T(2,128)(2,1)} %convert_element_type.72), calls=%async_computation.3 | async-start | bytes 524288 | tf_op jit(solution)/shard_map/all_to_all | solution.py:365
  185.7 3.4 %fusion.39 = bf16[384,560]{0,1:T(8,128)(2,1)S(1)} fusion(bf16[384,2240]{1,0:T(8,128)(2,1)S(1)} %copy-done.3, bf16[3,2240,560]{1,2,0:T(8,128)(2,1)} %param.9), kind=kOutput, calls=%fused_computation.36 | convolution fusion | flops 964884480 | bytes 4730880 | tf_op jit(solution)/shard_map/dot_general | solution.py:337
  189.1 10.4 %all-to-all-done.3 = bf16[64,1,989]{2,1,0:T(2,128)(2,1)S(1)} async-done(((bf16[64,1,989]{2,1,0:T(2,128)(2,1)}), bf16[64,1,989]{2,1,0:T(2,128)(2,1)S(1)}, u32[]{:S(2)}, u32[]{:S(2)}) %all-to-all-start.3) | async-done | bytes 126624 | tf_op jit(solution)/shard_map/all_to_all | solution.py:365
  200.7 6.0 %all-to-all-start.4 = ((bf16[64,1,989]{2,1,0:T(2,128)(2,1)}), bf16[64,1,989]{2,1,0:T(2,128)(2,1)S(1)}, u32[]{:S(2)}, u32[]{:S(2)}) async-start(bf16[64,1,989]{2,1,0:T(2,128)(2,1)} %copy.42), calls=%async_computation.4 | async-start | bytes 524288 | tf_op jit(solution)/shard_map/all_to_all | solution.py:369
  208.5 11.5 %all-to-all-done.4 = bf16[64,1,989]{2,1,0:T(2,128)(2,1)S(1)} async-done(((bf16[64,1,989]{2,1,0:T(2,128)(2,1)}), bf16[64,1,989]{2,1,0:T(2,128)(2,1)S(1)}, u32[]{:S(2)}, u32[]{:S(2)}) %all-to-all-start.4) | async-done | bytes 126624 | tf_op jit(solution)/shard_map/all_to_all | solution.py:369
  221.8 2.6 %fusion.30 = bf16[384,5,112]{0,2,1:T(8,128)(2,1)} fusion(f32[5,112,384]{2,1,0:T(8,128)S(1)} %fusion.63, bf16[384,5,112]{0,2,1:T(8,128)(2,1)S(1)} %bitcast.102, bf16[5,384,384]{1,2,0:T(8,128)(2,1)} %get-tuple-element.18, pred[384,384]{0,1:T(8,128)(4,1)S(1)} %iota_compare_fusion, f32[384,5]{0,1:T(8,128)S(1)} %fusion.59), kind=kOutput, calls=%fused_computation.26 | convolution fusion | flops 166533120 | bytes 3350016 | tf_op jit(solution)/shard_map/hts,she->the/dot_general | solution.py:349
  (78 shorter events, 24.4 us)
Async XLA Ops:
  0.0 0.9 copy-start
  27.1 20.8 %all-to-all-start.2 = ((bf16[8,8,70,128]{3,1,2,0:T(8,128)(2,1)}), bf16[8,8,70,128]{3,1,2,0:T(8,128)(2,1)S(1)}, u32[]{:S(2)}, u32[]{:S(2)}) async-start(bf16[8,8,70,128]{3,1,2,0:T(8,128)(2,1)} %broadcast_in_dim.38), calls=%async_computation.2 | async-start | bytes 2293760 | tf_op jit(solution)/shard_map/all_to_all | solution.py:45
  47.8 1.6 copy-start.1
  49.4 53.6 %all-to-all-start.1 = ((bf16[8,8,108,128]{3,1,2,0:T(8,128)(2,1)}), bf16[8,8,108,128]{3,1,2,0:T(8,128)(2,1)S(1)}, u32[]{:S(2)}, u32[]{:S(2)}) async-start(bf16[8,8,108,128]{3,1,2,0:T(8,128)(2,1)} %broadcast_in_dim.23), calls=%async_computation.1 | async-start | bytes 3538944 | tf_op jit(solution)/shard_map/all_to_all | solution.py:45
  53.0 13.4 %collective-permute-start.3 = (bf16[384,256]{1,0:T(8,128)(2,1)}, bf16[384,256]{1,0:T(8,128)(2,1)}, u32[]{:S(2)}, u32[]{:S(2)}) collective-permute-start(bf16[384,256]{1,0:T(8,128)(2,1)} %bitcast.3.refs_1_), channel_id=1, source_target_pairs={{0,8},{1,9},{2,10},{3,11},{4,12},{5,13},{6,14},{7,15},{8,16},{9,17... | collective-permute-start | bytes 589832 | tf_op jit(solution)/shard_map/ppermute | solution.py:35
  55.5 16.4 %collective-permute-start.4 = (bf16[384,256]{1,0:T(8,128)(2,1)}, bf16[384,256]{1,0:T(8,128)(2,1)}, u32[]{:S(2)}, u32[]{:S(2)}) collective-permute-start(bf16[384,256]{1,0:T(8,128)(2,1)} %bitcast.3.refs_1_), channel_id=1, source_target_pairs={{0,6},{1,7},{2,4},{3,5},{4,10},{5,11},{6,8},{7,9},{8,14},{9,15},{1... | collective-permute-start | bytes 589832 | tf_op jit(solution)/shard_map/ppermute | solution.py:35
  62.8 68.4 %collective-permute-start.14 = (bf16[2240,256]{1,0:T(8,128)(2,1)}, bf16[2240,256]{1,0:T(8,128)(2,1)S(1)}, u32[]{:S(2)}, u32[]{:S(2)}) collective-permute-start(bf16[2240,256]{1,0:T(8,128)(2,1)} %reshape_reshape.3.w0), channel_id=1, source_target_pairs={{0,2},{1,3},{2,0},{3,1},{4,6},{5,7},{6,4},{7,5},{8,10},{9,11},{10,... | collective-permute-start | bytes 3440648 | tf_op jit(solution)/shard_map/ppermute | solution.py:39
  73.0 31.9 %copy-start.4 = (bf16[2,384,256]{2,1,0:T(8,128)(2,1)}, bf16[2,384,256]{2,1,0:T(8,128)(2,1)S(1)}, u32[]{:S(2)}) copy-start(bf16[2,384,256]{2,1,0:T(8,128)(2,1)S(1)} %pad_maximum_fusion.refs_5_) | copy-start | bytes 1179652
  73.0 27.9 %collective-permute-start.6 = (bf16[2,384,256]{2,1,0:T(8,128)(2,1)S(1)}, bf16[2,384,256]{2,1,0:T(8,128)(2,1)}, u32[]{:S(2)}, u32[]{:S(2)}) collective-permute-start(bf16[2,384,256]{2,1,0:T(8,128)(2,1)S(1)} %pad_maximum_fusion.refs_5_), channel_id=1, source_target_pairs={{0,2},{1,3},{2,0},{3,1},{4,6},{5,7},{6,4},{7,5},{8,10},{9,11},{10,... | collective-permute-start | bytes 1179656 | tf_op jit(solution)/shard_map/ppermute | solution.py:39
  75.7 27.3 %collective-permute-start.1 = (bf16[384,256]{1,0:T(8,128)(2,1)}, bf16[384,256]{1,0:T(8,128)(2,1)}, u32[]{:S(2)}, u32[]{:S(2)}) collective-permute-start(bf16[384,256]{1,0:T(8,128)(2,1)} %bitcast.3.refs_1_), channel_id=1, source_target_pairs={{0,2},{1,3},{2,0},{3,1},{4,6},{5,7},{6,4},{7,5},{8,10},{9,11},{10,... | collective-permute-start | bytes 589832 | tf_op jit(solution)/shard_map/ppermute | solution.py:39
  75.8 30.3 %collective-permute-start.5 = (bf16[2,384,256]{2,1,0:T(8,128)(2,1)S(1)}, bf16[2,384,256]{2,1,0:T(8,128)(2,1)}, u32[]{:S(2)}, u32[]{:S(2)}) collective-permute-start(bf16[2,384,256]{2,1,0:T(8,128)(2,1)S(1)} %pad_maximum_fusion.refs_5_), channel_id=1, source_target_pairs={{0,1},{1,0},{2,3},{3,2},{4,5},{5,4},{6,7},{7,6},{8,9},{9,8},{10,11... | collective-permute-start | bytes 1179656 | tf_op jit(solution)/shard_map/ppermute | solution.py:39
  100.9 5.2 %collective-permute-start.7 = (bf16[2,384,256]{2,1,0:T(8,128)(2,1)}, bf16[2,384,256]{2,1,0:T(8,128)(2,1)}, u32[]{:S(2)}, u32[]{:S(2)}) collective-permute-start(bf16[2,384,256]{2,1,0:T(8,128)(2,1)} %collective-permute-done.6.refs_7_), channel_id=1, source_target_pairs={{0,1},{1,0},{2,3},{3,2},{4,5},{5,4},{6,7},{7,6},{8,9},{9,8},{10,11... | collective-permute-start | bytes 1179656 | tf_op jit(solution)/shard_map/ppermute | solution.py:39
  100.9 5.2 %collective-permute-start = (bf16[384,256]{1,0:T(8,128)(2,1)}, bf16[384,256]{1,0:T(8,128)(2,1)}, u32[]{:S(2)}, u32[]{:S(2)}) collective-permute-start(bf16[384,256]{1,0:T(8,128)(2,1)} %bitcast.3.refs_1_), channel_id=1, source_target_pairs={{0,1},{1,0},{2,3},{3,2},{4,5},{5,4},{6,7},{7,6},{8,9},{9,8},{10,11... | collective-permute-start | bytes 589832 | tf_op jit(solution)/shard_map/ppermute | solution.py:39
  103.0 3.1 %collective-permute-start.2 = (bf16[384,256]{1,0:T(8,128)(2,1)}, bf16[384,256]{1,0:T(8,128)(2,1)}, u32[]{:S(2)}, u32[]{:S(2)}) collective-permute-start(bf16[384,256]{1,0:T(8,128)(2,1)} %collective-permute-done.1.refs_3_), channel_id=1, source_target_pairs={{0,1},{1,0},{2,3},{3,2},{4,5},{5,4},{6,7},{7,6},{8,9},{9,8},{10,11... | collective-permute-start | bytes 589832 | tf_op jit(solution)/shard_map/ppermute | solution.py:39
  111.5 10.9 %collective-permute-start.8 = (bf16[1536,64]{1,0:T(8,128)(2,1)}, bf16[1536,64]{1,0:T(8,128)(2,1)}, u32[]{:S(2)}, u32[]{:S(2)}) collective-permute-start(bf16[1536,64]{1,0:T(8,128)(2,1)} %get-tuple-element.9.refs_3_), channel_id=1, source_target_pairs={{0,8},{1,9},{2,10},{3,11},{4,12},{5,13},{6,14},{7,15},{8,16},{9,17... | collective-permute-start | bytes 589832 | tf_op jit(solution)/shard_map/ppermute | solution.py:35
  113.5 11.1 %collective-permute-start.9 = (bf16[1536,64]{1,0:T(8,128)(2,1)}, bf16[1536,64]{1,0:T(8,128)(2,1)}, u32[]{:S(2)}, u32[]{:S(2)}) collective-permute-start(bf16[1536,64]{1,0:T(8,128)(2,1)} %get-tuple-element.9.refs_3_), channel_id=1, source_target_pairs={{0,6},{1,7},{2,4},{3,5},{4,10},{5,11},{6,8},{7,9},{8,14},{9,15},{1... | collective-permute-start | bytes 589832 | tf_op jit(solution)/shard_map/ppermute | solution.py:35
  116.9 13.8 %copy-start.2 = (bf16[2240,256]{1,0:T(8,128)(2,1)S(1)}, bf16[2240,256]{1,0:T(8,128)(2,1)}, u32[]{:S(2)}) copy-start(bf16[2240,256]{1,0:T(8,128)(2,1)} %reshape_reshape.3.w0) | copy-start | bytes 3440644
  130.6 1.9 collective-permute-start.10
  130.6 19.8 %collective-permute-start.13 = (bf16[2240,256]{1,0:T(8,128)(2,1)S(1)}, bf16[2240,256]{1,0:T(8,128)(2,1)}, u32[]{:S(2)}, u32[]{:S(2)}) collective-permute-start(bf16[2240,256]{1,0:T(8,128)(2,1)S(1)} %copy-done.2), channel_id=1, source_target_pairs={{0,1},{1,0},{2,3},{3,2},{4,5},{5,4},{6,7},{7,6},{8,9},{9,8},{10,11... | collective-permute-start | bytes 3440648 | tf_op jit(solution)/shard_map/ppermute | solution.py:39
  131.2 21.2 %copy-start.5 = (bf16[2240,256]{1,0:T(8,128)(2,1)}, bf16[2240,256]{1,0:T(8,128)(2,1)S(1)}, u32[]{:S(2)}) copy-start(bf16[2240,256]{1,0:T(8,128)(2,1)S(1)} %collective-permute-done.14.w2) | copy-start | bytes 3440644
  131.2 21.1 %collective-permute-start.15 = (bf16[2240,256]{1,0:T(8,128)(2,1)S(1)}, bf16[2240,256]{1,0:T(8,128)(2,1)}, u32[]{:S(2)}, u32[]{:S(2)}) collective-permute-start(bf16[2240,256]{1,0:T(8,128)(2,1)S(1)} %collective-permute-done.14.w2), channel_id=1, source_target_pairs={{0,1},{1,0},{2,3},{3,2},{4,5},{5,4},{6,7},{7,6},{8,9},{9,8},{10,11... | collective-permute-start | bytes 3440648 | tf_op jit(solution)/shard_map/ppermute | solution.py:39
  132.6 0.7 copy-start.6
  135.4 12.0 %collective-permute-start.11 = (bf16[768,256]{1,0:T(8,128)(2,1)}, bf16[768,256]{1,0:T(8,128)(2,1)S(1)}, u32[]{:S(2)}, u32[]{:S(2)}) collective-permute-start(bf16[768,256]{1,0:T(8,128)(2,1)} %chip_sum.1.refs_0_), channel_id=1, source_target_pairs={{0,2},{1,3},{2,0},{3,1},{4,6},{5,7},{6,4},{7,5},{8,10},{9,11},{10,... | collective-permute-start | bytes 1179656 | tf_op jit(solution)/shard_map/ppermute | solution.py:39
  147.3 0.7 copy-start.7
  150.4 1.9 collective-permute-start.12
  152.3 0.7 copy-start.8
  159.7 4.2 %copy-start.3 = (bf16[384,2240]{1,0:T(8,128)(2,1)S(1)}, bf16[384,2240]{1,0:T(8,128)(2,1)}, u32[]{:S(2)}) copy-start(bf16[384,2240]{1,0:T(8,128)(2,1)} %embed_tokens.1) | copy-start | bytes 5160964
  168.7 30.8 %all-to-all-start.3 = ((bf16[64,1,989]{2,1,0:T(2,128)(2,1)}), bf16[64,1,989]{2,1,0:T(2,128)(2,1)S(1)}, u32[]{:S(2)}, u32[]{:S(2)}) async-start(bf16[64,1,989]{2,1,0:T(2,128)(2,1)} %convert_element_type.72), calls=%async_computation.3 | async-start | bytes 524288 | tf_op jit(solution)/shard_map/all_to_all | solution.py:365
  200.7 19.3 %all-to-all-start.4 = ((bf16[64,1,989]{2,1,0:T(2,128)(2,1)}), bf16[64,1,989]{2,1,0:T(2,128)(2,1)S(1)}, u32[]{:S(2)}, u32[]{:S(2)}) async-start(bf16[64,1,989]{2,1,0:T(2,128)(2,1)} %copy.42), calls=%async_computation.4 | async-start | bytes 524288 | tf_op jit(solution)/shard_map/all_to_all | solution.py:369

commit v3 on v2

--- a/solution.py
+++ b/solution.py
@@ -143,8 +143,8 @@
         ]
     prod_ref[0:8, :] = jnp.zeros((8, 3 * width), F32)
     prod_ref[8 + tokens :, :] = jnp.zeros((8, 3 * width), F32)
-    chunk = tokens // 8
-    for part in range(8):
+    chunk = tokens // 4
+    for part in range(4):
         total = jnp.zeros((chunk, 3 * width), F32)
         for tap in range(3):
             start = part * chunk + tap * cols
@@ -233,25 +233,30 @@
     )(mine, far, res)
 
 
-def embed_kernel(me_ref, role_ref, mine_ref, near_ref, w0, w1, w2, w3, o_ref):
+def embed_kernel(me_ref, role_ref, mine_ref, near_ref, w0, w1, w2, w3, o_ref, all_ref):
     half = mine_ref.shape[0]
-    depth = w0.shape[1]
+    width, depth = w0.shape
     core = me_ref[0] & 1
     for side, ref in ((core, mine_ref), (1 - core, near_ref)):
+        all_ref[pl.ds(pl.multiple_of(side * half, 16), half), :] = ref[...]
+    for start in range(0, width, 256):
+        end = min(start + 256, width)
         total = None
         for k, w_ref in enumerate((w0, w1, w2, w3)):
             lanes = pl.ds(pl.multiple_of((role_ref[0] ^ k) * depth, depth), depth)
-            part = dot_nt(ref[:, lanes], w_ref[...])
+            part = dot_nt(all_ref[:, lanes], w_ref[start:end, :])
             total = part if total is None else total + part
-        o_ref[pl.ds(pl.multiple_of(side * half, 16), half), :] = total.astype(BF16)
+        o_ref[:, start:end] = total.astype(BF16)
 
 
 def embed_tokens(me, role, mine, near, weights):
+    tokens = 2 * mine.shape[0]
     return pl.pallas_call(
         embed_kernel,
-        out_shape=jax.ShapeDtypeStruct((2 * mine.shape[0], weights[0].shape[0]), BF16),
+        out_shape=jax.ShapeDtypeStruct((tokens, weights[0].shape[0]), BF16),
         in_specs=[SMEM_SPEC] * 2 + [VMEM_SPEC] * 6,
         out_specs=VMEM_SPEC,
+        scratch_shapes=[pltpu.VMEM((tokens, mine.shape[1]), BF16)],
         name="embed_tokens",
     )(me, role, mine, near, *weights)
 

time: 226 us -> 224 us (level)
  no operation moved by 1% of the time
where the time goes in v3:
time: 224 us; the launch traced here: 223 us
  waiting for transfers between devices  88.1 us (39%)
  starting transfers between devices  53.3 us (24%)
  blocking collectives  22.6 us (10%)
  Pallas kernels  20.7 us (9%)
  local copies, waits for them, and re-layouts  19.1 us (9%)
  matrix products  16.5 us (7%)
    ppermute x12, waiting for transfers between devices, other(): return lax.ppermute(x, 'narrow', [(i, i ^ mask) for i in range(4)])  39.5 us
    all_to_all x1, blocking collectives, spread(): lax.all_to_all(copies, axis, 0, 0, axis_index_groups=groups, tiled=True)  22.6 us
    all_to_all x1, starting transfers between devices, per_device(): lax.all_to_all(piece_grid.astype(BF16), 'wide', split_axis=0, concat_axis...  16.7 us
    all_to_all x2, waiting for transfers between devices, spread(): lax.all_to_all(copies, axis, 0, 0, axis_index_groups=groups, tiled=True)  15.4 us
    ppermute x4, starting transfers between devices, delayed(): return lax.ppermute(x, BOTH, pairs)  11.7 us
    all_to_all x1, waiting for transfers between devices, per_device(): lax.all_to_all(partial_sums.astype(BF16), 'wide', split_axis=0, concat_ax...  11.5 us
    ppermute x4, waiting for transfers between devices, delayed(): return lax.ppermute(x, BOTH, pairs)  11.3 us
    all_to_all x1, waiting for transfers between devices, per_device(): lax.all_to_all(piece_grid.astype(BF16), 'wide', split_axis=0, concat_axis...  10.5 us
  transfers between devices with their start and end apart: 20, of which 11 were waited for; matrix products, arithmetic and copies ran while one was open for 7% of the time, Pallas kernels for 7%

profile of v3, /device:TPU:8, one launch (start us, length us, event | category | flops | bytes accessed | tf_op | source)
XLA Modules:
  0.0 222.5 jit_solution(306524153022895236)
XLA Ops:
  3.2 22.6 %all_to_all.33 = bf16[8,178,128]{2,1,0:T(8,128)(2,1)S(1)} all-to-all(bf16[8,178,128]{2,1,0:T(8,128)(2,1)S(1)} %broadcast_in_dim.18), channel_id=1, replica_groups={{0,8,16,24,32,40,48,56},{4,12,20,28,36,44,52,60},{64,72,80,88,96,104,11..., dimensions={0} | all-to-all | bytes 729088 | tf_op jit(solution)/shard_map/all_to_all | solution.py:45
  27.1 5.3 %all-to-all-start.2 = ((bf16[8,8,70,128]{3,1,2,0:T(8,128)(2,1)}), bf16[8,8,70,128]{3,1,2,0:T(8,128)(2,1)S(1)}, u32[]{:S(2)}, u32[]{:S(2)}) async-start(bf16[8,8,70,128]{3,1,2,0:T(8,128)(2,1)} %broadcast_in_dim.38), calls=%async_computation.2 | async-start | bytes 2293760 | tf_op jit(solution)/shard_map/all_to_all | solution.py:45
  32.5 15.4 %all-to-all-done.2 = bf16[8,8,70,128]{3,1,2,0:T(8,128)(2,1)S(1)} async-done(((bf16[8,8,70,128]{3,1,2,0:T(8,128)(2,1)}), bf16[8,8,70,128]{3,1,2,0:T(8,128)(2,1)S(1)}, u32[]{:S(2)}, u32[]{:S(2)}) %all-to-all-start.2) | async-done | bytes 1146912 | tf_op jit(solution)/shard_map/all_to_all | solution.py:45
  49.4 3.6 %all-to-all-start.1 = ((bf16[8,8,108,128]{3,1,2,0:T(8,128)(2,1)}), bf16[8,8,108,128]{3,1,2,0:T(8,128)(2,1)S(1)}, u32[]{:S(2)}, u32[]{:S(2)}) async-start(bf16[8,8,108,128]{3,1,2,0:T(8,128)(2,1)} %broadcast_in_dim.23), calls=%async_computation.1 | async-start | bytes 3538944 | tf_op jit(solution)/shard_map/all_to_all | solution.py:45
  53.0 2.4 %collective-permute-start.3 = (bf16[384,256]{1,0:T(8,128)(2,1)}, bf16[384,256]{1,0:T(8,128)(2,1)}, u32[]{:S(2)}, u32[]{:S(2)}) collective-permute-start(bf16[384,256]{1,0:T(8,128)(2,1)} %bitcast.3.refs_1_), channel_id=1, source_target_pairs={{0,8},{1,9},{2,10},{3,11},{4,12},{5,13},{6,14},{7,15},{8,16},{9,17... | collective-permute-start | bytes 589832 | tf_op jit(solution)/shard_map/ppermute | solution.py:35
  55.5 4.5 %collective-permute-start.4 = (bf16[384,256]{1,0:T(8,128)(2,1)}, bf16[384,256]{1,0:T(8,128)(2,1)}, u32[]{:S(2)}, u32[]{:S(2)}) collective-permute-start(bf16[384,256]{1,0:T(8,128)(2,1)} %bitcast.3.refs_1_), channel_id=1, source_target_pairs={{0,6},{1,7},{2,4},{3,5},{4,10},{5,11},{6,8},{7,9},{8,14},{9,15},{1... | collective-permute-start | bytes 589832 | tf_op jit(solution)/shard_map/ppermute | solution.py:35
  62.8 3.6 %collective-permute-start.14 = (bf16[2240,256]{1,0:T(8,128)(2,1)}, bf16[2240,256]{1,0:T(8,128)(2,1)S(1)}, u32[]{:S(2)}, u32[]{:S(2)}) collective-permute-start(bf16[2240,256]{1,0:T(8,128)(2,1)} %reshape_reshape.3.w0), channel_id=1, source_target_pairs={{0,2},{1,3},{2,0},{3,1},{4,6},{5,7},{6,4},{7,5},{8,10},{9,11},{10,... | collective-permute-start | bytes 3440648 | tf_op jit(solution)/shard_map/ppermute | solution.py:39
  66.4 5.5 %collective-permute-done.4 = bf16[384,256]{1,0:T(8,128)(2,1)} collective-permute-done((bf16[384,256]{1,0:T(8,128)(2,1)}, bf16[384,256]{1,0:T(8,128)(2,1)}, u32[]{:S(2)}, u32[]{:S(2)}) %collective-permute-start.4) | collective-permute-done | bytes 196640 | tf_op jit(solution)/shard_map/ppermute | solution.py:35
  73.0 2.7 %collective-permute-start.6 = (bf16[2,384,256]{2,1,0:T(8,128)(2,1)S(1)}, bf16[2,384,256]{2,1,0:T(8,128)(2,1)}, u32[]{:S(2)}, u32[]{:S(2)}) collective-permute-start(bf16[2,384,256]{2,1,0:T(8,128)(2,1)S(1)} %pad_maximum_fusion.refs_5_), channel_id=1, source_target_pairs={{0,2},{1,3},{2,0},{3,1},{4,6},{5,7},{6,4},{7,5},{8,10},{9,11},{10,... | collective-permute-start | bytes 1179656 | tf_op jit(solution)/shard_map/ppermute | solution.py:39
  75.8 25.1 %collective-permute-done.6.refs_7_ = bf16[2,384,256]{2,1,0:T(8,128)(2,1)} collective-permute-done((bf16[2,384,256]{2,1,0:T(8,128)(2,1)S(1)}, bf16[2,384,256]{2,1,0:T(8,128)(2,1)}, u32[]{:S(2)}, u32[]{:S(2)}) %collective-permute-start.6) | collective-permute-done | bytes 393248 | tf_op jit(solution)/shard_map/ppermute | solution.py:39
  103.0 1.9 copy.35
  106.1 5.4 %first_conv.1 = (bf16[1536,64]{1,0:T(8,128)(2,1)}, bf16[768,256]{1,0:T(8,128)(2,1)}) custom-call(s32[1]{0:T(128)} %bitcast.refs_0_.me_ref, bf16[384,256]{1,0:T(8,128)(2,1)} %bitcast.3.refs_1_, bf16[384,256]{1,0:T(8,128)(2,1)} %collective-permute-done.refs_2_, bf16[384,256]{1,0:T(8,128)(2,1)} %collective-permute-done.1.refs_3_, ...), custom_call_target="tpu_custom_call" | custom-call | tf_op jit(solution)/shard_map/first_conv/pallas_call | solution.py:111
  111.5 2.1 collective-permute-start.8
  113.5 2.8 %collective-permute-start.9 = (bf16[1536,64]{1,0:T(8,128)(2,1)}, bf16[1536,64]{1,0:T(8,128)(2,1)}, u32[]{:S(2)}, u32[]{:S(2)}) collective-permute-start(bf16[1536,64]{1,0:T(8,128)(2,1)} %get-tuple-element.9.refs_3_), channel_id=1, source_target_pairs={{0,6},{1,7},{2,4},{3,5},{4,10},{5,11},{6,8},{7,9},{8,14},{9,15},{1... | collective-permute-start | bytes 589832 | tf_op jit(solution)/shard_map/ppermute | solution.py:35
  116.9 1.9 reshape.113.refs_4_
  118.8 3.6 %collective-permute-done.8.refs_1_ = bf16[1536,64]{1,0:T(8,128)(2,1)} collective-permute-done((bf16[1536,64]{1,0:T(8,128)(2,1)}, bf16[1536,64]{1,0:T(8,128)(2,1)}, u32[]{:S(2)}, u32[]{:S(2)}) %collective-permute-start.8) | collective-permute-done | bytes 196640 | tf_op jit(solution)/shard_map/ppermute | solution.py:35
  122.4 2.2 collective-permute-done.9.refs_2_
  124.6 5.1 %second_conv.1 = (f32[768,256]{1,0:T(8,128)}, bf16[768,256]{1,0:T(8,128)(2,1)}) custom-call(s32[1]{0:T(128)} %bitcast.2.refs_0_, bf16[1536,64]{1,0:T(8,128)(2,1)} %collective-permute-done.8.refs_1_, bf16[1536,64]{1,0:T(8,128)(2,1)} %collective-permute-done.9.refs_2_, bf16[1536,64]{1,0:T(8,128)(2,1)} %get-tuple-element.9.refs_3_, ...), custom_call_target="tpu_custom_call" | custom-call | tf_op jit(solution)/shard_map/second_conv/pallas_call | solution.py:173
  132.4 2.0 chip_sum.1.refs_0_
  134.4 2.3 %collective-permute-start.11 = (bf16[768,256]{1,0:T(8,128)(2,1)}, bf16[768,256]{1,0:T(8,128)(2,1)S(1)}, u32[]{:S(2)}, u32[]{:S(2)}) collective-permute-start(bf16[768,256]{1,0:T(8,128)(2,1)} %chip_sum.1.refs_0_), channel_id=1, source_target_pairs={{0,2},{1,3},{2,0},{3,1},{4,6},{5,7},{6,4},{7,5},{8,10},{9,11},{10,... | collective-permute-start | bytes 1179656 | tf_op jit(solution)/shard_map/ppermute | solution.py:39
  136.8 9.6 %collective-permute-done.11.refs_1_ = bf16[768,256]{1,0:T(8,128)(2,1)S(1)} collective-permute-done((bf16[768,256]{1,0:T(8,128)(2,1)}, bf16[768,256]{1,0:T(8,128)(2,1)S(1)}, u32[]{:S(2)}, u32[]{:S(2)}) %collective-permute-start.11) | collective-permute-done | bytes 393248 | tf_op jit(solution)/shard_map/ppermute | solution.py:39
  147.1 2.3 %patch_rows.1.mine_ref = bf16[192,1024]{1,0:T(8,128)(2,1)} custom-call(bf16[768,256]{1,0:T(8,128)(2,1)} %chip_sum.1.refs_0_, bf16[768,256]{1,0:T(8,128)(2,1)} %copy-done.7, bf16[768,256]{1,0:T(8,128)(2,1)} %get-tuple-element.12.refs_2_), custom_call_target="tpu_custom_call" | custom-call | tf_op jit(solution)/shard_map/patch_rows/pallas_call | solution.py:226
  149.5 1.9 collective-permute-done.12.near_ref
  152.1 5.9 %embed_tokens.1 = bf16[384,2240]{1,0:T(8,128)(2,1)} custom-call(s32[1]{0:T(128)} %bitcast.refs_0_.me_ref, s32[1]{0:T(128)} %bitcast.1.role_ref, bf16[192,1024]{1,0:T(8,128)(2,1)} %patch_rows.1.mine_ref, bf16[192,1024]{1,0:T(8,128)(2,1)} %copy-done.8, bf16[2240,256]{1,0:T(8,128)(2,1)} %reshape_reshape.3.w0, bf16[2240,256]{1,0:T(8,128)(2,1)} %collective-permute-done.13.w1, ...), custom_call_target="tpu_custom_call" | custom-call | tf_op jit(solution)/shard_map/embed_tokens/pallas_call | solution.py:254
  158.0 4.2 %fusion.62 = (bf16[560]{0:T(1024)(128)(2,1)S(1)}, bf16[384,560]{0,1:T(8,128)(2,1)S(1)}) fusion(bf16[384,2240]{1,0:T(8,128)(2,1)} %embed_tokens.1, bf16[3,2240,560]{1,2,0:T(8,128)(2,1)} %param.9), kind=kOutput, calls=%fused_computation.60 | convolution fusion | flops 965098944 | bytes 4781152 | tf_op jit(solution)/shard_map/dot_general | solution.py:339
  162.2 3.2 %fusion.15 = bf16[384,560]{0,1:T(8,128)(2,1)S(1)} fusion(bf16[384,2240]{1,0:T(8,128)(2,1)S(1)} %copy-done.3, bf16[3,2240,560]{1,2,0:T(8,128)(2,1)} %param.9), kind=kOutput, calls=%fused_computation.21 | convolution fusion | flops 963594240 | bytes 4730880 | tf_op jit(solution)/shard_map/dot_general | solution.py:340
  167.0 16.7 %all-to-all-start.3 = ((bf16[64,1,989]{2,1,0:T(2,128)(2,1)}), bf16[64,1,989]{2,1,0:T(2,128)(2,1)S(1)}, u32[]{:S(2)}, u32[]{:S(2)}) async-start(bf16[64,1,989]{2,1,0:T(2,128)(2,1)} %convert_element_type.72), calls=%async_computation.3 | async-start | bytes 524288 | tf_op jit(solution)/shard_map/all_to_all | solution.py:370
  183.8 3.4 %fusion.39 = bf16[384,560]{0,1:T(8,128)(2,1)S(1)} fusion(bf16[384,2240]{1,0:T(8,128)(2,1)S(1)} %copy-done.3, bf16[3,2240,560]{1,2,0:T(8,128)(2,1)} %param.9), kind=kOutput, calls=%fused_computation.36 | convolution fusion | flops 964884480 | bytes 4730880 | tf_op jit(solution)/shard_map/dot_general | solution.py:342
  187.2 10.5 %all-to-all-done.3 = bf16[64,1,989]{2,1,0:T(2,128)(2,1)S(1)} async-done(((bf16[64,1,989]{2,1,0:T(2,128)(2,1)}), bf16[64,1,989]{2,1,0:T(2,128)(2,1)S(1)}, u32[]{:S(2)}, u32[]{:S(2)}) %all-to-all-start.3) | async-done | bytes 126624 | tf_op jit(solution)/shard_map/all_to_all | solution.py:370
  198.7 6.0 %all-to-all-start.4 = ((bf16[64,1,989]{2,1,0:T(2,128)(2,1)}), bf16[64,1,989]{2,1,0:T(2,128)(2,1)S(1)}, u32[]{:S(2)}, u32[]{:S(2)}) async-start(bf16[64,1,989]{2,1,0:T(2,128)(2,1)} %copy.42), calls=%async_computation.4 | async-start | bytes 524288 | tf_op jit(solution)/shard_map/all_to_all | solution.py:374
  206.6 11.5 %all-to-all-done.4 = bf16[64,1,989]{2,1,0:T(2,128)(2,1)S(1)} async-done(((bf16[64,1,989]{2,1,0:T(2,128)(2,1)}), bf16[64,1,989]{2,1,0:T(2,128)(2,1)S(1)}, u32[]{:S(2)}, u32[]{:S(2)}) %all-to-all-start.4) | async-done | bytes 126624 | tf_op jit(solution)/shard_map/all_to_all | solution.py:374
  219.9 2.6 %fusion.30 = bf16[384,5,112]{0,2,1:T(8,128)(2,1)} fusion(f32[5,112,384]{2,1,0:T(8,128)S(1)} %fusion.63, bf16[384,5,112]{0,2,1:T(8,128)(2,1)S(1)} %bitcast.102, bf16[5,384,384]{1,2,0:T(8,128)(2,1)} %get-tuple-element.18, pred[384,384]{0,1:T(8,128)(4,1)S(1)} %iota_compare_fusion, f32[384,5]{0,1:T(8,128)S(1)} %fusion.59), kind=kOutput, calls=%fused_computation.26 | convolution fusion | flops 166533120 | bytes 3350016 | tf_op jit(solution)/shard_map/hts,she->the/dot_general | solution.py:354
  (78 shorter events, 24.4 us)
Async XLA Ops:
  0.0 0.9 copy-start
  27.1 20.8 %all-to-all-start.2 = ((bf16[8,8,70,128]{3,1,2,0:T(8,128)(2,1)}), bf16[8,8,70,128]{3,1,2,0:T(8,128)(2,1)S(1)}, u32[]{:S(2)}, u32[]{:S(2)}) async-start(bf16[8,8,70,128]{3,1,2,0:T(8,128)(2,1)} %broadcast_in_dim.38), calls=%async_computation.2 | async-start | bytes 2293760 | tf_op jit(solution)/shard_map/all_to_all | solution.py:45
  47.8 1.6 copy-start.1
  49.4 53.6 %all-to-all-start.1 = ((bf16[8,8,108,128]{3,1,2,0:T(8,128)(2,1)}), bf16[8,8,108,128]{3,1,2,0:T(8,128)(2,1)S(1)}, u32[]{:S(2)}, u32[]{:S(2)}) async-start(bf16[8,8,108,128]{3,1,2,0:T(8,128)(2,1)} %broadcast_in_dim.23), calls=%async_computation.1 | async-start | bytes 3538944 | tf_op jit(solution)/shard_map/all_to_all | solution.py:45
  53.0 13.4 %collective-permute-start.3 = (bf16[384,256]{1,0:T(8,128)(2,1)}, bf16[384,256]{1,0:T(8,128)(2,1)}, u32[]{:S(2)}, u32[]{:S(2)}) collective-permute-start(bf16[384,256]{1,0:T(8,128)(2,1)} %bitcast.3.refs_1_), channel_id=1, source_target_pairs={{0,8},{1,9},{2,10},{3,11},{4,12},{5,13},{6,14},{7,15},{8,16},{9,17... | collective-permute-start | bytes 589832 | tf_op jit(solution)/shard_map/ppermute | solution.py:35
  55.5 16.4 %collective-permute-start.4 = (bf16[384,256]{1,0:T(8,128)(2,1)}, bf16[384,256]{1,0:T(8,128)(2,1)}, u32[]{:S(2)}, u32[]{:S(2)}) collective-permute-start(bf16[384,256]{1,0:T(8,128)(2,1)} %bitcast.3.refs_1_), channel_id=1, source_target_pairs={{0,6},{1,7},{2,4},{3,5},{4,10},{5,11},{6,8},{7,9},{8,14},{9,15},{1... | collective-permute-start | bytes 589832 | tf_op jit(solution)/shard_map/ppermute | solution.py:35
  62.8 67.4 %collective-permute-start.14 = (bf16[2240,256]{1,0:T(8,128)(2,1)}, bf16[2240,256]{1,0:T(8,128)(2,1)S(1)}, u32[]{:S(2)}, u32[]{:S(2)}) collective-permute-start(bf16[2240,256]{1,0:T(8,128)(2,1)} %reshape_reshape.3.w0), channel_id=1, source_target_pairs={{0,2},{1,3},{2,0},{3,1},{4,6},{5,7},{6,4},{7,5},{8,10},{9,11},{10,... | collective-permute-start | bytes 3440648 | tf_op jit(solution)/shard_map/ppermute | solution.py:39
  73.0 31.9 %copy-start.4 = (bf16[2,384,256]{2,1,0:T(8,128)(2,1)}, bf16[2,384,256]{2,1,0:T(8,128)(2,1)S(1)}, u32[]{:S(2)}) copy-start(bf16[2,384,256]{2,1,0:T(8,128)(2,1)S(1)} %pad_maximum_fusion.refs_5_) | copy-start | bytes 1179652
  73.0 27.9 %collective-permute-start.6 = (bf16[2,384,256]{2,1,0:T(8,128)(2,1)S(1)}, bf16[2,384,256]{2,1,0:T(8,128)(2,1)}, u32[]{:S(2)}, u32[]{:S(2)}) collective-permute-start(bf16[2,384,256]{2,1,0:T(8,128)(2,1)S(1)} %pad_maximum_fusion.refs_5_), channel_id=1, source_target_pairs={{0,2},{1,3},{2,0},{3,1},{4,6},{5,7},{6,4},{7,5},{8,10},{9,11},{10,... | collective-permute-start | bytes 1179656 | tf_op jit(solution)/shard_map/ppermute | solution.py:39
  75.7 27.3 %collective-permute-start.1 = (bf16[384,256]{1,0:T(8,128)(2,1)}, bf16[384,256]{1,0:T(8,128)(2,1)}, u32[]{:S(2)}, u32[]{:S(2)}) collective-permute-start(bf16[384,256]{1,0:T(8,128)(2,1)} %bitcast.3.refs_1_), channel_id=1, source_target_pairs={{0,2},{1,3},{2,0},{3,1},{4,6},{5,7},{6,4},{7,5},{8,10},{9,11},{10,... | collective-permute-start | bytes 589832 | tf_op jit(solution)/shard_map/ppermute | solution.py:39
  75.8 30.3 %collective-permute-start.5 = (bf16[2,384,256]{2,1,0:T(8,128)(2,1)S(1)}, bf16[2,384,256]{2,1,0:T(8,128)(2,1)}, u32[]{:S(2)}, u32[]{:S(2)}) collective-permute-start(bf16[2,384,256]{2,1,0:T(8,128)(2,1)S(1)} %pad_maximum_fusion.refs_5_), channel_id=1, source_target_pairs={{0,1},{1,0},{2,3},{3,2},{4,5},{5,4},{6,7},{7,6},{8,9},{9,8},{10,11... | collective-permute-start | bytes 1179656 | tf_op jit(solution)/shard_map/ppermute | solution.py:39
  100.9 5.2 %collective-permute-start.7 = (bf16[2,384,256]{2,1,0:T(8,128)(2,1)}, bf16[2,384,256]{2,1,0:T(8,128)(2,1)}, u32[]{:S(2)}, u32[]{:S(2)}) collective-permute-start(bf16[2,384,256]{2,1,0:T(8,128)(2,1)} %collective-permute-done.6.refs_7_), channel_id=1, source_target_pairs={{0,1},{1,0},{2,3},{3,2},{4,5},{5,4},{6,7},{7,6},{8,9},{9,8},{10,11... | collective-permute-start | bytes 1179656 | tf_op jit(solution)/shard_map/ppermute | solution.py:39
  100.9 5.2 %collective-permute-start = (bf16[384,256]{1,0:T(8,128)(2,1)}, bf16[384,256]{1,0:T(8,128)(2,1)}, u32[]{:S(2)}, u32[]{:S(2)}) collective-permute-start(bf16[384,256]{1,0:T(8,128)(2,1)} %bitcast.3.refs_1_), channel_id=1, source_target_pairs={{0,1},{1,0},{2,3},{3,2},{4,5},{5,4},{6,7},{7,6},{8,9},{9,8},{10,11... | collective-permute-start | bytes 589832 | tf_op jit(solution)/shard_map/ppermute | solution.py:39
  103.0 3.1 %collective-permute-start.2 = (bf16[384,256]{1,0:T(8,128)(2,1)}, bf16[384,256]{1,0:T(8,128)(2,1)}, u32[]{:S(2)}, u32[]{:S(2)}) collective-permute-start(bf16[384,256]{1,0:T(8,128)(2,1)} %collective-permute-done.1.refs_3_), channel_id=1, source_target_pairs={{0,1},{1,0},{2,3},{3,2},{4,5},{5,4},{6,7},{7,6},{8,9},{9,8},{10,11... | collective-permute-start | bytes 589832 | tf_op jit(solution)/shard_map/ppermute | solution.py:39
  111.5 10.9 %collective-permute-start.8 = (bf16[1536,64]{1,0:T(8,128)(2,1)}, bf16[1536,64]{1,0:T(8,128)(2,1)}, u32[]{:S(2)}, u32[]{:S(2)}) collective-permute-start(bf16[1536,64]{1,0:T(8,128)(2,1)} %get-tuple-element.9.refs_3_), channel_id=1, source_target_pairs={{0,8},{1,9},{2,10},{3,11},{4,12},{5,13},{6,14},{7,15},{8,16},{9,17... | collective-permute-start | bytes 589832 | tf_op jit(solution)/shard_map/ppermute | solution.py:35
  113.5 11.1 %collective-permute-start.9 = (bf16[1536,64]{1,0:T(8,128)(2,1)}, bf16[1536,64]{1,0:T(8,128)(2,1)}, u32[]{:S(2)}, u32[]{:S(2)}) collective-permute-start(bf16[1536,64]{1,0:T(8,128)(2,1)} %get-tuple-element.9.refs_3_), channel_id=1, source_target_pairs={{0,6},{1,7},{2,4},{3,5},{4,10},{5,11},{6,8},{7,9},{8,14},{9,15},{1... | collective-permute-start | bytes 589832 | tf_op jit(solution)/shard_map/ppermute | solution.py:35
  116.9 12.8 %copy-start.2 = (bf16[2240,256]{1,0:T(8,128)(2,1)S(1)}, bf16[2240,256]{1,0:T(8,128)(2,1)}, u32[]{:S(2)}) copy-start(bf16[2240,256]{1,0:T(8,128)(2,1)} %reshape_reshape.3.w0) | copy-start | bytes 3440644
  129.7 1.9 collective-permute-start.10
  129.7 19.8 %collective-permute-start.13 = (bf16[2240,256]{1,0:T(8,128)(2,1)S(1)}, bf16[2240,256]{1,0:T(8,128)(2,1)}, u32[]{:S(2)}, u32[]{:S(2)}) collective-permute-start(bf16[2240,256]{1,0:T(8,128)(2,1)S(1)} %copy-done.2), channel_id=1, source_target_pairs={{0,1},{1,0},{2,3},{3,2},{4,5},{5,4},{6,7},{7,6},{8,9},{9,8},{10,11... | collective-permute-start | bytes 3440648 | tf_op jit(solution)/shard_map/ppermute | solution.py:39
  130.2 21.1 %copy-start.5 = (bf16[2240,256]{1,0:T(8,128)(2,1)}, bf16[2240,256]{1,0:T(8,128)(2,1)S(1)}, u32[]{:S(2)}) copy-start(bf16[2240,256]{1,0:T(8,128)(2,1)S(1)} %collective-permute-done.14.w2) | copy-start | bytes 3440644
  130.2 21.1 %collective-permute-start.15 = (bf16[2240,256]{1,0:T(8,128)(2,1)S(1)}, bf16[2240,256]{1,0:T(8,128)(2,1)}, u32[]{:S(2)}, u32[]{:S(2)}) collective-permute-start(bf16[2240,256]{1,0:T(8,128)(2,1)S(1)} %collective-permute-done.14.w2), channel_id=1, source_target_pairs={{0,1},{1,0},{2,3},{3,2},{4,5},{5,4},{6,7},{7,6},{8,9},{9,8},{10,11... | collective-permute-start | bytes 3440648 | tf_op jit(solution)/shard_map/ppermute | solution.py:39
  131.6 0.7 copy-start.6
  134.4 12.0 %collective-permute-start.11 = (bf16[768,256]{1,0:T(8,128)(2,1)}, bf16[768,256]{1,0:T(8,128)(2,1)S(1)}, u32[]{:S(2)}, u32[]{:S(2)}) collective-permute-start(bf16[768,256]{1,0:T(8,128)(2,1)} %chip_sum.1.refs_0_), channel_id=1, source_target_pairs={{0,2},{1,3},{2,0},{3,1},{4,6},{5,7},{6,4},{7,5},{8,10},{9,11},{10,... | collective-permute-start | bytes 1179656 | tf_op jit(solution)/shard_map/ppermute | solution.py:39
  146.4 0.7 copy-start.7
  149.4 1.9 collective-permute-start.12
  151.3 0.7 copy-start.8
  158.0 4.3 %copy-start.3 = (bf16[384,2240]{1,0:T(8,128)(2,1)S(1)}, bf16[384,2240]{1,0:T(8,128)(2,1)}, u32[]{:S(2)}) copy-start(bf16[384,2240]{1,0:T(8,128)(2,1)} %embed_tokens.1) | copy-start | bytes 5160964
  167.0 30.6 %all-to-all-start.3 = ((bf16[64,1,989]{2,1,0:T(2,128)(2,1)}), bf16[64,1,989]{2,1,0:T(2,128)(2,1)S(1)}, u32[]{:S(2)}, u32[]{:S(2)}) async-start(bf16[64,1,989]{2,1,0:T(2,128)(2,1)} %convert_element_type.72), calls=%async_computation.3 | async-start | bytes 524288 | tf_op jit(solution)/shard_map/all_to_all | solution.py:370
  198.7 19.3 %all-to-all-start.4 = ((bf16[64,1,989]{2,1,0:T(2,128)(2,1)}), bf16[64,1,989]{2,1,0:T(2,128)(2,1)S(1)}, u32[]{:S(2)}, u32[]{:S(2)}) async-start(bf16[64,1,989]{2,1,0:T(2,128)(2,1)} %copy.42), calls=%async_computation.4 | async-start | bytes 524288 | tf_op jit(solution)/shard_map/all_to_all | solution.py:374

commit v4 on v3

--- a/solution.py
+++ b/solution.py
@@ -366,23 +366,22 @@
     lower_ones = (
         lax.broadcasted_iota(jnp.int32, (peer_count, peer_count), 1)
         < lax.broadcasted_iota(jnp.int32, (peer_count, peer_count), 0)
-    ).astype(F32)
+    ).astype(BF16)
     arrived = lax.all_to_all(
         piece_grid.astype(BF16), "wide", split_axis=0, concat_axis=0, tiled=True
     )
-    partial_sums = jnp.dot(lower_ones, arrived.astype(F32), precision=lax.Precision.HIGHEST)
+    partial_sums = jnp.dot(lower_ones, arrived, preferred_element_type=F32)
     spread_back = lax.all_to_all(
         partial_sums.astype(BF16), "wide", split_axis=0, concat_axis=0, tiled=True
-    ).astype(F32)
+    )
     flat_prefix = spread_back.reshape(-1)[:length_all]
     state_size = state_local.size
     state_prev = flat_prefix[:state_size].reshape(state_local.shape)
     key_prev = flat_prefix[state_size:].reshape(key_local.shape)
-    query_wide = query_feat.astype(F32)
     carried_num = jnp.einsum(
-        "thd,hde->the", query_wide, state_prev, precision=lax.Precision.HIGHEST
-    )
-    carried_den = jnp.einsum("thd,hd->th", query_wide, key_prev, precision=lax.Precision.HIGHEST)
+        "thd,hde->the", query_feat, state_prev, preferred_element_type=F32
+    )
+    carried_den = jnp.einsum("thd,hd->th", query_feat, key_prev, preferred_element_type=F32)
     result = (local_num + carried_num) / (local_den.T + carried_den)[..., None]
     return result.astype(BF16).reshape(token_count, heads_here * HEAD_DIM)
 

time: 224 us -> 224 us (level)
  no operation moved by 1% of the time
where the time goes in v4:
time: 224 us; the launch traced here: 223 us
  waiting for transfers between devices  88.1 us (39%)
  starting transfers between devices  53.3 us (24%)
  blocking collectives  22.6 us (10%)
  Pallas kernels  20.7 us (9%)
  local copies, waits for them, and re-layouts  19.1 us (9%)
  matrix products  16.5 us (7%)
    ppermute x12, waiting for transfers between devices, other(): return lax.ppermute(x, 'narrow', [(i, i ^ mask) for i in range(4)])  39.5 us
    all_to_all x1, blocking collectives, spread(): lax.all_to_all(copies, axis, 0, 0, axis_index_groups=groups, tiled=True)  22.6 us
    all_to_all x1, starting transfers between devices, per_device(): lax.all_to_all(piece_grid.astype(BF16), 'wide', split_axis=0, concat_axis...  16.7 us
    all_to_all x2, waiting for transfers between devices, spread(): lax.all_to_all(copies, axis, 0, 0, axis_index_groups=groups, tiled=True)  15.4 us
    ppermute x4, starting transfers between devices, delayed(): return lax.ppermute(x, BOTH, pairs)  11.7 us
    all_to_all x1, waiting for transfers between devices, per_device(): lax.all_to_all(partial_sums.astype(BF16), 'wide', split_axis=0, concat_ax...  11.5 us
    ppermute x4, waiting for transfers between devices, delayed(): return lax.ppermute(x, BOTH, pairs)  11.3 us
    all_to_all x1, waiting for transfers between devices, per_device(): lax.all_to_all(piece_grid.astype(BF16), 'wide', split_axis=0, concat_axis...  10.5 us
  transfers between devices with their start and end apart: 20, of which 11 were waited for; matrix products, arithmetic and copies ran while one was open for 7% of the time, Pallas kernels for 7%

profile of v4, /device:TPU:8, one launch (start us, length us, event | category | flops | bytes accessed | tf_op | source)
XLA Modules:
  0.0 222.5 jit_solution(306524153022895236)
XLA Ops:
  3.2 22.6 %all_to_all.33 = bf16[8,178,128]{2,1,0:T(8,128)(2,1)S(1)} all-to-all(bf16[8,178,128]{2,1,0:T(8,128)(2,1)S(1)} %broadcast_in_dim.18), channel_id=1, replica_groups={{0,8,16,24,32,40,48,56},{4,12,20,28,36,44,52,60},{64,72,80,88,96,104,11..., dimensions={0} | all-to-all | bytes 729088 | tf_op jit(solution)/shard_map/all_to_all | solution.py:45
  27.1 5.3 %all-to-all-start.2 = ((bf16[8,8,70,128]{3,1,2,0:T(8,128)(2,1)}), bf16[8,8,70,128]{3,1,2,0:T(8,128)(2,1)S(1)}, u32[]{:S(2)}, u32[]{:S(2)}) async-start(bf16[8,8,70,128]{3,1,2,0:T(8,128)(2,1)} %broadcast_in_dim.38), calls=%async_computation.2 | async-start | bytes 2293760 | tf_op jit(solution)/shard_map/all_to_all | solution.py:45
  32.5 15.4 %all-to-all-done.2 = bf16[8,8,70,128]{3,1,2,0:T(8,128)(2,1)S(1)} async-done(((bf16[8,8,70,128]{3,1,2,0:T(8,128)(2,1)}), bf16[8,8,70,128]{3,1,2,0:T(8,128)(2,1)S(1)}, u32[]{:S(2)}, u32[]{:S(2)}) %all-to-all-start.2) | async-done | bytes 1146912 | tf_op jit(solution)/shard_map/all_to_all | solution.py:45
  49.4 3.6 %all-to-all-start.1 = ((bf16[8,8,108,128]{3,1,2,0:T(8,128)(2,1)}), bf16[8,8,108,128]{3,1,2,0:T(8,128)(2,1)S(1)}, u32[]{:S(2)}, u32[]{:S(2)}) async-start(bf16[8,8,108,128]{3,1,2,0:T(8,128)(2,1)} %broadcast_in_dim.23), calls=%async_computation.1 | async-start | bytes 3538944 | tf_op jit(solution)/shard_map/all_to_all | solution.py:45
  53.0 2.4 %collective-permute-start.3 = (bf16[384,256]{1,0:T(8,128)(2,1)}, bf16[384,256]{1,0:T(8,128)(2,1)}, u32[]{:S(2)}, u32[]{:S(2)}) collective-permute-start(bf16[384,256]{1,0:T(8,128)(2,1)} %bitcast.3.refs_1_), channel_id=1, source_target_pairs={{0,8},{1,9},{2,10},{3,11},{4,12},{5,13},{6,14},{7,15},{8,16},{9,17... | collective-permute-start | bytes 589832 | tf_op jit(solution)/shard_map/ppermute | solution.py:35
  55.5 4.5 %collective-permute-start.4 = (bf16[384,256]{1,0:T(8,128)(2,1)}, bf16[384,256]{1,0:T(8,128)(2,1)}, u32[]{:S(2)}, u32[]{:S(2)}) collective-permute-start(bf16[384,256]{1,0:T(8,128)(2,1)} %bitcast.3.refs_1_), channel_id=1, source_target_pairs={{0,6},{1,7},{2,4},{3,5},{4,10},{5,11},{6,8},{7,9},{8,14},{9,15},{1... | collective-permute-start | bytes 589832 | tf_op jit(solution)/shard_map/ppermute | solution.py:35
  62.8 3.6 %collective-permute-start.14 = (bf16[2240,256]{1,0:T(8,128)(2,1)}, bf16[2240,256]{1,0:T(8,128)(2,1)S(1)}, u32[]{:S(2)}, u32[]{:S(2)}) collective-permute-start(bf16[2240,256]{1,0:T(8,128)(2,1)} %reshape_reshape.3.w0), channel_id=1, source_target_pairs={{0,2},{1,3},{2,0},{3,1},{4,6},{5,7},{6,4},{7,5},{8,10},{9,11},{10,... | collective-permute-start | bytes 3440648 | tf_op jit(solution)/shard_map/ppermute | solution.py:39
  66.4 5.5 %collective-permute-done.4 = bf16[384,256]{1,0:T(8,128)(2,1)} collective-permute-done((bf16[384,256]{1,0:T(8,128)(2,1)}, bf16[384,256]{1,0:T(8,128)(2,1)}, u32[]{:S(2)}, u32[]{:S(2)}) %collective-permute-start.4) | collective-permute-done | bytes 196640 | tf_op jit(solution)/shard_map/ppermute | solution.py:35
  73.0 2.7 %collective-permute-start.6 = (bf16[2,384,256]{2,1,0:T(8,128)(2,1)S(1)}, bf16[2,384,256]{2,1,0:T(8,128)(2,1)}, u32[]{:S(2)}, u32[]{:S(2)}) collective-permute-start(bf16[2,384,256]{2,1,0:T(8,128)(2,1)S(1)} %pad_maximum_fusion.refs_5_), channel_id=1, source_target_pairs={{0,2},{1,3},{2,0},{3,1},{4,6},{5,7},{6,4},{7,5},{8,10},{9,11},{10,... | collective-permute-start | bytes 1179656 | tf_op jit(solution)/shard_map/ppermute | solution.py:39
  75.8 25.1 %collective-permute-done.6.refs_7_ = bf16[2,384,256]{2,1,0:T(8,128)(2,1)} collective-permute-done((bf16[2,384,256]{2,1,0:T(8,128)(2,1)S(1)}, bf16[2,384,256]{2,1,0:T(8,128)(2,1)}, u32[]{:S(2)}, u32[]{:S(2)}) %collective-permute-start.6) | collective-permute-done | bytes 393248 | tf_op jit(solution)/shard_map/ppermute | solution.py:39
  103.0 1.9 copy.35
  106.1 5.4 %first_conv.1 = (bf16[1536,64]{1,0:T(8,128)(2,1)}, bf16[768,256]{1,0:T(8,128)(2,1)}) custom-call(s32[1]{0:T(128)} %bitcast.refs_0_.me_ref, bf16[384,256]{1,0:T(8,128)(2,1)} %bitcast.3.refs_1_, bf16[384,256]{1,0:T(8,128)(2,1)} %collective-permute-done.refs_2_, bf16[384,256]{1,0:T(8,128)(2,1)} %collective-permute-done.1.refs_3_, ...), custom_call_target="tpu_custom_call" | custom-call | tf_op jit(solution)/shard_map/first_conv/pallas_call | solution.py:111
  111.5 2.1 collective-permute-start.8
  113.5 2.8 %collective-permute-start.9 = (bf16[1536,64]{1,0:T(8,128)(2,1)}, bf16[1536,64]{1,0:T(8,128)(2,1)}, u32[]{:S(2)}, u32[]{:S(2)}) collective-permute-start(bf16[1536,64]{1,0:T(8,128)(2,1)} %get-tuple-element.9.refs_3_), channel_id=1, source_target_pairs={{0,6},{1,7},{2,4},{3,5},{4,10},{5,11},{6,8},{7,9},{8,14},{9,15},{1... | collective-permute-start | bytes 589832 | tf_op jit(solution)/shard_map/ppermute | solution.py:35
  116.9 1.9 reshape.113.refs_4_
  118.8 3.6 %collective-permute-done.8.refs_1_ = bf16[1536,64]{1,0:T(8,128)(2,1)} collective-permute-done((bf16[1536,64]{1,0:T(8,128)(2,1)}, bf16[1536,64]{1,0:T(8,128)(2,1)}, u32[]{:S(2)}, u32[]{:S(2)}) %collective-permute-start.8) | collective-permute-done | bytes 196640 | tf_op jit(solution)/shard_map/ppermute | solution.py:35
  122.4 2.2 collective-permute-done.9.refs_2_
  124.6 5.1 %second_conv.1 = (f32[768,256]{1,0:T(8,128)}, bf16[768,256]{1,0:T(8,128)(2,1)}) custom-call(s32[1]{0:T(128)} %bitcast.2.refs_0_, bf16[1536,64]{1,0:T(8,128)(2,1)} %collective-permute-done.8.refs_1_, bf16[1536,64]{1,0:T(8,128)(2,1)} %collective-permute-done.9.refs_2_, bf16[1536,64]{1,0:T(8,128)(2,1)} %get-tuple-element.9.refs_3_, ...), custom_call_target="tpu_custom_call" | custom-call | tf_op jit(solution)/shard_map/second_conv/pallas_call | solution.py:173
  132.4 2.0 chip_sum.1.refs_0_
  134.4 2.3 %collective-permute-start.11 = (bf16[768,256]{1,0:T(8,128)(2,1)}, bf16[768,256]{1,0:T(8,128)(2,1)S(1)}, u32[]{:S(2)}, u32[]{:S(2)}) collective-permute-start(bf16[768,256]{1,0:T(8,128)(2,1)} %chip_sum.1.refs_0_), channel_id=1, source_target_pairs={{0,2},{1,3},{2,0},{3,1},{4,6},{5,7},{6,4},{7,5},{8,10},{9,11},{10,... | collective-permute-start | bytes 1179656 | tf_op jit(solution)/shard_map/ppermute | solution.py:39
  136.8 9.6 %collective-permute-done.11.refs_1_ = bf16[768,256]{1,0:T(8,128)(2,1)S(1)} collective-permute-done((bf16[768,256]{1,0:T(8,128)(2,1)}, bf16[768,256]{1,0:T(8,128)(2,1)S(1)}, u32[]{:S(2)}, u32[]{:S(2)}) %collective-permute-start.11) | collective-permute-done | bytes 393248 | tf_op jit(solution)/shard_map/ppermute | solution.py:39
  147.1 2.3 %patch_rows.1.mine_ref = bf16[192,1024]{1,0:T(8,128)(2,1)} custom-call(bf16[768,256]{1,0:T(8,128)(2,1)} %chip_sum.1.refs_0_, bf16[768,256]{1,0:T(8,128)(2,1)} %copy-done.7, bf16[768,256]{1,0:T(8,128)(2,1)} %get-tuple-element.12.refs_2_), custom_call_target="tpu_custom_call" | custom-call | tf_op jit(solution)/shard_map/patch_rows/pallas_call | solution.py:226
  149.5 1.9 collective-permute-done.12.near_ref
  152.1 5.9 %embed_tokens.1 = bf16[384,2240]{1,0:T(8,128)(2,1)} custom-call(s32[1]{0:T(128)} %bitcast.refs_0_.me_ref, s32[1]{0:T(128)} %bitcast.1.role_ref, bf16[192,1024]{1,0:T(8,128)(2,1)} %patch_rows.1.mine_ref, bf16[192,1024]{1,0:T(8,128)(2,1)} %copy-done.8, bf16[2240,256]{1,0:T(8,128)(2,1)} %reshape_reshape.3.w0, bf16[2240,256]{1,0:T(8,128)(2,1)} %collective-permute-done.13.w1, ...), custom_call_target="tpu_custom_call" | custom-call | tf_op jit(solution)/shard_map/embed_tokens/pallas_call | solution.py:254
  158.0 4.2 %fusion.62 = (bf16[560]{0:T(1024)(128)(2,1)S(1)}, bf16[384,560]{0,1:T(8,128)(2,1)S(1)}) fusion(bf16[384,2240]{1,0:T(8,128)(2,1)} %embed_tokens.1, bf16[3,2240,560]{1,2,0:T(8,128)(2,1)} %param.9), kind=kOutput, calls=%fused_computation.60 | convolution fusion | flops 965098944 | bytes 4781152 | tf_op jit(solution)/shard_map/dot_general | solution.py:339
  162.2 3.2 %fusion.15 = bf16[384,560]{0,1:T(8,128)(2,1)S(1)} fusion(bf16[384,2240]{1,0:T(8,128)(2,1)S(1)} %copy-done.3, bf16[3,2240,560]{1,2,0:T(8,128)(2,1)} %param.9), kind=kOutput, calls=%fused_computation.21 | convolution fusion | flops 963594240 | bytes 4730880 | tf_op jit(solution)/shard_map/dot_general | solution.py:340
  167.0 16.7 %all-to-all-start.3 = ((bf16[64,1,989]{2,1,0:T(2,128)(2,1)}), bf16[64,1,989]{2,1,0:T(2,128)(2,1)S(1)}, u32[]{:S(2)}, u32[]{:S(2)}) async-start(bf16[64,1,989]{2,1,0:T(2,128)(2,1)} %convert_element_type.69), calls=%async_computation.3 | async-start | bytes 524288 | tf_op jit(solution)/shard_map/all_to_all | solution.py:370
  183.8 3.4 %fusion.39 = bf16[384,560]{0,1:T(8,128)(2,1)S(1)} fusion(bf16[384,2240]{1,0:T(8,128)(2,1)S(1)} %copy-done.3, bf16[3,2240,560]{1,2,0:T(8,128)(2,1)} %param.9), kind=kOutput, calls=%fused_computation.36 | convolution fusion | flops 964884480 | bytes 4730880 | tf_op jit(solution)/shard_map/dot_general | solution.py:342
  187.2 10.5 %all-to-all-done.3 = bf16[64,1,989]{2,1,0:T(2,128)(2,1)S(1)} async-done(((bf16[64,1,989]{2,1,0:T(2,128)(2,1)}), bf16[64,1,989]{2,1,0:T(2,128)(2,1)S(1)}, u32[]{:S(2)}, u32[]{:S(2)}) %all-to-all-start.3) | async-done | bytes 126624 | tf_op jit(solution)/shard_map/all_to_all | solution.py:370
  198.7 6.0 %all-to-all-start.4 = ((bf16[64,1,989]{2,1,0:T(2,128)(2,1)}), bf16[64,1,989]{2,1,0:T(2,128)(2,1)S(1)}, u32[]{:S(2)}, u32[]{:S(2)}) async-start(bf16[64,1,989]{2,1,0:T(2,128)(2,1)} %copy.42), calls=%async_computation.4 | async-start | bytes 524288 | tf_op jit(solution)/shard_map/all_to_all | solution.py:374
  206.6 11.5 %all-to-all-done.4 = bf16[64,1,989]{2,1,0:T(2,128)(2,1)S(1)} async-done(((bf16[64,1,989]{2,1,0:T(2,128)(2,1)}), bf16[64,1,989]{2,1,0:T(2,128)(2,1)S(1)}, u32[]{:S(2)}, u32[]{:S(2)}) %all-to-all-start.4) | async-done | bytes 126624 | tf_op jit(solution)/shard_map/all_to_all | solution.py:374
  219.9 2.6 %fusion.30 = bf16[384,5,112]{0,2,1:T(8,128)(2,1)} fusion(f32[5,112,384]{2,1,0:T(8,128)S(1)} %fusion.63, bf16[384,5,112]{0,2,1:T(8,128)(2,1)S(1)} %bitcast.102, bf16[5,384,384]{1,2,0:T(8,128)(2,1)} %get-tuple-element.18, pred[384,384]{0,1:T(8,128)(4,1)S(1)} %iota_compare_fusion, f32[384,5]{0,1:T(8,128)S(1)} %fusion.59), kind=kOutput, calls=%fused_computation.26 | convolution fusion | flops 166533120 | bytes 3350016 | tf_op jit(solution)/shard_map/hts,she->the/dot_general | solution.py:354
  (78 shorter events, 24.4 us)
Async XLA Ops:
  0.0 0.9 copy-start
  27.1 20.8 %all-to-all-start.2 = ((bf16[8,8,70,128]{3,1,2,0:T(8,128)(2,1)}), bf16[8,8,70,128]{3,1,2,0:T(8,128)(2,1)S(1)}, u32[]{:S(2)}, u32[]{:S(2)}) async-start(bf16[8,8,70,128]{3,1,2,0:T(8,128)(2,1)} %broadcast_in_dim.38), calls=%async_computation.2 | async-start | bytes 2293760 | tf_op jit(solution)/shard_map/all_to_all | solution.py:45
  47.8 1.6 copy-start.1
  49.4 53.6 %all-to-all-start.1 = ((bf16[8,8,108,128]{3,1,2,0:T(8,128)(2,1)}), bf16[8,8,108,128]{3,1,2,0:T(8,128)(2,1)S(1)}, u32[]{:S(2)}, u32[]{:S(2)}) async-start(bf16[8,8,108,128]{3,1,2,0:T(8,128)(2,1)} %broadcast_in_dim.23), calls=%async_computation.1 | async-start | bytes 3538944 | tf_op jit(solution)/shard_map/all_to_all | solution.py:45
  53.0 13.4 %collective-permute-start.3 = (bf16[384,256]{1,0:T(8,128)(2,1)}, bf16[384,256]{1,0:T(8,128)(2,1)}, u32[]{:S(2)}, u32[]{:S(2)}) collective-permute-start(bf16[384,256]{1,0:T(8,128)(2,1)} %bitcast.3.refs_1_), channel_id=1, source_target_pairs={{0,8},{1,9},{2,10},{3,11},{4,12},{5,13},{6,14},{7,15},{8,16},{9,17... | collective-permute-start | bytes 589832 | tf_op jit(solution)/shard_map/ppermute | solution.py:35
  55.5 16.4 %collective-permute-start.4 = (bf16[384,256]{1,0:T(8,128)(2,1)}, bf16[384,256]{1,0:T(8,128)(2,1)}, u32[]{:S(2)}, u32[]{:S(2)}) collective-permute-start(bf16[384,256]{1,0:T(8,128)(2,1)} %bitcast.3.refs_1_), channel_id=1, source_target_pairs={{0,6},{1,7},{2,4},{3,5},{4,10},{5,11},{6,8},{7,9},{8,14},{9,15},{1... | collective-permute-start | bytes 589832 | tf_op jit(solution)/shard_map/ppermute | solution.py:35
  62.8 67.4 %collective-permute-start.14 = (bf16[2240,256]{1,0:T(8,128)(2,1)}, bf16[2240,256]{1,0:T(8,128)(2,1)S(1)}, u32[]{:S(2)}, u32[]{:S(2)}) collective-permute-start(bf16[2240,256]{1,0:T(8,128)(2,1)} %reshape_reshape.3.w0), channel_id=1, source_target_pairs={{0,2},{1,3},{2,0},{3,1},{4,6},{5,7},{6,4},{7,5},{8,10},{9,11},{10,... | collective-permute-start | bytes 3440648 | tf_op jit(solution)/shard_map/ppermute | solution.py:39
  73.0 31.9 %copy-start.4 = (bf16[2,384,256]{2,1,0:T(8,128)(2,1)}, bf16[2,384,256]{2,1,0:T(8,128)(2,1)S(1)}, u32[]{:S(2)}) copy-start(bf16[2,384,256]{2,1,0:T(8,128)(2,1)S(1)} %pad_maximum_fusion.refs_5_) | copy-start | bytes 1179652
  73.0 27.9 %collective-permute-start.6 = (bf16[2,384,256]{2,1,0:T(8,128)(2,1)S(1)}, bf16[2,384,256]{2,1,0:T(8,128)(2,1)}, u32[]{:S(2)}, u32[]{:S(2)}) collective-permute-start(bf16[2,384,256]{2,1,0:T(8,128)(2,1)S(1)} %pad_maximum_fusion.refs_5_), channel_id=1, source_target_pairs={{0,2},{1,3},{2,0},{3,1},{4,6},{5,7},{6,4},{7,5},{8,10},{9,11},{10,... | collective-permute-start | bytes 1179656 | tf_op jit(solution)/shard_map/ppermute | solution.py:39
  75.7 27.3 %collective-permute-start.1 = (bf16[384,256]{1,0:T(8,128)(2,1)}, bf16[384,256]{1,0:T(8,128)(2,1)}, u32[]{:S(2)}, u32[]{:S(2)}) collective-permute-start(bf16[384,256]{1,0:T(8,128)(2,1)} %bitcast.3.refs_1_), channel_id=1, source_target_pairs={{0,2},{1,3},{2,0},{3,1},{4,6},{5,7},{6,4},{7,5},{8,10},{9,11},{10,... | collective-permute-start | bytes 589832 | tf_op jit(solution)/shard_map/ppermute | solution.py:39
  75.8 30.3 %collective-permute-start.5 = (bf16[2,384,256]{2,1,0:T(8,128)(2,1)S(1)}, bf16[2,384,256]{2,1,0:T(8,128)(2,1)}, u32[]{:S(2)}, u32[]{:S(2)}) collective-permute-start(bf16[2,384,256]{2,1,0:T(8,128)(2,1)S(1)} %pad_maximum_fusion.refs_5_), channel_id=1, source_target_pairs={{0,1},{1,0},{2,3},{3,2},{4,5},{5,4},{6,7},{7,6},{8,9},{9,8},{10,11... | collective-permute-start | bytes 1179656 | tf_op jit(solution)/shard_map/ppermute | solution.py:39
  100.9 5.2 %collective-permute-start.7 = (bf16[2,384,256]{2,1,0:T(8,128)(2,1)}, bf16[2,384,256]{2,1,0:T(8,128)(2,1)}, u32[]{:S(2)}, u32[]{:S(2)}) collective-permute-start(bf16[2,384,256]{2,1,0:T(8,128)(2,1)} %collective-permute-done.6.refs_7_), channel_id=1, source_target_pairs={{0,1},{1,0},{2,3},{3,2},{4,5},{5,4},{6,7},{7,6},{8,9},{9,8},{10,11... | collective-permute-start | bytes 1179656 | tf_op jit(solution)/shard_map/ppermute | solution.py:39
  100.9 5.2 %collective-permute-start = (bf16[384,256]{1,0:T(8,128)(2,1)}, bf16[384,256]{1,0:T(8,128)(2,1)}, u32[]{:S(2)}, u32[]{:S(2)}) collective-permute-start(bf16[384,256]{1,0:T(8,128)(2,1)} %bitcast.3.refs_1_), channel_id=1, source_target_pairs={{0,1},{1,0},{2,3},{3,2},{4,5},{5,4},{6,7},{7,6},{8,9},{9,8},{10,11... | collective-permute-start | bytes 589832 | tf_op jit(solution)/shard_map/ppermute | solution.py:39
  103.0 3.1 %collective-permute-start.2 = (bf16[384,256]{1,0:T(8,128)(2,1)}, bf16[384,256]{1,0:T(8,128)(2,1)}, u32[]{:S(2)}, u32[]{:S(2)}) collective-permute-start(bf16[384,256]{1,0:T(8,128)(2,1)} %collective-permute-done.1.refs_3_), channel_id=1, source_target_pairs={{0,1},{1,0},{2,3},{3,2},{4,5},{5,4},{6,7},{7,6},{8,9},{9,8},{10,11... | collective-permute-start | bytes 589832 | tf_op jit(solution)/shard_map/ppermute | solution.py:39
  111.5 10.9 %collective-permute-start.8 = (bf16[1536,64]{1,0:T(8,128)(2,1)}, bf16[1536,64]{1,0:T(8,128)(2,1)}, u32[]{:S(2)}, u32[]{:S(2)}) collective-permute-start(bf16[1536,64]{1,0:T(8,128)(2,1)} %get-tuple-element.9.refs_3_), channel_id=1, source_target_pairs={{0,8},{1,9},{2,10},{3,11},{4,12},{5,13},{6,14},{7,15},{8,16},{9,17... | collective-permute-start | bytes 589832 | tf_op jit(solution)/shard_map/ppermute | solution.py:35
  113.5 11.1 %collective-permute-start.9 = (bf16[1536,64]{1,0:T(8,128)(2,1)}, bf16[1536,64]{1,0:T(8,128)(2,1)}, u32[]{:S(2)}, u32[]{:S(2)}) collective-permute-start(bf16[1536,64]{1,0:T(8,128)(2,1)} %get-tuple-element.9.refs_3_), channel_id=1, source_target_pairs={{0,6},{1,7},{2,4},{3,5},{4,10},{5,11},{6,8},{7,9},{8,14},{9,15},{1... | collective-permute-start | bytes 589832 | tf_op jit(solution)/shard_map/ppermute | solution.py:35
  116.9 12.8 %copy-start.2 = (bf16[2240,256]{1,0:T(8,128)(2,1)S(1)}, bf16[2240,256]{1,0:T(8,128)(2,1)}, u32[]{:S(2)}) copy-start(bf16[2240,256]{1,0:T(8,128)(2,1)} %reshape_reshape.3.w0) | copy-start | bytes 3440644
  129.7 1.9 collective-permute-start.10
  129.7 19.8 %collective-permute-start.13 = (bf16[2240,256]{1,0:T(8,128)(2,1)S(1)}, bf16[2240,256]{1,0:T(8,128)(2,1)}, u32[]{:S(2)}, u32[]{:S(2)}) collective-permute-start(bf16[2240,256]{1,0:T(8,128)(2,1)S(1)} %copy-done.2), channel_id=1, source_target_pairs={{0,1},{1,0},{2,3},{3,2},{4,5},{5,4},{6,7},{7,6},{8,9},{9,8},{10,11... | collective-permute-start | bytes 3440648 | tf_op jit(solution)/shard_map/ppermute | solution.py:39
  130.2 21.1 %copy-start.5 = (bf16[2240,256]{1,0:T(8,128)(2,1)}, bf16[2240,256]{1,0:T(8,128)(2,1)S(1)}, u32[]{:S(2)}) copy-start(bf16[2240,256]{1,0:T(8,128)(2,1)S(1)} %collective-permute-done.14.w2) | copy-start | bytes 3440644
  130.2 21.1 %collective-permute-start.15 = (bf16[2240,256]{1,0:T(8,128)(2,1)S(1)}, bf16[2240,256]{1,0:T(8,128)(2,1)}, u32[]{:S(2)}, u32[]{:S(2)}) collective-permute-start(bf16[2240,256]{1,0:T(8,128)(2,1)S(1)} %collective-permute-done.14.w2), channel_id=1, source_target_pairs={{0,1},{1,0},{2,3},{3,2},{4,5},{5,4},{6,7},{7,6},{8,9},{9,8},{10,11... | collective-permute-start | bytes 3440648 | tf_op jit(solution)/shard_map/ppermute | solution.py:39
  131.6 0.7 copy-start.6
  134.4 12.0 %collective-permute-start.11 = (bf16[768,256]{1,0:T(8,128)(2,1)}, bf16[768,256]{1,0:T(8,128)(2,1)S(1)}, u32[]{:S(2)}, u32[]{:S(2)}) collective-permute-start(bf16[768,256]{1,0:T(8,128)(2,1)} %chip_sum.1.refs_0_), channel_id=1, source_target_pairs={{0,2},{1,3},{2,0},{3,1},{4,6},{5,7},{6,4},{7,5},{8,10},{9,11},{10,... | collective-permute-start | bytes 1179656 | tf_op jit(solution)/shard_map/ppermute | solution.py:39
  146.4 0.7 copy-start.7
  149.4 1.9 collective-permute-start.12
  151.3 0.7 copy-start.8
  158.0 4.3 %copy-start.3 = (bf16[384,2240]{1,0:T(8,128)(2,1)S(1)}, bf16[384,2240]{1,0:T(8,128)(2,1)}, u32[]{:S(2)}) copy-start(bf16[384,2240]{1,0:T(8,128)(2,1)} %embed_tokens.1) | copy-start | bytes 5160964
  167.0 30.6 %all-to-all-start.3 = ((bf16[64,1,989]{2,1,0:T(2,128)(2,1)}), bf16[64,1,989]{2,1,0:T(2,128)(2,1)S(1)}, u32[]{:S(2)}, u32[]{:S(2)}) async-start(bf16[64,1,989]{2,1,0:T(2,128)(2,1)} %convert_element_type.69), calls=%async_computation.3 | async-start | bytes 524288 | tf_op jit(solution)/shard_map/all_to_all | solution.py:370
  198.7 19.3 %all-to-all-start.4 = ((bf16[64,1,989]{2,1,0:T(2,128)(2,1)}), bf16[64,1,989]{2,1,0:T(2,128)(2,1)S(1)}, u32[]{:S(2)}, u32[]{:S(2)}) async-start(bf16[64,1,989]{2,1,0:T(2,128)(2,1)} %copy.42), calls=%async_computation.4 | async-start | bytes 524288 | tf_op jit(solution)/shard_map/all_to_all | solution.py:374

commit v5 on v4

--- a/solution.py
+++ b/solution.py
@@ -356,21 +356,21 @@
     )
     state_local = jnp.einsum("thd,the->hde", key_feat, val_heads, preferred_element_type=F32)
     key_local = jnp.sum(key_feat, axis=0, dtype=F32)
-    flat_state = jnp.concatenate([state_local.reshape(-1), key_local.reshape(-1)])
+    flat_state = jnp.concatenate(
+        [state_local.astype(BF16).reshape(-1), key_local.astype(BF16).reshape(-1)]
+    )
     length_all = flat_state.shape[0]
     peer_count = lax.axis_size("wide")
-    per_peer = -(-length_all // peer_count)
+    per_peer = -(-length_all // (peer_count * 1024)) * 1024
     piece_grid = jnp.pad(flat_state, (0, per_peer * peer_count - length_all)).reshape(
-        peer_count, per_peer
+        peer_count, per_peer // 128, 128
     )
     lower_ones = (
         lax.broadcasted_iota(jnp.int32, (peer_count, peer_count), 1)
         < lax.broadcasted_iota(jnp.int32, (peer_count, peer_count), 0)
     ).astype(BF16)
-    arrived = lax.all_to_all(
-        piece_grid.astype(BF16), "wide", split_axis=0, concat_axis=0, tiled=True
-    )
-    partial_sums = jnp.dot(lower_ones, arrived, preferred_element_type=F32)
+    arrived = lax.all_to_all(piece_grid, "wide", split_axis=0, concat_axis=0, tiled=True)
+    partial_sums = jnp.einsum("fg,grl->frl", lower_ones, arrived, preferred_element_type=F32)
     spread_back = lax.all_to_all(
         partial_sums.astype(BF16), "wide", split_axis=0, concat_axis=0, tiled=True
     )

time: 224 us -> 217 us (0.969)
  matrix products: 16.5 us -> 14 us
  transfers between devices with their start and end apart: 20 -> 20, of which waited for: 11 -> 11; matrix products, arithmetic and copies ran while one was open for 7% -> 6% of each run, Pallas kernels for 7% -> 7%
where the time goes in v5:
time: 217 us; the launch traced here: 216 us
  waiting for transfers between devices  86.3 us (40%)
  starting transfers between devices  52.3 us (24%)
  blocking collectives  22.6 us (10%)
  Pallas kernels  20.7 us (10%)
  local copies, waits for them, and re-layouts  17.8 us (8%)
  matrix products  14 us (6%)
    ppermute x12, waiting for transfers between devices, other(): return lax.ppermute(x, 'narrow', [(i, i ^ mask) for i in range(4)])  39.5 us
    all_to_all x1, blocking collectives, spread(): lax.all_to_all(copies, axis, 0, 0, axis_index_groups=groups, tiled=True)  22.6 us
    all_to_all x1, starting transfers between devices, per_device(): lax.all_to_all(piece_grid, 'wide', split_axis=0, concat_axis=0, tiled=True)  17 us
    all_to_all x2, waiting for transfers between devices, spread(): lax.all_to_all(copies, axis, 0, 0, axis_index_groups=groups, tiled=True)  15.4 us
    ppermute x4, starting transfers between devices, delayed(): return lax.ppermute(x, BOTH, pairs)  11.7 us
    all_to_all x1, waiting for transfers between devices, per_device(): lax.all_to_all(partial_sums.astype(BF16), 'wide', split_axis=0, concat_ax...  11.5 us
    ppermute x4, waiting for transfers between devices, delayed(): return lax.ppermute(x, BOTH, pairs)  11.3 us
    ppermute x12, starting transfers between devices, other(): return lax.ppermute(x, 'narrow', [(i, i ^ mask) for i in range(4)])  9.94 us
  transfers between devices with their start and end apart: 20, of which 11 were waited for; matrix products, arithmetic and copies ran while one was open for 6% of the time, Pallas kernels for 7%

profile of v5, /device:TPU:8, one launch (start us, length us, event | category | flops | bytes accessed | tf_op | source)
XLA Modules:
  0.0 215.8 jit_solution(9575041319826899672)
XLA Ops:
  3.2 22.6 %all_to_all.25 = bf16[8,178,128]{2,1,0:T(8,128)(2,1)S(1)} all-to-all(bf16[8,178,128]{2,1,0:T(8,128)(2,1)S(1)} %broadcast_in_dim.18), channel_id=1, replica_groups={{0,8,16,24,32,40,48,56},{4,12,20,28,36,44,52,60},{64,72,80,88,96,104,11..., dimensions={0} | all-to-all | bytes 729088 | tf_op jit(solution)/shard_map/all_to_all | solution.py:45
  27.1 5.3 %all-to-all-start.2 = ((bf16[8,8,70,128]{3,1,2,0:T(8,128)(2,1)}), bf16[8,8,70,128]{3,1,2,0:T(8,128)(2,1)S(1)}, u32[]{:S(2)}, u32[]{:S(2)}) async-start(bf16[8,8,70,128]{3,1,2,0:T(8,128)(2,1)} %broadcast_in_dim.38), calls=%async_computation.2 | async-start | bytes 2293760 | tf_op jit(solution)/shard_map/all_to_all | solution.py:45
  32.5 15.4 %all-to-all-done.2 = bf16[8,8,70,128]{3,1,2,0:T(8,128)(2,1)S(1)} async-done(((bf16[8,8,70,128]{3,1,2,0:T(8,128)(2,1)}), bf16[8,8,70,128]{3,1,2,0:T(8,128)(2,1)S(1)}, u32[]{:S(2)}, u32[]{:S(2)}) %all-to-all-start.2) | async-done | bytes 1146912 | tf_op jit(solution)/shard_map/all_to_all | solution.py:45
  49.4 3.6 %all-to-all-start.1 = ((bf16[8,8,108,128]{3,1,2,0:T(8,128)(2,1)}), bf16[8,8,108,128]{3,1,2,0:T(8,128)(2,1)S(1)}, u32[]{:S(2)}, u32[]{:S(2)}) async-start(bf16[8,8,108,128]{3,1,2,0:T(8,128)(2,1)} %broadcast_in_dim.23), calls=%async_computation.1 | async-start | bytes 3538944 | tf_op jit(solution)/shard_map/all_to_all | solution.py:45
  53.0 2.4 %collective-permute-start.3 = (bf16[384,256]{1,0:T(8,128)(2,1)}, bf16[384,256]{1,0:T(8,128)(2,1)}, u32[]{:S(2)}, u32[]{:S(2)}) collective-permute-start(bf16[384,256]{1,0:T(8,128)(2,1)} %bitcast.3.refs_1_), channel_id=1, source_target_pairs={{0,8},{1,9},{2,10},{3,11},{4,12},{5,13},{6,14},{7,15},{8,16},{9,17... | collective-permute-start | bytes 589832 | tf_op jit(solution)/shard_map/ppermute | solution.py:35
  55.4 4.5 %collective-permute-start.4 = (bf16[384,256]{1,0:T(8,128)(2,1)}, bf16[384,256]{1,0:T(8,128)(2,1)}, u32[]{:S(2)}, u32[]{:S(2)}) collective-permute-start(bf16[384,256]{1,0:T(8,128)(2,1)} %bitcast.3.refs_1_), channel_id=1, source_target_pairs={{0,6},{1,7},{2,4},{3,5},{4,10},{5,11},{6,8},{7,9},{8,14},{9,15},{1... | collective-permute-start | bytes 589832 | tf_op jit(solution)/shard_map/ppermute | solution.py:35
  62.8 3.6 %collective-permute-start.14 = (bf16[2240,256]{1,0:T(8,128)(2,1)}, bf16[2240,256]{1,0:T(8,128)(2,1)S(1)}, u32[]{:S(2)}, u32[]{:S(2)}) collective-permute-start(bf16[2240,256]{1,0:T(8,128)(2,1)} %reshape_reshape.3.w0), channel_id=1, source_target_pairs={{0,2},{1,3},{2,0},{3,1},{4,6},{5,7},{6,4},{7,5},{8,10},{9,11},{10,... | collective-permute-start | bytes 3440648 | tf_op jit(solution)/shard_map/ppermute | solution.py:39
  66.4 5.5 %collective-permute-done.4 = bf16[384,256]{1,0:T(8,128)(2,1)} collective-permute-done((bf16[384,256]{1,0:T(8,128)(2,1)}, bf16[384,256]{1,0:T(8,128)(2,1)}, u32[]{:S(2)}, u32[]{:S(2)}) %collective-permute-start.4) | collective-permute-done | bytes 196640 | tf_op jit(solution)/shard_map/ppermute | solution.py:35
  73.0 2.7 %collective-permute-start.6 = (bf16[2,384,256]{2,1,0:T(8,128)(2,1)S(1)}, bf16[2,384,256]{2,1,0:T(8,128)(2,1)}, u32[]{:S(2)}, u32[]{:S(2)}) collective-permute-start(bf16[2,384,256]{2,1,0:T(8,128)(2,1)S(1)} %pad_maximum_fusion.refs_5_), channel_id=1, source_target_pairs={{0,2},{1,3},{2,0},{3,1},{4,6},{5,7},{6,4},{7,5},{8,10},{9,11},{10,... | collective-permute-start | bytes 1179656 | tf_op jit(solution)/shard_map/ppermute | solution.py:39
  75.8 25.1 %collective-permute-done.6.refs_7_ = bf16[2,384,256]{2,1,0:T(8,128)(2,1)} collective-permute-done((bf16[2,384,256]{2,1,0:T(8,128)(2,1)S(1)}, bf16[2,384,256]{2,1,0:T(8,128)(2,1)}, u32[]{:S(2)}, u32[]{:S(2)}) %collective-permute-start.6) | collective-permute-done | bytes 393248 | tf_op jit(solution)/shard_map/ppermute | solution.py:39
  101.4 1.6 collective-permute-done.1.refs_3_
  103.0 1.9 copy.27
  106.1 5.4 %first_conv.1 = (bf16[1536,64]{1,0:T(8,128)(2,1)}, bf16[768,256]{1,0:T(8,128)(2,1)}) custom-call(s32[1]{0:T(128)} %bitcast.refs_0_.me_ref, bf16[384,256]{1,0:T(8,128)(2,1)} %bitcast.3.refs_1_, bf16[384,256]{1,0:T(8,128)(2,1)} %collective-permute-done.refs_2_, bf16[384,256]{1,0:T(8,128)(2,1)} %collective-permute-done.1.refs_3_, ...), custom_call_target="tpu_custom_call" | custom-call | tf_op jit(solution)/shard_map/first_conv/pallas_call | solution.py:111
  111.5 2.1 collective-permute-start.8
  113.5 2.8 %collective-permute-start.9 = (bf16[1536,64]{1,0:T(8,128)(2,1)}, bf16[1536,64]{1,0:T(8,128)(2,1)}, u32[]{:S(2)}, u32[]{:S(2)}) collective-permute-start(bf16[1536,64]{1,0:T(8,128)(2,1)} %get-tuple-element.9.refs_3_), channel_id=1, source_target_pairs={{0,6},{1,7},{2,4},{3,5},{4,10},{5,11},{6,8},{7,9},{8,14},{9,15},{1... | collective-permute-start | bytes 589832 | tf_op jit(solution)/shard_map/ppermute | solution.py:35
  116.9 1.9 reshape.98.refs_4_
  118.8 3.6 %collective-permute-done.8.refs_1_ = bf16[1536,64]{1,0:T(8,128)(2,1)} collective-permute-done((bf16[1536,64]{1,0:T(8,128)(2,1)}, bf16[1536,64]{1,0:T(8,128)(2,1)}, u32[]{:S(2)}, u32[]{:S(2)}) %collective-permute-start.8) | collective-permute-done | bytes 196640 | tf_op jit(solution)/shard_map/ppermute | solution.py:35
  122.4 2.2 %collective-permute-done.9.refs_2_ = bf16[1536,64]{1,0:T(8,128)(2,1)} collective-permute-done((bf16[1536,64]{1,0:T(8,128)(2,1)}, bf16[1536,64]{1,0:T(8,128)(2,1)}, u32[]{:S(2)}, u32[]{:S(2)}) %collective-permute-start.9) | collective-permute-done | bytes 196640 | tf_op jit(solution)/shard_map/ppermute | solution.py:35
  124.6 5.1 %second_conv.1 = (f32[768,256]{1,0:T(8,128)}, bf16[768,256]{1,0:T(8,128)(2,1)}) custom-call(s32[1]{0:T(128)} %bitcast.2.refs_0_, bf16[1536,64]{1,0:T(8,128)(2,1)} %collective-permute-done.8.refs_1_, bf16[1536,64]{1,0:T(8,128)(2,1)} %collective-permute-done.9.refs_2_, bf16[1536,64]{1,0:T(8,128)(2,1)} %get-tuple-element.9.refs_3_, ...), custom_call_target="tpu_custom_call" | custom-call | tf_op jit(solution)/shard_map/second_conv/pallas_call | solution.py:173
  132.4 2.1 chip_sum.1.refs_0_
  134.4 2.4 %collective-permute-start.11 = (bf16[768,256]{1,0:T(8,128)(2,1)}, bf16[768,256]{1,0:T(8,128)(2,1)S(1)}, u32[]{:S(2)}, u32[]{:S(2)}) collective-permute-start(bf16[768,256]{1,0:T(8,128)(2,1)} %chip_sum.1.refs_0_), channel_id=1, source_target_pairs={{0,2},{1,3},{2,0},{3,1},{4,6},{5,7},{6,4},{7,5},{8,10},{9,11},{10,... | collective-permute-start | bytes 1179656 | tf_op jit(solution)/shard_map/ppermute | solution.py:39
  136.8 9.6 %collective-permute-done.11.refs_1_ = bf16[768,256]{1,0:T(8,128)(2,1)S(1)} collective-permute-done((bf16[768,256]{1,0:T(8,128)(2,1)}, bf16[768,256]{1,0:T(8,128)(2,1)S(1)}, u32[]{:S(2)}, u32[]{:S(2)}) %collective-permute-start.11) | collective-permute-done | bytes 393248 | tf_op jit(solution)/shard_map/ppermute | solution.py:39
  147.2 2.3 %patch_rows.1.mine_ref = bf16[192,1024]{1,0:T(8,128)(2,1)} custom-call(bf16[768,256]{1,0:T(8,128)(2,1)} %chip_sum.1.refs_0_, bf16[768,256]{1,0:T(8,128)(2,1)} %copy-done.7, bf16[768,256]{1,0:T(8,128)(2,1)} %get-tuple-element.12.refs_2_), custom_call_target="tpu_custom_call" | custom-call | tf_op jit(solution)/shard_map/patch_rows/pallas_call | solution.py:226
  149.5 1.9 collective-permute-done.12.near_ref
  152.1 5.9 %embed_tokens.1 = bf16[384,2240]{1,0:T(8,128)(2,1)} custom-call(s32[1]{0:T(128)} %bitcast.refs_0_.me_ref, s32[1]{0:T(128)} %bitcast.1.role_ref, bf16[192,1024]{1,0:T(8,128)(2,1)} %patch_rows.1.mine_ref, bf16[192,1024]{1,0:T(8,128)(2,1)} %copy-done.8, bf16[2240,256]{1,0:T(8,128)(2,1)} %reshape_reshape.3.w0, bf16[2240,256]{1,0:T(8,128)(2,1)} %collective-permute-done.13.w1, ...), custom_call_target="tpu_custom_call" | custom-call | tf_op jit(solution)/shard_map/embed_tokens/pallas_call | solution.py:254
  158.0 4.2 %fusion.63 = (bf16[560]{0:T(1024)(128)(2,1)S(1)}, bf16[384,560]{0,1:T(8,128)(2,1)S(1)}) fusion(bf16[384,2240]{1,0:T(8,128)(2,1)} %embed_tokens.1, bf16[3,2240,560]{1,2,0:T(8,128)(2,1)} %param.9), kind=kOutput, calls=%fused_computation.60 | convolution fusion | flops 965098944 | bytes 4781152 | tf_op jit(solution)/shard_map/dot_general | solution.py:339
  162.2 3.2 %fusion.15 = bf16[384,560]{0,1:T(8,128)(2,1)S(1)} fusion(bf16[384,2240]{1,0:T(8,128)(2,1)S(1)} %copy-done.3, bf16[3,2240,560]{1,2,0:T(8,128)(2,1)} %param.9), kind=kOutput, calls=%fused_computation.21 | convolution fusion | flops 963594240 | bytes 4730880 | tf_op jit(solution)/shard_map/dot_general | solution.py:340
  166.7 17.0 %all-to-all-start.3 = ((bf16[64,8,128]{2,1,0:T(8,128)(2,1)}), bf16[64,8,128]{2,1,0:T(8,128)(2,1)S(1)}, u32[]{:S(2)}, u32[]{:S(2)}) async-start(bf16[64,8,128]{2,1,0:T(8,128)(2,1)} %fusion.53), calls=%async_computation.3 | async-start | bytes 262144 | tf_op jit(solution)/shard_map/all_to_all | solution.py:372
  183.7 3.4 %fusion.38 = bf16[384,560]{0,1:T(8,128)(2,1)S(1)} fusion(bf16[384,2240]{1,0:T(8,128)(2,1)S(1)} %copy-done.3, bf16[3,2240,560]{1,2,0:T(8,128)(2,1)} %param.9), kind=kOutput, calls=%fused_computation.35 | convolution fusion | flops 964884480 | bytes 4730880 | tf_op jit(solution)/shard_map/dot_general | solution.py:342
  187.1 8.7 %all-to-all-done.3 = bf16[64,8,128]{2,1,0:T(8,128)(2,1)S(1)} async-done(((bf16[64,8,128]{2,1,0:T(8,128)(2,1)}), bf16[64,8,128]{2,1,0:T(8,128)(2,1)S(1)}, u32[]{:S(2)}, u32[]{:S(2)}) %all-to-all-start.3) | async-done | bytes 131104 | tf_op jit(solution)/shard_map/all_to_all | solution.py:372
  196.8 4.7 %all-to-all-start.4 = ((bf16[64,8,128]{2,1,0:T(8,128)(2,1)}), bf16[64,8,128]{2,1,0:T(8,128)(2,1)S(1)}, u32[]{:S(2)}, u32[]{:S(2)}) async-start(bf16[64,8,128]{2,1,0:T(8,128)(2,1)} %copy.34), calls=%async_computation.4 | async-start | bytes 262144 | tf_op jit(solution)/shard_map/all_to_all | solution.py:374
  202.2 11.5 %all-to-all-done.4 = bf16[64,8,128]{2,1,0:T(8,128)(2,1)S(1)} async-done(((bf16[64,8,128]{2,1,0:T(8,128)(2,1)}), bf16[64,8,128]{2,1,0:T(8,128)(2,1)S(1)}, u32[]{:S(2)}, u32[]{:S(2)}) %all-to-all-start.4) | async-done | bytes 131104 | tf_op jit(solution)/shard_map/all_to_all | solution.py:374
  (76 shorter events, 21.5 us)
Async XLA Ops:
  0.0 0.9 copy-start
  27.1 20.8 %all-to-all-start.2 = ((bf16[8,8,70,128]{3,1,2,0:T(8,128)(2,1)}), bf16[8,8,70,128]{3,1,2,0:T(8,128)(2,1)S(1)}, u32[]{:S(2)}, u32[]{:S(2)}) async-start(bf16[8,8,70,128]{3,1,2,0:T(8,128)(2,1)} %broadcast_in_dim.38), calls=%async_computation.2 | async-start | bytes 2293760 | tf_op jit(solution)/shard_map/all_to_all | solution.py:45
  47.8 1.6 copy-start.1
  49.4 53.6 %all-to-all-start.1 = ((bf16[8,8,108,128]{3,1,2,0:T(8,128)(2,1)}), bf16[8,8,108,128]{3,1,2,0:T(8,128)(2,1)S(1)}, u32[]{:S(2)}, u32[]{:S(2)}) async-start(bf16[8,8,108,128]{3,1,2,0:T(8,128)(2,1)} %broadcast_in_dim.23), calls=%async_computation.1 | async-start | bytes 3538944 | tf_op jit(solution)/shard_map/all_to_all | solution.py:45
  53.0 13.4 %collective-permute-start.3 = (bf16[384,256]{1,0:T(8,128)(2,1)}, bf16[384,256]{1,0:T(8,128)(2,1)}, u32[]{:S(2)}, u32[]{:S(2)}) collective-permute-start(bf16[384,256]{1,0:T(8,128)(2,1)} %bitcast.3.refs_1_), channel_id=1, source_target_pairs={{0,8},{1,9},{2,10},{3,11},{4,12},{5,13},{6,14},{7,15},{8,16},{9,17... | collective-permute-start | bytes 589832 | tf_op jit(solution)/shard_map/ppermute | solution.py:35
  55.4 16.4 %collective-permute-start.4 = (bf16[384,256]{1,0:T(8,128)(2,1)}, bf16[384,256]{1,0:T(8,128)(2,1)}, u32[]{:S(2)}, u32[]{:S(2)}) collective-permute-start(bf16[384,256]{1,0:T(8,128)(2,1)} %bitcast.3.refs_1_), channel_id=1, source_target_pairs={{0,6},{1,7},{2,4},{3,5},{4,10},{5,11},{6,8},{7,9},{8,14},{9,15},{1... | collective-permute-start | bytes 589832 | tf_op jit(solution)/shard_map/ppermute | solution.py:35
  62.8 67.5 %collective-permute-start.14 = (bf16[2240,256]{1,0:T(8,128)(2,1)}, bf16[2240,256]{1,0:T(8,128)(2,1)S(1)}, u32[]{:S(2)}, u32[]{:S(2)}) collective-permute-start(bf16[2240,256]{1,0:T(8,128)(2,1)} %reshape_reshape.3.w0), channel_id=1, source_target_pairs={{0,2},{1,3},{2,0},{3,1},{4,6},{5,7},{6,4},{7,5},{8,10},{9,11},{10,... | collective-permute-start | bytes 3440648 | tf_op jit(solution)/shard_map/ppermute | solution.py:39
  73.0 31.9 %copy-start.4 = (bf16[2,384,256]{2,1,0:T(8,128)(2,1)}, bf16[2,384,256]{2,1,0:T(8,128)(2,1)S(1)}, u32[]{:S(2)}) copy-start(bf16[2,384,256]{2,1,0:T(8,128)(2,1)S(1)} %pad_maximum_fusion.refs_5_) | copy-start | bytes 1179652
  73.0 27.9 %collective-permute-start.6 = (bf16[2,384,256]{2,1,0:T(8,128)(2,1)S(1)}, bf16[2,384,256]{2,1,0:T(8,128)(2,1)}, u32[]{:S(2)}, u32[]{:S(2)}) collective-permute-start(bf16[2,384,256]{2,1,0:T(8,128)(2,1)S(1)} %pad_maximum_fusion.refs_5_), channel_id=1, source_target_pairs={{0,2},{1,3},{2,0},{3,1},{4,6},{5,7},{6,4},{7,5},{8,10},{9,11},{10,... | collective-permute-start | bytes 1179656 | tf_op jit(solution)/shard_map/ppermute | solution.py:39
  75.7 27.3 %collective-permute-start.1 = (bf16[384,256]{1,0:T(8,128)(2,1)}, bf16[384,256]{1,0:T(8,128)(2,1)}, u32[]{:S(2)}, u32[]{:S(2)}) collective-permute-start(bf16[384,256]{1,0:T(8,128)(2,1)} %bitcast.3.refs_1_), channel_id=1, source_target_pairs={{0,2},{1,3},{2,0},{3,1},{4,6},{5,7},{6,4},{7,5},{8,10},{9,11},{10,... | collective-permute-start | bytes 589832 | tf_op jit(solution)/shard_map/ppermute | solution.py:39
  75.8 30.3 %collective-permute-start.5 = (bf16[2,384,256]{2,1,0:T(8,128)(2,1)S(1)}, bf16[2,384,256]{2,1,0:T(8,128)(2,1)}, u32[]{:S(2)}, u32[]{:S(2)}) collective-permute-start(bf16[2,384,256]{2,1,0:T(8,128)(2,1)S(1)} %pad_maximum_fusion.refs_5_), channel_id=1, source_target_pairs={{0,1},{1,0},{2,3},{3,2},{4,5},{5,4},{6,7},{7,6},{8,9},{9,8},{10,11... | collective-permute-start | bytes 1179656 | tf_op jit(solution)/shard_map/ppermute | solution.py:39
  100.9 5.2 %collective-permute-start.7 = (bf16[2,384,256]{2,1,0:T(8,128)(2,1)}, bf16[2,384,256]{2,1,0:T(8,128)(2,1)}, u32[]{:S(2)}, u32[]{:S(2)}) collective-permute-start(bf16[2,384,256]{2,1,0:T(8,128)(2,1)} %collective-permute-done.6.refs_7_), channel_id=1, source_target_pairs={{0,1},{1,0},{2,3},{3,2},{4,5},{5,4},{6,7},{7,6},{8,9},{9,8},{10,11... | collective-permute-start | bytes 1179656 | tf_op jit(solution)/shard_map/ppermute | solution.py:39
  100.9 5.2 %collective-permute-start = (bf16[384,256]{1,0:T(8,128)(2,1)}, bf16[384,256]{1,0:T(8,128)(2,1)}, u32[]{:S(2)}, u32[]{:S(2)}) collective-permute-start(bf16[384,256]{1,0:T(8,128)(2,1)} %bitcast.3.refs_1_), channel_id=1, source_target_pairs={{0,1},{1,0},{2,3},{3,2},{4,5},{5,4},{6,7},{7,6},{8,9},{9,8},{10,11... | collective-permute-start | bytes 589832 | tf_op jit(solution)/shard_map/ppermute | solution.py:39
  103.0 3.1 %collective-permute-start.2 = (bf16[384,256]{1,0:T(8,128)(2,1)}, bf16[384,256]{1,0:T(8,128)(2,1)}, u32[]{:S(2)}, u32[]{:S(2)}) collective-permute-start(bf16[384,256]{1,0:T(8,128)(2,1)} %collective-permute-done.1.refs_3_), channel_id=1, source_target_pairs={{0,1},{1,0},{2,3},{3,2},{4,5},{5,4},{6,7},{7,6},{8,9},{9,8},{10,11... | collective-permute-start | bytes 589832 | tf_op jit(solution)/shard_map/ppermute | solution.py:39
  111.5 10.9 %collective-permute-start.8 = (bf16[1536,64]{1,0:T(8,128)(2,1)}, bf16[1536,64]{1,0:T(8,128)(2,1)}, u32[]{:S(2)}, u32[]{:S(2)}) collective-permute-start(bf16[1536,64]{1,0:T(8,128)(2,1)} %get-tuple-element.9.refs_3_), channel_id=1, source_target_pairs={{0,8},{1,9},{2,10},{3,11},{4,12},{5,13},{6,14},{7,15},{8,16},{9,17... | collective-permute-start | bytes 589832 | tf_op jit(solution)/shard_map/ppermute | solution.py:35
  113.5 11.1 %collective-permute-start.9 = (bf16[1536,64]{1,0:T(8,128)(2,1)}, bf16[1536,64]{1,0:T(8,128)(2,1)}, u32[]{:S(2)}, u32[]{:S(2)}) collective-permute-start(bf16[1536,64]{1,0:T(8,128)(2,1)} %get-tuple-element.9.refs_3_), channel_id=1, source_target_pairs={{0,6},{1,7},{2,4},{3,5},{4,10},{5,11},{6,8},{7,9},{8,14},{9,15},{1... | collective-permute-start | bytes 589832 | tf_op jit(solution)/shard_map/ppermute | solution.py:35
  116.9 12.8 %copy-start.2 = (bf16[2240,256]{1,0:T(8,128)(2,1)S(1)}, bf16[2240,256]{1,0:T(8,128)(2,1)}, u32[]{:S(2)}) copy-start(bf16[2240,256]{1,0:T(8,128)(2,1)} %reshape_reshape.3.w0) | copy-start | bytes 3440644
  129.7 1.9 collective-permute-start.10
  129.7 19.8 %collective-permute-start.13 = (bf16[2240,256]{1,0:T(8,128)(2,1)S(1)}, bf16[2240,256]{1,0:T(8,128)(2,1)}, u32[]{:S(2)}, u32[]{:S(2)}) collective-permute-start(bf16[2240,256]{1,0:T(8,128)(2,1)S(1)} %copy-done.2), channel_id=1, source_target_pairs={{0,1},{1,0},{2,3},{3,2},{4,5},{5,4},{6,7},{7,6},{8,9},{9,8},{10,11... | collective-permute-start | bytes 3440648 | tf_op jit(solution)/shard_map/ppermute | solution.py:39
  130.2 21.1 %copy-start.5 = (bf16[2240,256]{1,0:T(8,128)(2,1)}, bf16[2240,256]{1,0:T(8,128)(2,1)S(1)}, u32[]{:S(2)}) copy-start(bf16[2240,256]{1,0:T(8,128)(2,1)S(1)} %collective-permute-done.14.w2) | copy-start | bytes 3440644
  130.2 21.1 %collective-permute-start.15 = (bf16[2240,256]{1,0:T(8,128)(2,1)S(1)}, bf16[2240,256]{1,0:T(8,128)(2,1)}, u32[]{:S(2)}, u32[]{:S(2)}) collective-permute-start(bf16[2240,256]{1,0:T(8,128)(2,1)S(1)} %collective-permute-done.14.w2), channel_id=1, source_target_pairs={{0,1},{1,0},{2,3},{3,2},{4,5},{5,4},{6,7},{7,6},{8,9},{9,8},{10,11... | collective-permute-start | bytes 3440648 | tf_op jit(solution)/shard_map/ppermute | solution.py:39
  131.6 0.7 copy-start.6
  134.4 12.0 %collective-permute-start.11 = (bf16[768,256]{1,0:T(8,128)(2,1)}, bf16[768,256]{1,0:T(8,128)(2,1)S(1)}, u32[]{:S(2)}, u32[]{:S(2)}) collective-permute-start(bf16[768,256]{1,0:T(8,128)(2,1)} %chip_sum.1.refs_0_), channel_id=1, source_target_pairs={{0,2},{1,3},{2,0},{3,1},{4,6},{5,7},{6,4},{7,5},{8,10},{9,11},{10,... | collective-permute-start | bytes 1179656 | tf_op jit(solution)/shard_map/ppermute | solution.py:39
  146.4 0.7 copy-start.7
  149.4 1.9 collective-permute-start.12
  151.4 0.7 copy-start.8
  158.0 4.3 %copy-start.3 = (bf16[384,2240]{1,0:T(8,128)(2,1)S(1)}, bf16[384,2240]{1,0:T(8,128)(2,1)}, u32[]{:S(2)}) copy-start(bf16[384,2240]{1,0:T(8,128)(2,1)} %embed_tokens.1) | copy-start | bytes 5160964
  166.7 29.1 %all-to-all-start.3 = ((bf16[64,8,128]{2,1,0:T(8,128)(2,1)}), bf16[64,8,128]{2,1,0:T(8,128)(2,1)S(1)}, u32[]{:S(2)}, u32[]{:S(2)}) async-start(bf16[64,8,128]{2,1,0:T(8,128)(2,1)} %fusion.53), calls=%async_computation.3 | async-start | bytes 262144 | tf_op jit(solution)/shard_map/all_to_all | solution.py:372
  196.8 16.9 %all-to-all-start.4 = ((bf16[64,8,128]{2,1,0:T(8,128)(2,1)}), bf16[64,8,128]{2,1,0:T(8,128)(2,1)S(1)}, u32[]{:S(2)}, u32[]{:S(2)}) async-start(bf16[64,8,128]{2,1,0:T(8,128)(2,1)} %copy.34), calls=%async_computation.4 | async-start | bytes 262144 | tf_op jit(solution)/shard_map/all_to_all | solution.py:374
